TPU v7x, 128 devices: a whole 4x4x4 slice. The times are simulated.
128 devices in a mesh: gx: 8 (over y, core), gy: 16 (over z, x).
Axes of the slice: x: 4, y: 4, z: 4, core: 2. Of those that a mesh axis runs over, the one named last changes fastest.
Arguments:
- stored: bfloat16 [128, 4096, 360], P(('gx', 'gy')), may hold values from -6 to 6
- counts: int32 [128, 128], P(('gx', 'gy')), may hold values from 0 to 32, as said below
- owners: int32 [128, 2048], P('gx', 'gy'), may hold values from 0 to 4095, as said below
- land_mask: int32 [128, 2048], P('gx', 'gy'), may hold values 0 or 1
- flow_x: float32 [128, 2048], P('gx', 'gy'), may hold values from -4 to 4
- flow_y: float32 [128, 2048], P('gx', 'gy'), may hold values from -4 to 4
- costate: float32 [3, 60, 128, 2048], P(None, None, 'gx', 'gy'), may hold values from -6 to 6
- weight_in: float32 [180, 256], replicated, may hold values from -0.4375 to 0.4375
- bias_in: float32 [256], replicated, may hold values from -3 to 3
- weight_mid: float32 [256, 256], replicated, may hold values from -0.375 to 0.375
- bias_mid: float32 [256], replicated, may hold values from -3 to 3
- weight_out: float32 [256, 60], replicated, may hold values from -0.375 to 0.375
- bias_out: float32 [60], replicated, may hold values from -4 to 4
Outputs:
- adjoint: float32 [3, 60, 128, 2048], P(None, None, 'gx', 'gy')
- grad_weight_in: float32 [180, 256], replicated
- grad_bias_in: float32 [256], replicated
- grad_weight_mid: float32 [256, 256], replicated
- grad_bias_mid: float32 [256], replicated
- grad_weight_out: float32 [256, 60], replicated
- grad_bias_out: float32 [60], replicated
Inputs may be any that keep to these rules, and one draw needn't show every extreme that they name: counts[s, d] rows of device s belong to tile d; over s they sum to 2048 for every tile; some tile takes exactly 32 rows from one device. owners[x, y] = s * 32 + r with r < counts[s, d] for the column's tile d; within a tile every value appears once.
All inputs are finite; a program needn't handle non-finite values. No bound on the sum of `land_mask` on one device may be relied on, other than what follows from the above.
Results may differ from a plain program's by a relative error of at most 0.0003.
Values may be sent and summed in bfloat16 or wider, within the bound.
No kernel may reach another device: no remote copies, remote signals or barrier semaphores. Data moves between devices by JAX's collectives and lax.ppermute only.
A program may use at most 128 MiB of HBM per device.

v0:
```python
import jax
import jax.numpy as jnp
from jax import lax
from jax.sharding import PartitionSpec as P

NZ = 60
TRACERS = 3
TSTEPS = 2
IN = 180


step_size = 0.25
flat_mix = 0.25
kappa_top = 1.5


def padded_2(value, sides, width):
    for axis, dim in sides:
        count, length = (lax.axis_size(axis), value.shape[dim])
        up = [(i, (i + 1) % count) for i in range(count - 1)]
        down = [(j, i) for i, j in up]
        last = lax.slice_in_dim(value, length - width, length, axis=dim)
        initial = lax.slice_in_dim(value, 0, width, axis=dim)
        before = lax.ppermute(last, axis, up)
        after = lax.ppermute(initial, axis, down)
        value = jnp.concatenate([before, value, after], axis=dim)
    return value


def vertical(columns, params):
    weight_in, bias_in, weight_mid, bias_mid, weight_out, bias_out = params
    hp = lax.Precision.HIGHEST
    first = jnp.tanh(jnp.dot(weight_in.T, columns, precision=hp) + bias_in[:, None])
    second = jnp.tanh(jnp.dot(weight_mid.T, first, precision=hp) + bias_mid[:, None])
    kappa = kappa_top * jax.nn.sigmoid(
        jnp.dot(weight_out.T, second, precision=hp) + bias_out[:, None]
    )
    field = columns.reshape(TRACERS, NZ, columns.shape[1])
    flux = kappa[None, :-1, :] * (field[:, 1:, :] - field[:, :-1, :])
    edge = jnp.zeros_like(flux[:, :1, :])
    upper = jnp.concatenate([flux, edge], axis=1)
    lower = jnp.concatenate([edge, flux], axis=1)
    return (upper - lower).reshape(columns.shape)


def transport(padded, padded_x, padded_y, weighted):
    near = (
        padded[..., 2:, 1:-1]
        + padded[..., :-2, 1:-1]
        + padded[..., 1:-1, 2:]
        + padded[..., 1:-1, :-2]
    )
    result = flat_mix * (near - 4.0 * weighted)
    result = result + 0.5 * (padded_x[..., 2:, 1:-1] - padded_x[..., :-2, 1:-1])
    return result + 0.5 * (padded_y[..., 1:-1, 2:] - padded_y[..., 1:-1, :-2])


def on_device(
    stored,
    counts,
    owners,
    land_mask,
    flow_x,
    flow_y,
    costate,
    weight_in,
    bias_in,
    weight_mid,
    bias_mid,
    weight_out,
    bias_out,
):
    width_x = lax.axis_size("gx")
    width_y = lax.axis_size("gy")
    devices = width_x * width_y
    tile_x, tile_y = owners.shape
    ncols = tile_x * tile_y
    slot = 2 * ncols // devices
    feat = stored.shape[2]
    my_counts = counts[0]
    starts = jnp.cumsum(my_counts) - my_counts
    row_index = jnp.minimum(
        starts[:, None] + jnp.arange(slot, dtype=jnp.int32)[None, :], stored.shape[1] - 1
    )
    outgoing = stored[0][row_index]
    arrived = lax.all_to_all(outgoing, ("gx", "gy"), split_axis=0, concat_axis=0, tiled=True)
    picked = arrived.reshape(devices * slot, feat)[owners.reshape(-1)]
    states = picked.T.reshape(TSTEPS, TRACERS, NZ, tile_x, tile_y).astype(jnp.float32)
    params = (weight_in, bias_in, weight_mid, bias_mid, weight_out, bias_out)
    totals = jax.tree.map(jnp.zeros_like, params)
    ocean = land_mask.astype(jnp.float32)
    lam = costate
    for moment in range(TSTEPS - 1, -1, -1):
        state = states[moment]
        weighted = lam * ocean
        stacked = jnp.stack([weighted, flow_x * weighted, flow_y * weighted])
        padded = padded_2(stacked, (("gx", 3), ("gy", 4)), 1)
        across = transport(padded[0], padded[1], padded[2], weighted)
        unused, pullback = jax.vjp(vertical, state.reshape(IN, ncols), params)
        grad_state, grad_params = pullback(weighted.reshape(IN, ncols))
        down = grad_state.reshape(TRACERS, NZ, tile_x, tile_y)
        lam = lam + step_size * (across + down)
        totals = jax.tree.map(lambda left, right: left + step_size * right, totals, grad_params)
    summed = lax.psum(
        (totals[0], totals[1], totals[2], totals[3], totals[4], totals[5]), ("gx", "gy")
    )
    scale = 1.0 / jnp.sqrt(jnp.float32(ncols * devices))
    return (
        lam,
        summed[0] * scale,
        summed[1] * scale,
        summed[2] * scale,
        summed[3] * scale,
        summed[4] * scale,
        summed[5] * scale,
    )


def solution(mesh):
    in_specs = (
        P(("gx", "gy"), None, None),
        P(("gx", "gy"), None),
        P("gx", "gy"),
        P("gx", "gy"),
        P("gx", "gy"),
        P("gx", "gy"),
        P(None, None, "gx", "gy"),
        P(),
        P(),
        P(),
        P(),
        P(),
        P(),
    )
    out_specs = (P(None, None, "gx", "gy"), P(), P(), P(), P(), P(), P())
    return jax.shard_map(
        on_device, mesh=mesh, in_specs=in_specs, out_specs=out_specs, check_vma=False
    )
```

profile of v0, /device:TPU:1, one launch (start us, length us, event | category | flops | bytes accessed | tf_op | source)
XLA Modules:
  0.0 548.9 jit_solution(17194821409840462331)
XLA Ops:
  13.1 4.6 collective-permute-start
  23.6 17.1 %gather_fusion = bf16[4096,360]{1,0:T(8,128)(2,1)} fusion(bf16[4096,360]{1,0:T(8,128)(2,1)S(1)} %bitcast.88, s32[4096]{0:T(1024)S(1)} %broadcast_clamp_fusion), kind=kCustom, calls=%fused_computation | custom fusion | bytes 5914624 | tf_op jit(solution)/shard_map/gather | solution.py:85
  40.8 10.5 %all-to-all-start = ((bf16[128,32,360]{2,1,0:T(8,128)(2,1)}), bf16[128,32,360]{2,1,0:T(8,128)(2,1)S(1)}, u32[]{:S(2)}, u32[]{:S(2)}) async-start(bf16[128,32,360]{2,1,0:T(8,128)(2,1)} %bitcast.94), calls=%async_computation | async-start | bytes 6291456 | tf_op jit(solution)/shard_map/all_to_all | solution.py:86
  51.4 5.1 pad_maximum_fusion.2
  56.5 11.3 %fusion.61 = (f32[3,3,60,18,1]{4,3,2,1,0:T(8,128)}, f32[3,3,60,18,1]{4,3,2,1,0:T(8,128)}) fusion(f32[3,3,60,18,128]{4,3,2,1,0:T(8,128)} %pad_maximum_fusion.2), kind=kLoop, calls=%fused_computation.134 | loop fusion | bytes 155520 | tf_op jit(solution)/shard_map/slice | solution.py:22
  67.8 4.5 copy.64
  72.4 3.9 collective-permute-start.2
  76.3 5.2 copy.65
  85.7 5.2 copy.66
  90.9 5.3 copy.67
  96.1 16.7 %pad_maximum_fusion = f32[3,3,60,18,130]{4,3,2,1,0:T(8,128)} fusion(f32[3,3,60,18,1]{4,3,2,1,0:T(8,128)} %copy.67, f32[3,3,60,1,128]{4,3,2,1,0:T(1,128)} %collective-permute-done.1, f32[1,3,60,16,128]{4,3,2,1,0:T(8,128)} %copy-done.14, f32[1,3,60,16,128]{4,3,2,1,0:T(8,128)} %copy-done.13, f32[1,3,60,16,128]{4,3,2,1,0:T(8,128)} %copy-done.12, ...), kind=kLoop, calls=%fused_computation.2 | loop fusion | flops 7581600 | bytes 10108800 | tf_op jit(solution)/shard_map/concatenate | solution.py:26
  112.8 9.9 %slice_bitcast_fusion.5 = (f32[3,60,18,130]{3,2,1,0:T(8,128)}, f32[3,60,18,130]{3,2,1,0:T(8,128)}, f32[3,60,18,130]{3,2,1,0:T(8,128)}) fusion(f32[3,3,60,18,130]{4,3,2,1,0:T(8,128)} %pad_maximum_fusion), kind=kLoop, calls=%fused_computation.11 | loop fusion | bytes 10108800 | tf_op jit(solution)/shard_map/squeeze | solution.py:98
  122.7 9.3 %gather_fusion.1 = bf16[2048,360]{1,0:T(8,128)(2,1)} fusion(bf16[4096,360]{1,0:T(8,128)(2,1)S(1)} %bitcast.89, s32[2048]{0:T(1024)S(1)} %broadcast_clamp_fusion.1), kind=kCustom, calls=%fused_computation.1 | custom fusion | bytes 2957312 | tf_op jit(solution)/shard_map/gather | solution.py:87
  159.3 3.9 fusion.63
  164.8 4.5 fusion.4
  170.9 11.8 %fusion.49 = (f32[1,3,60,16,128]{4,3,2,1,0:T(8,128)}, f32[3,60,16,128]{3,2,1,0:T(8,128)S(1)}) fusion(f32[16,128]{1,0:T(8,128)S(1)} %convert_element_type.7, f32[3,60,16,128]{3,2,1,0:T(8,128)S(1)} %copy-done.30, f32[3,60,16,128]{3,2,1,0:T(8,128)S(1)} %bitcast.100, f32[3,60,18,130]{3,2,1,0:T(8,128)} %get-tuple-element.37, ...), kind=kLoop, calls=%fused_computation.106 | loop fusion | flops 6266880 | bytes 17702912 | tf_op jit(solution)/shard_map/stack | solution.py:96
  201.9 5.9 %fusion.58 = (f32[3,59,2048]{2,1,0:T(8,128)}, f32[3,59,2048]{2,1,0:T(8,128)}, f32[59,2048]{1,0:T(8,128)S(1)}) fusion(f32[3,60,2048]{2,1,0:T(8,128)} %reshape_reshape.7, f32[59,2048]{1,0:T(8,128)} %slice_multiply_fusion, f32[3,60,2048]{2,1,0:T(8,128)} %reshape_reshape_squeeze.7), kind=kLoop, calls=%fused_computation.131 | loop fusion | flops 2416640 | bytes 9666560 | tf_op jit(solution)/shard_map/transpose(jvp())/neg | solution.py:39
  210.2 4.3 fusion.67
  221.8 70.1 %all-reduce.6 = (f32[256]{0:T(256)S(1)}, f32[256]{0:T(256)S(1)}, f32[256,60]{0,1:T(8,128)S(1)}, f32[60]{0:T(128)S(1)}) all-reduce(f32[256]{0:T(256)S(1)} %add_multiply_fusion.1, f32[256]{0:T(256)S(1)} %add_multiply_fusion, f32[256,60]{0,1:T(8,128)S(1)} %fusion.40, ...), channel_id=1, replica_groups=mesh['gx'=8,'gy'=16] {'gx','gy'}, use_global_device_ids=true, to_apply=%region_6.7 | all-reduce | flops 15932 | bytes 127456 | tf_op jit(solution)/shard_map/psum | solution.py:104
  292.6 6.5 %fusion.38 = f32[256,256]{1,0:T(8,128)} fusion(f32[256,256]{1,0:T(8,128)} %fusion.67, f32[2048,256]{1,0:T(8,128)} %fusion.2, f32[2048,256]{1,0:T(8,128)} %copy-done.19), kind=kOutput, calls=%fused_computation.85 | convolution fusion | flops 1610743808 | bytes 4718592 | tf_op jit(solution)/shard_map/transpose(jvp())/dot_general | solution.py:34
  309.9 3.7 fusion.39
  313.5 4.3 fusion.5
  320.6 140.1 %all-reduce.10.cloned.1.call-done = (f32[180,256]{1,0:T(8,128)}, f32[256,256]{1,0:T(8,128)}) async-done(((f32[180,256]{1,0:T(8,128)}, f32[256,256]{1,0:T(8,128)}), (f32[180,256]{1,0:T(8,128)}, f32[256,256]{1,0:T(8,128)})) %all-reduce.10.cloned.1.call-update) | async-done | bytes 446480 | tf_op jit(solution)/shard_map/psum | solution.py:104
  462.4 4.9 pad_maximum_fusion.3
  467.3 11.3 %fusion.60 = (f32[3,3,60,18,1]{4,3,2,1,0:T(8,128)}, f32[3,3,60,18,1]{4,3,2,1,0:T(8,128)}) fusion(f32[3,3,60,18,128]{4,3,2,1,0:T(8,128)} %pad_maximum_fusion.3), kind=kLoop, calls=%fused_computation.133 | loop fusion | bytes 155520 | tf_op jit(solution)/shard_map/slice | solution.py:22
  478.6 4.5 copy.71
  486.0 5.2 copy.72
  493.2 5.2 copy.73
  498.4 5.3 copy.74
  503.6 16.2 %pad_maximum_fusion.1 = f32[3,3,60,18,130]{4,3,2,1,0:T(8,128)} fusion(f32[3,3,60,18,1]{4,3,2,1,0:T(8,128)} %copy.74, f32[3,3,60,1,128]{4,3,2,1,0:T(1,128)} %collective-permute-done.5, f32[1,3,60,16,128]{4,3,2,1,0:T(8,128)S(1)} %copy-done.11, f32[1,3,60,16,128]{4,3,2,1,0:T(8,128)S(1)} %get-tuple-element.51, f32[1,3,60,16,128]{4,3,2,1,0:T(8,128)} %get-tuple-element.27, ...), kind=kLoop, calls=%fused_computation.3 | loop fusion | flops 7581600 | bytes 10108800 | tf_op jit(solution)/shard_map/concatenate | solution.py:26
  519.8 10.1 %slice_bitcast_fusion.2 = (f32[3,60,18,130]{3,2,1,0:T(8,128)}, f32[3,60,18,130]{3,2,1,0:T(8,128)}, f32[3,60,18,130]{3,2,1,0:T(8,128)}) fusion(f32[3,3,60,18,130]{4,3,2,1,0:T(8,128)} %pad_maximum_fusion.1), kind=kLoop, calls=%fused_computation.8 | loop fusion | bytes 10108800 | tf_op jit(solution)/shard_map/squeeze | solution.py:98
  529.9 11.7 %fusion.24 = f32[3,60,16,128]{3,2,1,0:T(8,128)} fusion(f32[3,60,16,128]{3,2,1,0:T(8,128)S(1)} %copy-done.22, f32[3,60,16,128]{3,2,1,0:T(8,128)S(1)} %bitcast.99, f32[3,60,18,130]{3,2,1,0:T(8,128)} %get-tuple-element.34, f32[3,60,18,130]{3,2,1,0:T(8,128)} %get-tuple-element.35, f32[3,60,18,130]{3,2,1,0:T(8,128)} %get-tuple-element.33, ...), kind=kLoop, calls=%fused_computation.57 | loop fusion | flops 5898240 | bytes 16228352 | tf_op jit(solution)/shard_map/add | solution.py:102
  (163 shorter events, 95.8 us)
Async XLA Ops:
  7.2 130.2 %copy-start = (f32[256,256]{1,0:T(8,128)S(1)}, f32[256,256]{1,0:T(8,128)}, u32[]{:S(2)}) copy-start(f32[256,256]{1,0:T(8,128)} %param.22) | copy-start | bytes 786436
  13.1 38.3 %collective-permute-start = (f32[3,3,60,1,128]{4,3,2,1,0:T(1,128)}, f32[3,3,60,1,128]{4,3,2,1,0:T(1,128)}, u32[]{:S(2)}, u32[]{:S(2)}) collective-permute-start(f32[3,3,60,1,128]{4,3,2,1,0:T(1,128)} %get-tuple-element.45), channel_id=1, source_target_pairs={{0,16},{16,32},{32,48},{48,64},{64,80},{80,96},{96,112},{1,17},{17... | collective-permute-start | bytes 829448 | tf_op jit(solution)/shard_map/ppermute | solution.py:24
  17.7 5.3 copy-start.43
  17.7 33.7 %collective-permute-start.1 = (f32[3,3,60,1,128]{4,3,2,1,0:T(1,128)}, f32[3,3,60,1,128]{4,3,2,1,0:T(1,128)}, u32[]{:S(2)}, u32[]{:S(2)}) collective-permute-start(f32[3,3,60,1,128]{4,3,2,1,0:T(1,128)} %get-tuple-element.46), channel_id=1, source_target_pairs={{16,0},{32,16},{48,32},{64,48},{80,64},{96,80},{112,96},{17,1},{33... | collective-permute-start | bytes 829448 | tf_op jit(solution)/shard_map/ppermute | solution.py:25
  40.8 10.6 %copy-start.37 = (s32[16,128]{1,0:T(8,128)S(1)}, s32[16,128]{1,0:T(8,128)}, u32[]{:S(2)}) copy-start(s32[16,128]{1,0:T(8,128)} %param.15) | copy-start | bytes 24580
  40.8 81.9 %all-to-all-start = ((bf16[128,32,360]{2,1,0:T(8,128)(2,1)}), bf16[128,32,360]{2,1,0:T(8,128)(2,1)S(1)}, u32[]{:S(2)}, u32[]{:S(2)}) async-start(bf16[128,32,360]{2,1,0:T(8,128)(2,1)} %bitcast.94), calls=%async_computation | async-start | bytes 6291456 | tf_op jit(solution)/shard_map/all_to_all | solution.py:86
  51.3 409.4 %all-reduce.10.cloned.1.call-start = ((), (), s32[]{:S(2)}) async-start(), calls=%async_computation.1 | async-start | bytes 901120 | tf_op jit(solution)/shard_map/psum | solution.py:104
  72.4 13.3 %collective-permute-start.2 = (f32[3,3,60,18,1]{2,4,3,1,0:T(1,128)S(1)}, f32[3,3,60,18,1]{2,4,3,1,0:T(1,128)}, u32[]{:S(2)}, u32[]{:S(2)}) collective-permute-start(f32[3,3,60,18,1]{2,4,3,1,0:T(1,128)S(1)} %copy.64), channel_id=1, source_target_pairs={{0,1},{1,2},{2,3},{3,4},{4,5},{5,6},{6,7},{7,8},{8,9},{9,10},{10,1... | collective-permute-start | bytes 116648 | tf_op jit(solution)/shard_map/ppermute | solution.py:24
  81.5 9.4 %collective-permute-start.3 = (f32[3,3,60,18,1]{2,4,3,1,0:T(1,128)}, f32[3,3,60,18,1]{2,4,3,1,0:T(1,128)}, u32[]{:S(2)}, u32[]{:S(2)}) collective-permute-start(f32[3,3,60,18,1]{2,4,3,1,0:T(1,128)} %copy.65), channel_id=1, source_target_pairs={{1,0},{2,1},{3,2},{4,3},{5,4},{6,5},{7,6},{8,7},{9,8},{10,9},{11,1... | collective-permute-start | bytes 116648 | tf_op jit(solution)/shard_map/ppermute | solution.py:25
  135.0 4.3 copy-start.3
  170.9 11.8 %copy-start.35 = (f32[16,128]{1,0:T(8,128)S(1)}, f32[16,128]{1,0:T(8,128)}, u32[]{:S(2)}) copy-start(f32[16,128]{1,0:T(8,128)} %param.17) | copy-start | bytes 24580
  170.9 11.8 %copy-start.36 = (f32[16,128]{1,0:T(8,128)S(1)}, f32[16,128]{1,0:T(8,128)}, u32[]{:S(2)}) copy-start(f32[16,128]{1,0:T(8,128)} %param.18) | copy-start | bytes 24580
  187.5 4.9 copy-start.42
  201.8 5.9 %copy-start.24 = (f32[60,2048]{1,0:T(8,128)S(1)}, f32[60,2048]{1,0:T(8,128)}, u32[]{:S(2)}) copy-start(f32[60,2048]{1,0:T(8,128)} %copy-done.23) | copy-start | bytes 1474564
  201.9 6.1 %copy-start.7 = (f32[2048,256]{1,0:T(8,128)S(1)}, f32[2048,256]{1,0:T(8,128)}, u32[]{:S(2)}) copy-start(f32[2048,256]{1,0:T(8,128)} %copy-done.6) | copy-start | bytes 6291460
  210.2 8.1 %copy-start.19 = (f32[2048,256]{1,0:T(8,128)}, f32[2048,256]{1,0:T(8,128)S(1)}, u32[]{:S(2)}) copy-start(f32[2048,256]{1,0:T(8,128)S(1)} %get-tuple-element.65) | copy-start | bytes 6291460
  210.2 4.3 copy-start.18
  218.5 3.3 copy-start.44
  218.5 3.3 copy-start.40
  292.6 6.5 %copy-start.10 = (f32[1,3,60,16,128]{4,3,2,1,0:T(8,128)S(1)}, f32[1,3,60,16,128]{4,3,2,1,0:T(8,128)}, u32[]{:S(2)}) copy-start(f32[1,3,60,16,128]{4,3,2,1,0:T(8,128)} %get-tuple-element.52) | copy-start | bytes 4423684
  292.6 6.5 %copy-start.15 = (f32[1,3,60,16,128]{4,3,2,1,0:T(8,128)S(1)}, f32[1,3,60,16,128]{4,3,2,1,0:T(8,128)}, u32[]{:S(2)}) copy-start(f32[1,3,60,16,128]{4,3,2,1,0:T(8,128)} %get-tuple-element.27) | copy-start | bytes 4423684
  299.1 6.6 %copy-start.27 = (f32[3,59,2048]{2,1,0:T(8,128)S(1)}, f32[3,59,2048]{2,1,0:T(8,128)}, u32[]{:S(2)}) copy-start(f32[3,59,2048]{2,1,0:T(8,128)} %get-tuple-element.29) | copy-start | bytes 4349956
  299.1 6.6 %copy-start.28 = (f32[3,59,2048]{2,1,0:T(8,128)S(1)}, f32[3,59,2048]{2,1,0:T(8,128)}, u32[]{:S(2)}) copy-start(f32[3,59,2048]{2,1,0:T(8,128)} %get-tuple-element.30) | copy-start | bytes 4349956
  300.4 162.0 %collective-permute-start.4 = (f32[3,3,60,1,128]{4,3,2,1,0:T(1,128)}, f32[3,3,60,1,128]{4,3,2,1,0:T(1,128)}, u32[]{:S(2)}, u32[]{:S(2)}) collective-permute-start(f32[3,3,60,1,128]{4,3,2,1,0:T(1,128)} %get-tuple-element.43), channel_id=1, source_target_pairs={{0,16},{16,32},{32,48},{48,64},{64,80},{80,96},{96,112},{1,17},{17... | collective-permute-start | bytes 829448 | tf_op jit(solution)/shard_map/ppermute | solution.py:24
  303.8 158.5 %collective-permute-start.5 = (f32[3,3,60,1,128]{4,3,2,1,0:T(1,128)}, f32[3,3,60,1,128]{4,3,2,1,0:T(1,128)}, u32[]{:S(2)}, u32[]{:S(2)}) collective-permute-start(f32[3,3,60,1,128]{4,3,2,1,0:T(1,128)} %get-tuple-element.44), channel_id=1, source_target_pairs={{16,0},{32,16},{48,32},{64,48},{80,64},{96,80},{112,96},{17,1},{33... | collective-permute-start | bytes 829448 | tf_op jit(solution)/shard_map/ppermute | solution.py:25
  309.9 3.7 copy-start.32
  319.2 143.1 %copy-start.11 = (f32[1,3,60,16,128]{4,3,2,1,0:T(8,128)S(1)}, f32[1,3,60,16,128]{4,3,2,1,0:T(8,128)}, u32[]{:S(2)}) copy-start(f32[1,3,60,16,128]{4,3,2,1,0:T(8,128)} %get-tuple-element.52) | copy-start | bytes 4423684
  483.2 10.1 %collective-permute-start.6 = (f32[3,3,60,18,1]{2,4,3,1,0:T(1,128)S(1)}, f32[3,3,60,18,1]{2,4,3,1,0:T(1,128)}, u32[]{:S(2)}, u32[]{:S(2)}) collective-permute-start(f32[3,3,60,18,1]{2,4,3,1,0:T(1,128)S(1)} %copy.71), channel_id=1, source_target_pairs={{0,1},{1,2},{2,3},{3,4},{4,5},{5,6},{6,7},{7,8},{8,9},{9,10},{10,1... | collective-permute-start | bytes 116648 | tf_op jit(solution)/shard_map/ppermute | solution.py:24
  486.0 6.5 %copy-start.34 = (f32[180,256]{1,0:T(8,128)S(1)}, f32[180,256]{1,0:T(8,128)}, u32[]{:S(2)}) copy-start(f32[180,256]{1,0:T(8,128)} %get-tuple-element.25) | copy-start | bytes 552964
  491.2 7.2 %collective-permute-start.7 = (f32[3,3,60,18,1]{2,4,3,1,0:T(1,128)}, f32[3,3,60,18,1]{2,4,3,1,0:T(1,128)}, u32[]{:S(2)}, u32[]{:S(2)}) collective-permute-start(f32[3,3,60,18,1]{2,4,3,1,0:T(1,128)} %copy.72), channel_id=1, source_target_pairs={{1,0},{2,1},{3,2},{4,3},{5,4},{6,5},{7,6},{8,7},{9,8},{10,9},{11,1... | collective-permute-start | bytes 116648 | tf_op jit(solution)/shard_map/ppermute | solution.py:25
  519.8 10.1 %copy-start.22 = (f32[3,60,16,128]{3,2,1,0:T(8,128)S(1)}, f32[3,60,16,128]{3,2,1,0:T(8,128)}, u32[]{:S(2)}) copy-start(f32[3,60,16,128]{3,2,1,0:T(8,128)} %copy-done.21) | copy-start | bytes 4423684
  519.8 10.1 %copy-start.29 = (f32[180,16,128]{2,1,0:T(8,128)S(1)}, f32[180,16,128]{2,1,0:T(8,128)}, u32[]{:S(2)}) copy-start(f32[180,16,128]{2,1,0:T(8,128)} %slice.203) | copy-start | bytes 4423684
  (23 other events, 45.2 us)
Sparse Core Ops, SparseCore 0:
  318.6 142.0 all-reduce.9
where the time goes:
time: 556 us; the launch traced here: 549 us
  local copies, waits for them, and re-layouts  144 us (26%)
  waiting for transfers between devices  140 us (25%)
  other arithmetic  94 us (17%)
  blocking collectives  70.1 us (13%)
  matrix products  53.1 us (10%)
  starting transfers between devices  32 us (6%)
  between operations  15.1 us (3%)
    psum x1, waiting for transfers between devices, on_device(): lax.psum((totals[0], totals[1], totals[2], totals[3], totals[4], totals[5...  140 us
    psum x1, blocking collectives, on_device(): lax.psum((totals[0], totals[1], totals[2], totals[3], totals[4], totals[5...  70.1 us
    concatenate x4, other arithmetic, padded_2(): value = jnp.concatenate([before, value, after], axis=dim)  42.8 us
    slice x4, local copies, waits for them, and re-layouts, padded_2(): last = lax.slice_in_dim(value, length - width, length, axis=dim)  31.7 us
    dot_general x6, matrix products, vertical(): jnp.dot(weight_mid.T, first, precision=hp) + bias_mid[:, None]  23.4 us
    squeeze x2, local copies, waits for them, and re-layouts, on_device(): across = transport(padded[0], padded[1], padded[2], weighted)  20 us
    dot_general x6, matrix products, vertical(): jnp.dot(weight_in.T, columns, precision=hp) + bias_in[:, None]  18.3 us
    gather x1, local copies, waits for them, and re-layouts, on_device(): outgoing = stored[0][row_index]  17.1 us
  transfers between devices with their start and end apart: 10, of which 1 were waited for; matrix products, arithmetic and copies ran while one was open for 21% of the time, Pallas kernels for 0%

commit v1 on v0

v1 whole, which is shorter than its diff:
```python
import functools

import jax
import jax.numpy as jnp
import numpy as np
from jax import lax
from jax.experimental import pallas as pl
from jax.experimental.pallas import tpu as pltpu
from jax.sharding import PartitionSpec as P

NZ = 60
TRACERS = 3
PAD = 64
FEATS = TRACERS * PAD
HID = 256
SLOT = 32
HALF = SLOT // 2
CX = 16
CY = 128
DEV = 128
STORE = 4096
PLANES = 4
COLS = PLANES * CY

BF = jnp.bfloat16
F32 = jnp.float32
NT = (((1,), (1,)), ((), ()))
PARAMS = pltpu.CompilerParams(vmem_limit_bytes=56 * 2**20)

step_size = 0.25
flat_mix = 0.25
kappa_top = 1.5


def split(value):
    high = value.astype(BF)
    return high, (value - high.astype(F32)).astype(BF)


def dot(left, right):
    return jnp.dot(left, right, preferred_element_type=F32)


def dot_nt(left, right):
    return lax.dot_general(left, right, NT, preferred_element_type=F32)


def pack_kernel(counts_ref, stored_ref, late_ref, early_ref, padded):
    padded[...] = jnp.zeros_like(padded)
    for block in range(2 * TRACERS):
        padded[block * PAD : block * PAD + NZ, :] = stored_ref[block * NZ : (block + 1) * NZ, :]
    lane = lax.broadcasted_iota(jnp.int32, (SLOT, 256), 1)
    offset = lane - lax.broadcasted_iota(jnp.int32, (SLOT, 256), 0)

    def group(g, start):
        base = pl.multiple_of(jnp.minimum((start // 128) * 128, STORE - 256), 128)
        hots = []
        for i in range(4):
            hots.append(jnp.where(offset == start - base, 1.0, 0.0))
            start = start + counts_ref[0, 4 * g + i]
        hot = jnp.concatenate(hots, axis=0).astype(BF)
        low = jnp.concatenate([h[:HALF] for h in hots], axis=0).astype(BF)
        high = jnp.concatenate([h[HALF:] for h in hots], axis=0).astype(BF)
        for out_ref, first in ((late_ref, FEATS), (early_ref, 0)):
            main = dot_nt(hot, padded[first : first + 2 * PAD, pl.ds(base, 256)]).astype(BF)
            last = padded[first + 2 * PAD : first + FEATS, pl.ds(base, 256)]
            rest = jnp.concatenate([dot_nt(low, last), dot_nt(high, last)], axis=1).astype(BF)
            for i in range(4):
                out_ref[4 * g + i, :SLOT, :] = main[i * SLOT : (i + 1) * SLOT]
                out_ref[4 * g + i, SLOT:, :] = rest[i * HALF : (i + 1) * HALF]
        return start

    lax.fori_loop(0, DEV // 4, group, jnp.int32(0))


def pack(counts, stored_t):
    out = jax.ShapeDtypeStruct((DEV, SLOT + HALF, 128), BF)
    return pl.pallas_call(
        pack_kernel,
        out_shape=(out, out),
        in_specs=[pl.BlockSpec(memory_space=pltpu.SMEM), pl.BlockSpec(memory_space=pltpu.VMEM)],
        out_specs=(pl.BlockSpec(memory_space=pltpu.VMEM),) * 2,
        scratch_shapes=[pltpu.VMEM((2 * FEATS, STORE), BF)],
        compiler_params=PARAMS,
        name="pack",
    )(counts, stored_t)


def weights_kernel(w1_ref, b1_ref, w2_ref, w3t_ref, f1_ref, f2_ref, f3_ref, r3_ref, r2_ref, r1_ref, wide, tall):
    wide[...] = jnp.zeros_like(wide)
    for t in range(TRACERS):
        wide[t * PAD : t * PAD + NZ, :] = w1_ref[t * NZ : (t + 1) * NZ, :]
    high, low = split(wide[...])
    r1_ref[:FEATS, :] = high
    r1_ref[FEATS:, :] = low
    wide[NZ : NZ + 1, :] = b1_ref[...]
    high, low = split(wide[...].T)
    f1_ref[:HID, :] = high
    f1_ref[HID:, :] = low
    high, low = split(w2_ref[...])
    r2_ref[:HID, :] = high
    r2_ref[HID:, :] = low
    high, low = split(w2_ref[...].T)
    f2_ref[:HID, :] = high
    f2_ref[HID:, :] = low
    tall[...] = jnp.zeros_like(tall)
    tall[:NZ, :] = w3t_ref[...]
    high, low = split(tall[:PAD, :])
    f3_ref[:PAD, :] = high
    f3_ref[PAD:, :] = low
    tall[PAD : 2 * PAD, :] = tall[:PAD, :]
    tall[2 * PAD :, :] = tall[:PAD, :]
    high, low = split(tall[...].T)
    lane = lax.broadcasted_iota(jnp.int32, high.shape, 1)
    middle = (lane >= PAD) & (lane < 2 * PAD)
    r3_ref[...] = jnp.where(middle, low.astype(F32), high.astype(F32)).astype(BF)


def weights(w1, b1, w2, w3t):
    shapes = ((2 * HID, FEATS), (2 * HID, HID), (2 * PAD, HID), (HID, FEATS), (2 * HID, HID), (2 * FEATS, HID))
    return pl.pallas_call(
        weights_kernel,
        out_shape=tuple(jax.ShapeDtypeStruct(s, BF) for s in shapes),
        scratch_shapes=[pltpu.VMEM((FEATS, HID), F32), pltpu.VMEM((FEATS, HID), F32)],
        compiler_params=PARAMS,
        name="weights",
    )(w1, b1, w2, w3t)


def edge_plane(x, plane, mask_row, fx_row, fy_row, ew_ref, ee_ref):
    weighted = plane * mask_row
    lane = lax.broadcasted_iota(jnp.int32, plane.shape, 1)
    west = pltpu.roll(weighted * (flat_mix + 0.5 * fy_row), x, 1)
    east = pltpu.roll(weighted * (flat_mix - 0.5 * fy_row), x + 1, 1)
    ew_ref[...] = jnp.where(lane == x, west, ew_ref[...])
    ee_ref[...] = jnp.where(lane == x, east, ee_ref[...])


def north_edge(plane, mask_row, fx_row):
    return plane * mask_row * (flat_mix + 0.5 * fx_row)


def south_edge(plane, mask_row, fx_row):
    return plane * mask_row * (flat_mix - 0.5 * fx_row)


def edges_kernel(raw_ref, mask_ref, fx_ref, fy_ref, planes_ref, en_ref, es_ref, ew_ref, ee_ref):
    planes_ref[...] = jnp.zeros_like(planes_ref)
    ew_ref[...] = jnp.zeros_like(ew_ref)
    ee_ref[...] = jnp.zeros_like(ee_ref)
    for x in range(CX):
        for t in range(TRACERS):
            planes_ref[x, t * PAD : t * PAD + NZ, :] = raw_ref[pl.ds(t * NZ * CX + x, NZ, stride=CX), :]
        mask_row = mask_ref[x : x + 1, :].astype(F32)
        edge_plane(x, planes_ref[x], mask_row, None, fy_ref[x : x + 1, :], ew_ref, ee_ref)
    en_ref[...] = north_edge(planes_ref[0], mask_ref[0:1, :].astype(F32), fx_ref[0:1, :])
    es_ref[...] = south_edge(planes_ref[CX - 1], mask_ref[CX - 1 :, :].astype(F32), fx_ref[CX - 1 :, :])


EDGE = jax.ShapeDtypeStruct((FEATS, CY), F32)
PLANE = jax.ShapeDtypeStruct((CX, FEATS, CY), F32)


def edges(raw, mask, fx, fy):
    return pl.pallas_call(
        edges_kernel,
        out_shape=(PLANE, EDGE, EDGE, EDGE, EDGE),
        compiler_params=PARAMS,
        name="edges",
    )(raw, mask, fx, fy)


def stencil_plane(x, lam_ref, mask_ref, fx_ref, fy_ref, hn_ref, hs_ref, hw_ref, he_ref):
    def row(ref, at):
        return ref[at : at + 1, :].astype(F32)

    plane = lam_ref[x]
    weighted = plane * row(mask_ref, x)
    if x < CX - 1:
        total = north_edge(lam_ref[x + 1], row(mask_ref, x + 1), row(fx_ref, x + 1))
    else:
        total = hn_ref[...]
    if x > 0:
        total = total + south_edge(lam_ref[x - 1], row(mask_ref, x - 1), row(fx_ref, x - 1))
    else:
        total = total + hs_ref[...]
    lane = lax.broadcasted_iota(jnp.int32, plane.shape, 1)
    fy = row(fy_ref, x)
    west = pltpu.roll(weighted * (flat_mix + 0.5 * fy), CY - 1, 1)
    total = total + jnp.where(lane == CY - 1, pltpu.roll(hw_ref[...], CY - 1 - x, 1), west)
    east = pltpu.roll(weighted * (flat_mix - 0.5 * fy), 1, 1)
    from_east = he_ref[...] if x == 0 else pltpu.roll(he_ref[...], CY - x, 1)
    total = total + jnp.where(lane == 0, from_east, east)
    return plane, total - weighted


def first_kernel(lam_ref, mask_ref, fx_ref, fy_ref, hn_ref, hs_ref, hw_ref, he_ref, out_ref):
    for x in range(CX):
        plane, total = stencil_plane(x, lam_ref, mask_ref, fx_ref, fy_ref, hn_ref, hs_ref, hw_ref, he_ref)
        out_ref[x] = plane + step_size * total


def first_stencil(lam, mask, fx, fy, halos):
    return pl.pallas_call(first_kernel, out_shape=PLANE, compiler_params=PARAMS, name="stencil1")(
        lam, mask, fx, fy, *halos
    )


def last_kernel(lam_ref, down_ref, mask_ref, fx_ref, fy_ref, hn_ref, hs_ref, hw_ref, he_ref, out_ref):
    for x in range(CX):
        plane, total = stencil_plane(x, lam_ref, mask_ref, fx_ref, fy_ref, hn_ref, hs_ref, hw_ref, he_ref)
        value = plane + step_size * (total + down_ref[x])
        for t in range(TRACERS):
            out_ref[pl.ds(t * NZ * CX + x, NZ, stride=CX), :] = value[t * PAD : t * PAD + NZ]


def last_stencil(lam, down, mask, fx, fy, halos):
    return pl.pallas_call(
        last_kernel,
        out_shape=jax.ShapeDtypeStruct((TRACERS * NZ * CX, CY), F32),
        compiler_params=PARAMS,
        name="stencil0",
    )(lam, down, mask, fx, fy, *halos)


def closure_kernel(first, *refs):
    (owner_ref, mask_ref, got_ref, lam_ref, f1_ref, f2_ref, f3_ref, r3_ref, r2_ref, r1_ref, b2_ref, b3_ref) = refs[:12]
    refs = refs[12:]
    if first:
        fx_ref, fy_ref, base_ref, out_ref, grads_ref, en_ref, es_ref, ew_ref, ee_ref = refs[:9]
        refs = refs[9:]
    else:
        before_ref, out_ref, grads_ref = refs[:3]
        refs = refs[3:]
    rows_ref, total = refs
    block = pl.program_id(0)

    @pl.when(block == 0)
    def _():
        for half in range(2):
            for g in range(DEV // 8):
                at = half * (STORE // 2) + g * 128
                main = [got_ref[8 * g + i, half * HALF : (half + 1) * HALF, :] for i in range(8)]
                rows_ref[: 2 * PAD, at : at + 128] = jnp.concatenate(main, axis=0).T
        for g in range(DEV // 8):
            rest = [got_ref[8 * g + i, SLOT:, :] for i in range(8)]
            both = jnp.concatenate(rest, axis=0).T
            rows_ref[2 * PAD :, g * 128 : (g + 1) * 128] = both[:PAD]
            at = STORE // 2 + g * 128
            rows_ref[2 * PAD :, at : at + 128] = both[PAD:]
        if first:
            total[...] = jnp.zeros_like(total)
            ew_ref[...] = jnp.zeros_like(ew_ref)
            ee_ref[...] = jnp.zeros_like(ee_ref)
        else:
            total[...] = before_ref[...]

    x0 = block * PLANES

    def wide(ref):
        return jnp.concatenate([ref[pl.ds(x0 + i, 1), :] for i in range(PLANES)], axis=1)

    owner = wide(owner_ref)
    at = ((owner >> 4) & 1) * (STORE // 2) + (owner >> 5) * HALF + (owner & (HALF - 1))
    level = lax.broadcasted_iota(jnp.int32, (256, COLS), 0)
    picked = None
    for k in range(STORE // 256):
        hot = jnp.where(level == at - 256 * k, 1.0, 0.0).astype(BF)
        part = dot(rows_ref[:, 256 * k : 256 * (k + 1)], hot)
        picked = part if picked is None else picked + part
    row = lax.broadcasted_iota(jnp.int32, (FEATS, COLS), 0)
    inputs = jnp.where(row == NZ, 1.0, picked).astype(BF)

    both = dot(f1_ref[...], inputs)
    h1 = jnp.tanh(both[:HID] + both[HID:])
    h1_high, h1_low = split(h1)
    both = dot(f2_ref[...], h1_high)
    h2 = jnp.tanh(both[:HID] + both[HID:] + dot(f2_ref[:HID], h1_low) + b2_ref[...])
    h2_high, h2_low = split(h2)
    both = dot(f3_ref[...], h2_high)
    sig = jax.nn.sigmoid(both[:PAD] + both[PAD:] + dot(f3_ref[:PAD], h2_low) + b3_ref[...])
    inner = lax.broadcasted_iota(jnp.int32, (PAD, COLS), 0) < NZ - 1
    kappa = jnp.where(inner, kappa_top * sig, 0.0)

    mask_row = wide(mask_ref).astype(F32)
    slope = jnp.zeros((PAD, COLS), F32)
    direct = []
    for t in range(TRACERS):
        lo, hi = t * PAD, (t + 1) * PAD
        mu = jnp.concatenate([lam_ref[i, lo:hi, :] for i in range(PLANES)], axis=1) * mask_row
        gap = mu - pltpu.roll(mu, PAD - 1, 0)
        column = picked[lo:hi]
        slope = slope + gap * (pltpu.roll(column, PAD - 1, 0) - column)
        flow = kappa * gap
        direct.append(pltpu.roll(flow, 1, 0) - flow)
    d3 = slope * kappa * (1.0 - sig)
    d3_high, d3_low = split(d3)
    d2 = dot(r3_ref[...], jnp.concatenate([d3_high, d3_high, d3_low], axis=0)) * (1.0 - h2 * h2)
    d2_high, d2_low = split(d2)
    both = dot(r2_ref[...], d2_high)
    d1 = (both[:HID] + both[HID:] + dot(r2_ref[:HID], d2_low)) * (1.0 - h1 * h1)
    d1_high, d1_low = split(d1)
    both = dot(r1_ref[...], d1_high)
    d0 = both[:FEATS] + both[FEATS:] + dot(r1_ref[:FEATS], d1_low)

    ones = jnp.ones((16, COLS), BF)
    total[:FEATS, :] += dot_nt(inputs, d1_high) + dot_nt(inputs, d1_low)
    both = dot_nt(jnp.concatenate([h1_high, h1_low, ones], axis=0), d2_high)
    other = dot_nt(jnp.concatenate([h1_high, ones], axis=0), d2_low)
    total[FEATS : FEATS + HID, :] += both[:HID] + both[HID : 2 * HID] + other[:HID]
    total[NZ + 1 : NZ + 2, :] += both[2 * HID : 2 * HID + 1] + other[HID : HID + 1]
    d3_both = jnp.concatenate([d3_high, d3_low], axis=0)
    both = dot_nt(d3_both, h2_high)
    total[FEATS + HID :, :] += both[:PAD] + both[PAD:] + dot_nt(d3_high, h2_low)
    both = dot_nt(ones, d3_both)
    total[NZ + 2 : NZ + 3, :PAD] += both[:1, :PAD] + both[:1, PAD:]

    for i in range(PLANES):
        part = slice(i * CY, (i + 1) * CY)
        for t in range(TRACERS):
            lo, hi = t * PAD, (t + 1) * PAD
            down = d0[lo:hi, part] + direct[t][:, part]
            if first:
                out_ref[i, lo:hi, :] = base_ref[i, lo:hi, :] + step_size * down
            else:
                out_ref[i, lo:hi, :] = down
        if first:
            x = x0 + i
            edge_plane(
                x, out_ref[i], mask_ref[pl.ds(x, 1), :].astype(F32), None, fy_ref[pl.ds(x, 1), :], ew_ref, ee_ref
            )

    if first:

        @pl.when(block == 0)
        def _():
            en_ref[...] = north_edge(out_ref[0], mask_ref[0:1, :].astype(F32), fx_ref[0:1, :])

    @pl.when(block == CX // PLANES - 1)
    def _():
        if first:
            es_ref[...] = south_edge(out_ref[PLANES - 1], mask_ref[CX - 1 :, :].astype(F32), fx_ref[CX - 1 :, :])
            grads_ref[...] = total[...]
        else:
            grads_ref[: 2 * HID, :] = total[:, :128]
            grads_ref[2 * HID :, :] = total[:, 128:]


def closure(first, owners, mask, got, lam, split_weights, b2, b3, *extra):
    whole = pl.BlockSpec(memory_space=pltpu.VMEM)
    planes = pl.BlockSpec((PLANES, FEATS, CY), lambda b: (b, 0, 0))
    in_specs = [whole, whole, whole, planes] + [whole] * 8
    if first:
        in_specs += [whole, whole, planes]
        out_shape = (PLANE, jax.ShapeDtypeStruct((2 * HID, HID), F32), EDGE, EDGE, EDGE, EDGE)
        out_specs = (planes,) + (whole,) * 5
    else:
        in_specs += [whole]
        out_shape = (PLANE, jax.ShapeDtypeStruct((4 * HID, 128), F32))
        out_specs = (planes, whole)
    return pl.pallas_call(
        functools.partial(closure_kernel, first),
        grid=(CX // PLANES,),
        out_shape=out_shape,
        in_specs=in_specs,
        out_specs=out_specs,
        scratch_shapes=[pltpu.VMEM((FEATS, STORE), BF), pltpu.VMEM((2 * HID, HID), F32)],
        compiler_params=PARAMS,
        name="closure1" if first else "closure0",
    )(owners, mask, got, lam, *split_weights, b2, b3, *extra)


def sum_kernel(parts_ref, out_ref):
    value = parts_ref[0:8, :]
    for i in range(1, DEV):
        value = value + parts_ref[8 * i : 8 * i + 8, :]
    for i in range(DEV):
        out_ref[8 * i : 8 * i + 8, :] = value


def unpack_kernel(scale, sums_ref, w1_ref, b1_ref, w2_ref, b2_ref, w3t_ref, b3_ref):
    for part in range(2):
        lanes = slice(part * 128, (part + 1) * 128)
        top = part * 2 * HID
        for t in range(TRACERS):
            w1_ref[t * NZ : (t + 1) * NZ, lanes] = sums_ref[top + t * PAD : top + t * PAD + NZ, :] * scale
        b1_ref[:, lanes] = sums_ref[top + NZ : top + NZ + 1, :] * scale
        b2_ref[:, lanes] = sums_ref[top + NZ + 1 : top + NZ + 2, :] * scale
        w2_ref[:, lanes] = sums_ref[top + FEATS : top + FEATS + HID, :] * scale
        w3t_ref[:, lanes] = sums_ref[top + FEATS + HID : top + FEATS + HID + NZ, :] * scale
    b3_ref[...] = sums_ref[NZ + 2 : NZ + 3, :NZ] * scale


def reduce_params(packed, count):
    parts = lax.all_to_all(packed, ("gx", "gy"), split_axis=0, concat_axis=0, tiled=True)
    spread = pl.pallas_call(
        sum_kernel, out_shape=jax.ShapeDtypeStruct(packed.shape, F32), compiler_params=PARAMS, name="sum"
    )(parts)
    sums = lax.all_to_all(spread, ("gx", "gy"), split_axis=0, concat_axis=0, tiled=True)
    shapes = ((TRACERS * NZ, HID), (1, HID), (HID, HID), (1, HID), (NZ, HID), (1, NZ))
    return pl.pallas_call(
        functools.partial(unpack_kernel, step_size / float(np.sqrt(count))),
        out_shape=tuple(jax.ShapeDtypeStruct(s, F32) for s in shapes),
        compiler_params=PARAMS,
        name="unpack",
    )(sums)


def exchange(north, south, west, east):
    gx, gy = lax.axis_size("gx"), lax.axis_size("gy")
    down_x = [(i + 1, i) for i in range(gx - 1)]
    up_x = [(i, i + 1) for i in range(gx - 1)]
    down_y = [(i + 1, i) for i in range(gy - 1)]
    up_y = [(i, i + 1) for i in range(gy - 1)]
    return (
        lax.ppermute(north, "gx", down_x),
        lax.ppermute(south, "gx", up_x),
        lax.ppermute(west, "gy", down_y),
        lax.ppermute(east, "gy", up_y),
    )


def on_device(
    stored,
    counts,
    owners,
    land_mask,
    flow_x,
    flow_y,
    costate,
    weight_in,
    bias_in,
    weight_mid,
    bias_mid,
    weight_out,
    bias_out,
):
    late, early = pack(counts, stored[0].T)
    late = lax.all_to_all(late, ("gx", "gy"), split_axis=0, concat_axis=0, tiled=True)
    early = lax.all_to_all(early, ("gx", "gy"), split_axis=0, concat_axis=0, tiled=True)
    split_weights = weights(weight_in, bias_in[None, :], weight_mid, weight_out.T)
    b2 = bias_mid[:, None]
    b3 = jnp.pad(bias_out, (0, PAD - NZ))[:, None]
    planes, *sides = edges(costate.reshape(TRACERS * NZ * CX, CY), land_mask, flow_x, flow_y)
    halos = exchange(*sides)
    base = first_stencil(planes, land_mask, flow_x, flow_y, halos)
    lam, grads, *sides = closure(
        True, owners, land_mask, late, planes, split_weights, b2, b3, flow_x, flow_y, base
    )
    halos = exchange(*sides)
    down, packed = closure(False, owners, land_mask, early, lam, split_weights, b2, b3, grads)
    adjoint = last_stencil(lam, down, land_mask, flow_x, flow_y, halos)
    count = CX * CY * lax.axis_size("gx") * lax.axis_size("gy")
    g1, gb1, g2, gb2, g3, gb3 = reduce_params(packed, count)
    return (adjoint.reshape(costate.shape), g1, gb1[0], g2, gb2[0], g3.T, gb3[0])


def solution(mesh):
    in_specs = (
        P(("gx", "gy"), None, None),
        P(("gx", "gy"), None),
        P("gx", "gy"),
        P("gx", "gy"),
        P("gx", "gy"),
        P("gx", "gy"),
        P(None, None, "gx", "gy"),
        P(),
        P(),
        P(),
        P(),
        P(),
        P(),
    )
    out_specs = (P(None, None, "gx", "gy"), P(), P(), P(), P(), P(), P())
    return jax.shard_map(
        on_device, mesh=mesh, in_specs=in_specs, out_specs=out_specs, check_vma=False
    )
```

time: 556 us -> 172 us (0.31)
  the two profiles are of different devices: /device:TPU:1 before, /device:TPU:33 now
where the time goes in v1:
time: 172 us; the launch traced here: 171 us
  Pallas kernels  66.5 us (39%)
  blocking collectives  54.4 us (32%)
  starting transfers between devices  34.5 us (20%)
  waiting for transfers between devices  10.4 us (6%)
  local copies, waits for them, and re-layouts  4.72 us (3%)
    pallas_call x2, Pallas kernels, closure(): pl.pallas_call(functools.partial(closure_kernel, first), grid=(CX // PLAN...  34.5 us
    all_to_all x1, blocking collectives, on_device(): lax.all_to_all(late, ('gx', 'gy'), split_axis=0, concat_axis=0, tiled=True)  34.3 us
    all_to_all x1, blocking collectives, reduce_params(): lax.all_to_all(packed, ('gx', 'gy'), split_axis=0, concat_axis=0, tiled=T...  20.1 us
    pallas_call x1, Pallas kernels, pack(): pl.pallas_call(pack_kernel, out_shape=(out, out), in_specs=[pl.BlockSpec(...  12.7 us
    ppermute x2, waiting for transfers between devices, exchange(): lax.ppermute(east, 'gy', up_y)  8.88 us
    ppermute x2, starting transfers between devices, exchange(): lax.ppermute(west, 'gy', down_y)  8.16 us
    ppermute x2, starting transfers between devices, exchange(): lax.ppermute(south, 'gx', up_x)  6.59 us
    all_to_all x1, starting transfers between devices, reduce_params(): lax.all_to_all(spread, ('gx', 'gy'), split_axis=0, concat_axis=0, tiled=T...  5.82 us
  transfers between devices with their start and end apart: 10, of which 4 were waited for; matrix products, arithmetic and copies ran while one was open for 1% of the time, Pallas kernels for 19%

profile of v1, /device:TPU:33, one launch (start us, length us, event | category | flops | bytes accessed | tf_op | source)
XLA Modules:
  0.0 171.4 jit_solution(16464407215516951981)
XLA Ops:
  0.6 12.7 %pack.1 = (bf16[128,48,128]{2,1,0:T(8,128)(2,1)}, bf16[128,48,128]{2,1,0:T(8,128)(2,1)}) custom-call(s32[1,128]{1,0:T(1,128)} %counts_ref.1, bf16[360,4096]{1,0:T(8,128)(2,1)} %bitcast.18), custom_call_target="tpu_custom_call" | custom-call | tf_op jit(solution)/shard_map/pack/pallas_call | solution.py:78
  13.3 34.3 %all_to_all.32.refs_2_ = bf16[128,48,128]{2,1,0:T(8,128)(2,1)} all-to-all(bf16[128,48,128]{2,1,0:T(8,128)(2,1)} %get-tuple-element.34), channel_id=1, replica_groups=mesh['gx'=8,'gy'=16] {'gx','gy'}, dimensions={0} | all-to-all | bytes 3145728 | tf_op jit(solution)/shard_map/all_to_all | solution.py:439
  47.6 5.6 %all-to-all-start.1 = ((bf16[128,48,128]{2,1,0:T(8,128)(2,1)}), bf16[128,48,128]{2,1,0:T(8,128)(2,1)S(1)}, u32[]{:S(2)}, u32[]{:S(2)}) async-start(bf16[128,48,128]{2,1,0:T(8,128)(2,1)} %get-tuple-element.47), calls=%async_computation.1 | async-start | bytes 3145728 | tf_op jit(solution)/shard_map/all_to_all | solution.py:440
  53.2 3.6 %edges.1 = (f32[16,192,128]{2,1,0:T(8,128)}, f32[192,128]{1,0:T(8,128)}, f32[192,128]{1,0:T(8,128)}, f32[192,128]{1,0:T(8,128)}, f32[192,128]{1,0:T(8,128)}) custom-call(f32[2880,128]{1,0:T(8,128)} %bitcast.22, s32[16,128]{1,0:T(8,128)} %mask_ref.5, f32[16,128]{1,0:T(8,128)} %fx_ref.5, f32[16,128]{1,0:T(8,128)} %fy_ref.5), custom_call_target="tpu_custom_call" | custom-call | tf_op jit(solution)/shard_map/edges/pallas_call | solution.py:165
  56.8 2.3 %collective-permute-start = (f32[192,128]{1,0:T(8,128)}, f32[192,128]{1,0:T(8,128)S(1)}, u32[]{:S(2)}, u32[]{:S(2)}) collective-permute-start(f32[192,128]{1,0:T(8,128)} %get-tuple-element.42), channel_id=1, source_target_pairs={{16,0},{32,16},{48,32},{64,48},{80,64},{96,80},{112,96},{17,1},{33... | collective-permute-start | bytes 294920 | tf_op jit(solution)/shard_map/ppermute | solution.py:416
  59.1 3.3 %collective-permute-start.1 = (f32[192,128]{1,0:T(8,128)}, f32[192,128]{1,0:T(8,128)S(1)}, u32[]{:S(2)}, u32[]{:S(2)}) collective-permute-start(f32[192,128]{1,0:T(8,128)} %get-tuple-element.43), channel_id=1, source_target_pairs={{0,16},{16,32},{32,48},{48,64},{64,80},{80,96},{96,112},{1,17},{17... | collective-permute-start | bytes 294920 | tf_op jit(solution)/shard_map/ppermute | solution.py:417
  62.4 4.1 %collective-permute-start.2 = (f32[192,128]{1,0:T(8,128)}, f32[192,128]{1,0:T(8,128)S(1)}, u32[]{:S(2)}, u32[]{:S(2)}) collective-permute-start(f32[192,128]{1,0:T(8,128)} %get-tuple-element.44), channel_id=1, source_target_pairs={{1,0},{2,1},{3,2},{4,3},{5,4},{6,5},{7,6},{8,7},{9,8},{10,9},{11,1... | collective-permute-start | bytes 294920 | tf_op jit(solution)/shard_map/ppermute | solution.py:418
  66.5 1.9 %collective-permute-start.3 = (f32[192,128]{1,0:T(8,128)}, f32[192,128]{1,0:T(8,128)S(1)}, u32[]{:S(2)}, u32[]{:S(2)}) collective-permute-start(f32[192,128]{1,0:T(8,128)} %get-tuple-element.45), channel_id=1, source_target_pairs={{0,1},{1,2},{2,3},{3,4},{4,5},{5,6},{6,7},{7,8},{8,9},{9,10},{10,1... | collective-permute-start | bytes 294920 | tf_op jit(solution)/shard_map/ppermute | solution.py:419
  68.4 0.7 copy.23.refs_11_
  69.1 0.8 copy.22.refs_10_
  69.9 2.2 %weights.1 = (bf16[512,192]{1,0:T(8,128)(2,1)}, bf16[512,256]{1,0:T(8,128)(2,1)}, bf16[128,256]{1,0:T(8,128)(2,1)}, bf16[256,192]{1,0:T(8,128)(2,1)}, bf16[512,2...) custom-call(f32[180,256]{1,0:T(8,128)} %w1_ref.1, f32[1,256]{1,0:T(1,128)} %bitcast.27, f32[256,256]{1,0:T(8,128)} %w2_ref.1, ...), custom_call_target="tpu_custom_call" | custom-call | tf_op jit(solution)/shard_map/weights/pallas_call | solution.py:121
  72.2 1.3 collective-permute-done.2.hw_ref
  73.4 2.5 %collective-permute-done.3.he_ref = f32[192,128]{1,0:T(8,128)S(1)} collective-permute-done((f32[192,128]{1,0:T(8,128)}, f32[192,128]{1,0:T(8,128)S(1)}, u32[]{:S(2)}, u32[]{:S(2)}) %collective-permute-start.3) | collective-permute-done | bytes 98336 | tf_op jit(solution)/shard_map/ppermute | solution.py:419
  76.0 0.6 copy-done.5
  76.6 4.3 %stencil1.1.refs_14_ = f32[16,192,128]{2,1,0:T(8,128)} custom-call(f32[16,192,128]{2,1,0:T(8,128)} %get-tuple-element.35.lam_ref.refs_3_, s32[16,128]{1,0:T(8,128)} %mask_ref.5, f32[16,128]{1,0:T(8,128)} %fx_ref.5, f32[16,128]{1,0:T(8,128)} %fy_ref.5, f32[192,128]{1,0:T(8,128)} %copy-done.2, f32[192,128]{1,0:T(8,128)} %copy-done.3, f32[192,128]{1,0:T(8,128)} %copy-done.4, ...), custom_call_target="tpu_custom_call" | custom-call | tf_op jit(solution)/shard_map/stencil1/pallas_call | solution.py:204
  80.9 17.4 %closure1.1 = (f32[16,192,128]{2,1,0:T(8,128)}, f32[512,256]{1,0:T(8,128)}, f32[192,128]{1,0:T(8,128)}, f32[192,128]{1,0:T(8,128)}, f32[192,128]{1,0:T(8,128)}, /*index=5*/f32[192,128]{1,0:T(8,128)}) custom-call(s32[16,128]{1,0:T(8,128)} %refs_0_.3, s32[16,128]{1,0:T(8,128)} %mask_ref.5, bf16[128,48,128]{2,1,0:T(8,128)(2,1)} %all_to_all.32.refs_2_, ...), custom_call_target="tpu_custom_call" | custom-call | tf_op jit(solution)/shard_map/closure1/pallas_call | solution.py:361
  98.3 1.1 copy-done
  99.5 17.1 %closure0.1 = (f32[16,192,128]{2,1,0:T(8,128)}, f32[1024,128]{1,0:T(8,128)}) custom-call(s32[16,128]{1,0:T(8,128)} %refs_0_.3, s32[16,128]{1,0:T(8,128)} %mask_ref.5, bf16[128,48,128]{2,1,0:T(8,128)(2,1)} %copy-done, f32[16,192,128]{2,1,0:T(8,128)} %get-tuple-element.46.refs_3_.lam_ref, bf16[512,192]{1,0:T(8,128)(2,1)} %get-tuple-element.36.refs_4_, ...), custom_call_target="tpu_custom_call" | custom-call | tf_op jit(solution)/shard_map/closure0/pallas_call | solution.py:361
  116.6 20.1 %all_to_all.33 = f32[128,8,128]{2,1,0:T(8,128)} all-to-all(f32[128,8,128]{2,1,0:T(8,128)} %bitcast.24), channel_id=1, replica_groups=mesh['gx'=8,'gy'=16] {'gx','gy'}, dimensions={0} | all-to-all | bytes 1048576 | tf_op jit(solution)/shard_map/all_to_all | solution.py:395
  136.8 2.0 %sum.1 = f32[1024,128]{1,0:T(8,128)} custom-call(f32[1024,128]{1,0:T(8,128)} %bitcast.21), custom_call_target="tpu_custom_call" | custom-call | tf_op jit(solution)/shard_map/sum/pallas_call | solution.py:396
  138.7 5.8 %all-to-all-start.3 = ((f32[128,8,128]{2,1,0:T(8,128)}), f32[128,8,128]{2,1,0:T(8,128)S(1)}, u32[]{:S(2)}, u32[]{:S(2)}) async-start(f32[128,8,128]{2,1,0:T(8,128)} %bitcast.20), calls=%async_computation.3 | async-start | bytes 1048576 | tf_op jit(solution)/shard_map/all_to_all | solution.py:399
  144.6 2.3 %collective-permute-start.4 = (f32[192,128]{1,0:T(8,128)S(1)}, f32[192,128]{1,0:T(8,128)S(1)}, u32[]{:S(2)}, u32[]{:S(2)}) collective-permute-start(f32[192,128]{1,0:T(8,128)S(1)} %copy-done.14), channel_id=1, source_target_pairs={{16,0},{32,16},{48,32},{64,48},{80,64},{96,80},{112,96},{17,1},{33... | collective-permute-start | bytes 294920 | tf_op jit(solution)/shard_map/ppermute | solution.py:416
  146.9 3.3 %collective-permute-start.5 = (f32[192,128]{1,0:T(8,128)S(1)}, f32[192,128]{1,0:T(8,128)S(1)}, u32[]{:S(2)}, u32[]{:S(2)}) collective-permute-start(f32[192,128]{1,0:T(8,128)S(1)} %copy-done.13), channel_id=1, source_target_pairs={{0,16},{16,32},{32,48},{48,64},{64,80},{80,96},{96,112},{1,17},{17... | collective-permute-start | bytes 294920 | tf_op jit(solution)/shard_map/ppermute | solution.py:417
  150.2 4.1 %collective-permute-start.6 = (f32[192,128]{1,0:T(8,128)S(1)}, f32[192,128]{1,0:T(8,128)S(1)}, u32[]{:S(2)}, u32[]{:S(2)}) collective-permute-start(f32[192,128]{1,0:T(8,128)S(1)} %copy-done.12), channel_id=1, source_target_pairs={{1,0},{2,1},{3,2},{4,3},{5,4},{6,5},{7,6},{8,7},{9,8},{10,9},{11,1... | collective-permute-start | bytes 294920 | tf_op jit(solution)/shard_map/ppermute | solution.py:418
  154.3 1.9 %collective-permute-start.7 = (f32[192,128]{1,0:T(8,128)S(1)}, f32[192,128]{1,0:T(8,128)S(1)}, u32[]{:S(2)}, u32[]{:S(2)}) collective-permute-start(f32[192,128]{1,0:T(8,128)S(1)} %copy-done.11), channel_id=1, source_target_pairs={{0,1},{1,2},{2,3},{3,4},{4,5},{5,6},{6,7},{7,8},{8,9},{9,10},{10,1... | collective-permute-start | bytes 294920 | tf_op jit(solution)/shard_map/ppermute | solution.py:419
  156.2 0.0 copy-start.6
  156.3 0.2 collective-permute-done.6.hw_ref
  156.5 6.3 %collective-permute-done.7.he_ref = f32[192,128]{1,0:T(8,128)S(1)} collective-permute-done((f32[192,128]{1,0:T(8,128)S(1)}, f32[192,128]{1,0:T(8,128)S(1)}, u32[]{:S(2)}, u32[]{:S(2)}) %collective-permute-start.7) | collective-permute-done | bytes 98336 | tf_op jit(solution)/shard_map/ppermute | solution.py:419
  162.8 0.6 copy-done.9
  163.5 5.3 %stencil0.1 = f32[2880,128]{1,0:T(8,128)} custom-call(f32[16,192,128]{2,1,0:T(8,128)} %get-tuple-element.46.refs_3_.lam_ref, f32[16,192,128]{2,1,0:T(8,128)} %get-tuple-element.49.down_ref, s32[16,128]{1,0:T(8,128)} %mask_ref.5, f32[16,128]{1,0:T(8,128)} %fx_ref.5, f32[16,128]{1,0:T(8,128)} %fy_ref.5, f32[192,128]{1,0:T(8,128)} %copy-done.6, ...), custom_call_target="tpu_custom_call" | custom-call | tf_op jit(solution)/shard_map/stencil0/pallas_call | solution.py:218
  168.8 0.8 copy-done.1
  169.5 1.9 %unpack.1 = (f32[180,256]{1,0:T(8,128)}, f32[1,256]{1,0:T(1,128)}, f32[256,256]{1,0:T(8,128)}, f32[1,256]{1,0:T(1,128)}, f32[60,256]{1,0:T(8,128)}, /*index=5*/f32[1,60]{1,0:T(1,128)}) custom-call(f32[1024,128]{1,0:T(8,128)} %bitcast.19), custom_call_target="tpu_custom_call" | custom-call | tf_op jit(solution)/shard_map/unpack/pallas_call | solution.py:401
  (34 shorter events, 0.1 us)
Async XLA Ops:
  47.6 20.8 %copy-start.15 = (f32[60]{0:T(128)S(1)}, f32[60]{0:T(128)}, u32[]{:S(2)}) copy-start(f32[60]{0:T(128)} %param.25) | copy-start | bytes 724
  47.6 21.5 %copy-start.10 = (f32[256]{0:T(256)S(1)}, f32[256]{0:T(256)}, u32[]{:S(2)}) copy-start(f32[256]{0:T(256)} %param.23) | copy-start | bytes 3076
  47.6 50.7 %all-to-all-start.1 = ((bf16[128,48,128]{2,1,0:T(8,128)(2,1)}), bf16[128,48,128]{2,1,0:T(8,128)(2,1)S(1)}, u32[]{:S(2)}, u32[]{:S(2)}) async-start(bf16[128,48,128]{2,1,0:T(8,128)(2,1)} %get-tuple-element.47), calls=%async_computation.1 | async-start | bytes 3145728 | tf_op jit(solution)/shard_map/all_to_all | solution.py:440
  56.8 15.3 %collective-permute-start = (f32[192,128]{1,0:T(8,128)}, f32[192,128]{1,0:T(8,128)S(1)}, u32[]{:S(2)}, u32[]{:S(2)}) collective-permute-start(f32[192,128]{1,0:T(8,128)} %get-tuple-element.42), channel_id=1, source_target_pairs={{16,0},{32,16},{48,32},{64,48},{80,64},{96,80},{112,96},{17,1},{33... | collective-permute-start | bytes 294920 | tf_op jit(solution)/shard_map/ppermute | solution.py:416
  59.1 13.1 %collective-permute-start.1 = (f32[192,128]{1,0:T(8,128)}, f32[192,128]{1,0:T(8,128)S(1)}, u32[]{:S(2)}, u32[]{:S(2)}) collective-permute-start(f32[192,128]{1,0:T(8,128)} %get-tuple-element.43), channel_id=1, source_target_pairs={{0,16},{16,32},{32,48},{48,64},{64,80},{80,96},{96,112},{1,17},{17... | collective-permute-start | bytes 294920 | tf_op jit(solution)/shard_map/ppermute | solution.py:417
  62.4 11.1 %collective-permute-start.2 = (f32[192,128]{1,0:T(8,128)}, f32[192,128]{1,0:T(8,128)S(1)}, u32[]{:S(2)}, u32[]{:S(2)}) collective-permute-start(f32[192,128]{1,0:T(8,128)} %get-tuple-element.44), channel_id=1, source_target_pairs={{1,0},{2,1},{3,2},{4,3},{5,4},{6,5},{7,6},{8,7},{9,8},{10,9},{11,1... | collective-permute-start | bytes 294920 | tf_op jit(solution)/shard_map/ppermute | solution.py:418
  66.5 9.5 %collective-permute-start.3 = (f32[192,128]{1,0:T(8,128)}, f32[192,128]{1,0:T(8,128)S(1)}, u32[]{:S(2)}, u32[]{:S(2)}) collective-permute-start(f32[192,128]{1,0:T(8,128)} %get-tuple-element.45), channel_id=1, source_target_pairs={{0,1},{1,2},{2,3},{3,4},{4,5},{5,6},{6,7},{7,8},{8,9},{9,10},{10,1... | collective-permute-start | bytes 294920 | tf_op jit(solution)/shard_map/ppermute | solution.py:419
  72.1 3.8 %copy-start.2 = (f32[192,128]{1,0:T(8,128)}, f32[192,128]{1,0:T(8,128)S(1)}, u32[]{:S(2)}) copy-start(f32[192,128]{1,0:T(8,128)S(1)} %collective-permute-done.hn_ref) | copy-start | bytes 294916
  72.2 3.8 %copy-start.3 = (f32[192,128]{1,0:T(8,128)}, f32[192,128]{1,0:T(8,128)S(1)}, u32[]{:S(2)}) copy-start(f32[192,128]{1,0:T(8,128)S(1)} %collective-permute-done.1.hs_ref) | copy-start | bytes 294916
  73.4 2.5 %copy-start.4 = (f32[192,128]{1,0:T(8,128)}, f32[192,128]{1,0:T(8,128)S(1)}, u32[]{:S(2)}) copy-start(f32[192,128]{1,0:T(8,128)S(1)} %collective-permute-done.2.hw_ref) | copy-start | bytes 294916
  76.0 0.6 copy-start.5
  98.3 1.1 copy-start
  116.6 28.0 %copy-start.14 = (f32[192,128]{1,0:T(8,128)S(1)}, f32[192,128]{1,0:T(8,128)}, u32[]{:S(2)}) copy-start(f32[192,128]{1,0:T(8,128)} %get-tuple-element.50) | copy-start | bytes 294916
  116.6 30.3 %copy-start.13 = (f32[192,128]{1,0:T(8,128)S(1)}, f32[192,128]{1,0:T(8,128)}, u32[]{:S(2)}) copy-start(f32[192,128]{1,0:T(8,128)} %get-tuple-element.51) | copy-start | bytes 294916
  116.6 33.6 %copy-start.12 = (f32[192,128]{1,0:T(8,128)S(1)}, f32[192,128]{1,0:T(8,128)}, u32[]{:S(2)}) copy-start(f32[192,128]{1,0:T(8,128)} %get-tuple-element.52) | copy-start | bytes 294916
  116.6 37.7 %copy-start.11 = (f32[192,128]{1,0:T(8,128)S(1)}, f32[192,128]{1,0:T(8,128)}, u32[]{:S(2)}) copy-start(f32[192,128]{1,0:T(8,128)} %get-tuple-element.53) | copy-start | bytes 294916
  138.7 30.0 %all-to-all-start.3 = ((f32[128,8,128]{2,1,0:T(8,128)}), f32[128,8,128]{2,1,0:T(8,128)S(1)}, u32[]{:S(2)}, u32[]{:S(2)}) async-start(f32[128,8,128]{2,1,0:T(8,128)} %bitcast.20), calls=%async_computation.3 | async-start | bytes 1048576 | tf_op jit(solution)/shard_map/all_to_all | solution.py:399
  144.6 11.6 %collective-permute-start.4 = (f32[192,128]{1,0:T(8,128)S(1)}, f32[192,128]{1,0:T(8,128)S(1)}, u32[]{:S(2)}, u32[]{:S(2)}) collective-permute-start(f32[192,128]{1,0:T(8,128)S(1)} %copy-done.14), channel_id=1, source_target_pairs={{16,0},{32,16},{48,32},{64,48},{80,64},{96,80},{112,96},{17,1},{33... | collective-permute-start | bytes 294920 | tf_op jit(solution)/shard_map/ppermute | solution.py:416
  146.9 9.4 %collective-permute-start.5 = (f32[192,128]{1,0:T(8,128)S(1)}, f32[192,128]{1,0:T(8,128)S(1)}, u32[]{:S(2)}, u32[]{:S(2)}) collective-permute-start(f32[192,128]{1,0:T(8,128)S(1)} %copy-done.13), channel_id=1, source_target_pairs={{0,16},{16,32},{32,48},{48,64},{64,80},{80,96},{96,112},{1,17},{17... | collective-permute-start | bytes 294920 | tf_op jit(solution)/shard_map/ppermute | solution.py:417
  150.2 6.3 %collective-permute-start.6 = (f32[192,128]{1,0:T(8,128)S(1)}, f32[192,128]{1,0:T(8,128)S(1)}, u32[]{:S(2)}, u32[]{:S(2)}) collective-permute-start(f32[192,128]{1,0:T(8,128)S(1)} %copy-done.12), channel_id=1, source_target_pairs={{1,0},{2,1},{3,2},{4,3},{5,4},{6,5},{7,6},{8,7},{9,8},{10,9},{11,1... | collective-permute-start | bytes 294920 | tf_op jit(solution)/shard_map/ppermute | solution.py:418
  154.3 8.5 %collective-permute-start.7 = (f32[192,128]{1,0:T(8,128)S(1)}, f32[192,128]{1,0:T(8,128)S(1)}, u32[]{:S(2)}, u32[]{:S(2)}) collective-permute-start(f32[192,128]{1,0:T(8,128)S(1)} %copy-done.11), channel_id=1, source_target_pairs={{0,1},{1,2},{2,3},{3,4},{4,5},{5,6},{6,7},{7,8},{8,9},{9,10},{10,1... | collective-permute-start | bytes 294920 | tf_op jit(solution)/shard_map/ppermute | solution.py:419
  156.2 6.6 %copy-start.6 = (f32[192,128]{1,0:T(8,128)}, f32[192,128]{1,0:T(8,128)S(1)}, u32[]{:S(2)}) copy-start(f32[192,128]{1,0:T(8,128)S(1)} %collective-permute-done.4.hn_ref) | copy-start | bytes 294916
  156.2 6.6 %copy-start.7 = (f32[192,128]{1,0:T(8,128)}, f32[192,128]{1,0:T(8,128)S(1)}, u32[]{:S(2)}) copy-start(f32[192,128]{1,0:T(8,128)S(1)} %collective-permute-done.5.hs_ref) | copy-start | bytes 294916
  156.5 6.4 %copy-start.8 = (f32[192,128]{1,0:T(8,128)}, f32[192,128]{1,0:T(8,128)S(1)}, u32[]{:S(2)}) copy-start(f32[192,128]{1,0:T(8,128)S(1)} %collective-permute-done.6.hw_ref) | copy-start | bytes 294916
  162.8 0.6 copy-start.9
  168.8 0.8 copy-start.1

commit v2 on v1

--- a/solution.py
+++ b/solution.py
@@ -19,7 +19,8 @@
 CY = 128
 DEV = 128
 STORE = 4096
-PLANES = 4
+PLANES = 16
+UNROLL = 8
 COLS = PLANES * CY
 
 BF = jnp.bfloat16
@@ -45,44 +46,54 @@
     return lax.dot_general(left, right, NT, preferred_element_type=F32)
 
 
-def pack_kernel(counts_ref, stored_ref, late_ref, early_ref, padded):
-    padded[...] = jnp.zeros_like(padded)
-    for block in range(2 * TRACERS):
-        padded[block * PAD : block * PAD + NZ, :] = stored_ref[block * NZ : (block + 1) * NZ, :]
+def pack_kernel(moment, counts_ref, stored_ref, out_ref, near, padded, sem):
+    top = moment * TRACERS * NZ // 8 * 8
+    copy = pltpu.make_async_copy(stored_ref.at[top : top + near.shape[0], :], near, sem)
+    copy.start()
     lane = lax.broadcasted_iota(jnp.int32, (SLOT, 256), 1)
     offset = lane - lax.broadcasted_iota(jnp.int32, (SLOT, 256), 0)
+    for t in range(TRACERS):
+        padded[t * PAD + NZ : (t + 1) * PAD, :] = jnp.zeros((PAD - NZ, STORE), BF)
+    copy.wait()
+    skip = moment * TRACERS * NZ - top
+    for t in range(TRACERS):
+        padded[t * PAD : t * PAD + NZ, :] = near[skip + t * NZ : skip + (t + 1) * NZ, :]
 
     def group(g, start):
         base = pl.multiple_of(jnp.minimum((start // 128) * 128, STORE - 256), 128)
         hots = []
         for i in range(4):
-            hots.append(jnp.where(offset == start - base, 1.0, 0.0))
+            hots.append(jnp.where(offset == start - base, 1.0, 0.0).astype(BF))
             start = start + counts_ref[0, 4 * g + i]
-        hot = jnp.concatenate(hots, axis=0).astype(BF)
-        low = jnp.concatenate([h[:HALF] for h in hots], axis=0).astype(BF)
-        high = jnp.concatenate([h[HALF:] for h in hots], axis=0).astype(BF)
-        for out_ref, first in ((late_ref, FEATS), (early_ref, 0)):
-            main = dot_nt(hot, padded[first : first + 2 * PAD, pl.ds(base, 256)]).astype(BF)
-            last = padded[first + 2 * PAD : first + FEATS, pl.ds(base, 256)]
-            rest = jnp.concatenate([dot_nt(low, last), dot_nt(high, last)], axis=1).astype(BF)
-            for i in range(4):
-                out_ref[4 * g + i, :SLOT, :] = main[i * SLOT : (i + 1) * SLOT]
-                out_ref[4 * g + i, SLOT:, :] = rest[i * HALF : (i + 1) * HALF]
+        rows = dot_nt(jnp.concatenate(hots, axis=0), padded[:, pl.ds(base, 256)])
+        for i in range(4):
+            mine = rows[i * SLOT : (i + 1) * SLOT]
+            rest = jnp.concatenate([mine[:HALF, 2 * PAD :], mine[HALF:, 2 * PAD :]], axis=1)
+            out_ref[4 * g + i, :SLOT, :] = mine[:, : 2 * PAD].astype(BF)
+            out_ref[4 * g + i, SLOT:, :] = rest.astype(BF)
         return start
 
-    lax.fori_loop(0, DEV // 4, group, jnp.int32(0))
-
-
-def pack(counts, stored_t):
-    out = jax.ShapeDtypeStruct((DEV, SLOT + HALF, 128), BF)
-    return pl.pallas_call(
-        pack_kernel,
-        out_shape=(out, out),
-        in_specs=[pl.BlockSpec(memory_space=pltpu.SMEM), pl.BlockSpec(memory_space=pltpu.VMEM)],
-        out_specs=(pl.BlockSpec(memory_space=pltpu.VMEM),) * 2,
-        scratch_shapes=[pltpu.VMEM((2 * FEATS, STORE), BF)],
-        compiler_params=PARAMS,
-        name="pack",
+    def groups(j, start):
+        for u in range(UNROLL):
+            start = group(j * UNROLL + u, start)
+        return start
+
+    lax.fori_loop(0, DEV // 4 // UNROLL, groups, jnp.int32(0))
+
+
+def pack(moment, counts, stored_t):
+    return pl.pallas_call(
+        functools.partial(pack_kernel, moment),
+        out_shape=jax.ShapeDtypeStruct((DEV, SLOT + HALF, 128), BF),
+        in_specs=[pl.BlockSpec(memory_space=pltpu.SMEM), pl.BlockSpec(memory_space=pl.ANY)],
+        out_specs=pl.BlockSpec(memory_space=pltpu.VMEM),
+        scratch_shapes=[
+            pltpu.VMEM((TRACERS * NZ + 4, STORE), BF),
+            pltpu.VMEM((FEATS, STORE), BF),
+            pltpu.SemaphoreType.DMA,
+        ],
+        compiler_params=PARAMS,
+        name=f"pack{moment}",
     )(counts, stored_t)
 
 
@@ -435,15 +446,19 @@
     weight_out,
     bias_out,
 ):
-    late, early = pack(counts, stored[0].T)
+    stored_t = stored[0].T
+    late = pack(1, counts, stored_t)
+    stored_t, costate, weight_mid, late = lax.optimization_barrier((stored_t, costate, weight_mid, late))
     late = lax.all_to_all(late, ("gx", "gy"), split_axis=0, concat_axis=0, tiled=True)
-    early = lax.all_to_all(early, ("gx", "gy"), split_axis=0, concat_axis=0, tiled=True)
+    early = pack(0, counts, stored_t)
     split_weights = weights(weight_in, bias_in[None, :], weight_mid, weight_out.T)
     b2 = bias_mid[:, None]
     b3 = jnp.pad(bias_out, (0, PAD - NZ))[:, None]
     planes, *sides = edges(costate.reshape(TRACERS * NZ * CX, CY), land_mask, flow_x, flow_y)
     halos = exchange(*sides)
     base = first_stencil(planes, land_mask, flow_x, flow_y, halos)
+    early, base, split_weights = lax.optimization_barrier((early, base, split_weights))
+    early = lax.all_to_all(early, ("gx", "gy"), split_axis=0, concat_axis=0, tiled=True)
     lam, grads, *sides = closure(
         True, owners, land_mask, late, planes, split_weights, b2, b3, flow_x, flow_y, base
     )

time: 172 us -> 149 us (0.87)
  blocking collectives: 54.4 us -> 18.9 us
  starting transfers between devices: 34.5 us -> 50.3 us
  Pallas kernels: 66.5 us -> 57.1 us
  waiting for transfers between devices: 10.4 us -> 14.7 us
    all_to_all x1 -> x0, blocking collectives: 34.3 us -> none  [on_device(): lax.all_to_all(late, ('gx', 'gy'), split_axis=0, concat_axis=0, tiled=True)]
    all_to_all x0 -> x1, starting transfers between devices: none -> 10.5 us  [on_device(): lax.all_to_all(late, ('gx', 'gy'), split_axis=0, concat_axis=0, tiled=True)]
    all_to_all x1, waiting for transfers between devices: 0.01 us -> 8.1 us  [on_device(): lax.all_to_all(early, ('gx', 'gy'), split_axis=0, concat_axis=0, tiled=True)]
    pallas_call x2, Pallas kernels: 34.5 us -> 27.3 us  [closure(): pl.pallas_call(functools.partial(closure_kernel, first), grid=(CX // PLAN...]
    all_to_all x1, starting transfers between devices: 5.57 us -> 10.7 us  [on_device(): lax.all_to_all(early, ('gx', 'gy'), split_axis=0, concat_axis=0, tiled=True)]
    ppermute x2, waiting for transfers between devices: 8.88 us -> 6.4 us  [exchange(): lax.ppermute(east, 'gy', up_y)]
    pallas_call x1 -> x2, Pallas kernels: 12.7 us -> 10.5 us  [pack(): pl.pallas_call(functools.partial(pack_kernel, moment), out_shape=jax.Shap...]
    unnamed x32 -> x34, local copies, waits for them, and re-layouts: 3.21 us -> 4.38 us
  transfers between devices with their start and end apart: 10 -> 11, of which waited for: 4 -> 3; matrix products, arithmetic and copies ran while one was open for 1% -> 1% of each run, Pallas kernels for 19% -> 23%
where the time goes in v2:
time: 149 us; the launch traced here: 148 us
  Pallas kernels  57.1 us (38%)
  starting transfers between devices  50.3 us (34%)
  blocking collectives  18.9 us (13%)
  waiting for transfers between devices  14.7 us (10%)
  local copies, waits for them, and re-layouts  5.88 us (4%)
    pallas_call x2, Pallas kernels, closure(): pl.pallas_call(functools.partial(closure_kernel, first), grid=(CX // PLAN...  27.3 us
    all_to_all x1, blocking collectives, reduce_params(): lax.all_to_all(packed, ('gx', 'gy'), split_axis=0, concat_axis=0, tiled=T...  18.9 us
    all_to_all x1, starting transfers between devices, on_device(): lax.all_to_all(early, ('gx', 'gy'), split_axis=0, concat_axis=0, tiled=True)  10.7 us
    all_to_all x1, starting transfers between devices, on_device(): lax.all_to_all(late, ('gx', 'gy'), split_axis=0, concat_axis=0, tiled=True)  10.5 us
    pallas_call x2, Pallas kernels, pack(): pl.pallas_call(functools.partial(pack_kernel, moment), out_shape=jax.Shap...  10.5 us
    ppermute x2, starting transfers between devices, exchange(): lax.ppermute(west, 'gy', down_y)  8.26 us
    all_to_all x1, waiting for transfers between devices, on_device(): lax.all_to_all(early, ('gx', 'gy'), split_axis=0, concat_axis=0, tiled=True)  8.1 us
    ppermute x2, starting transfers between devices, exchange(): lax.ppermute(south, 'gx', up_x)  6.59 us
  transfers between devices with their start and end apart: 11, of which 3 were waited for; matrix products, arithmetic and copies ran while one was open for 1% of the time, Pallas kernels for 23%

profile of v2, /device:TPU:33, one launch (start us, length us, event | category | flops | bytes accessed | tf_op | source)
XLA Modules:
  0.0 147.8 jit_solution(13263348489292121931)
XLA Ops:
  0.6 5.3 %pack1.1 = bf16[128,48,128]{2,1,0:T(8,128)(2,1)} custom-call(s32[1,128]{1,0:T(1,128)} %counts_ref.3, bf16[360,4096]{1,0:T(8,128)(2,1)} %bitcast.18), custom_call_target="tpu_custom_call" | custom-call | tf_op jit(solution)/shard_map/pack1/pallas_call | solution.py:85
  5.9 10.5 %all-to-all-start = ((bf16[128,48,128]{2,1,0:T(8,128)(2,1)}), bf16[128,48,128]{2,1,0:T(8,128)(2,1)S(1)}, u32[]{:S(2)}, u32[]{:S(2)}) async-start(bf16[128,48,128]{2,1,0:T(8,128)(2,1)} %pack1.1), calls=%async_computation | async-start | bytes 3145728 | tf_op jit(solution)/shard_map/all_to_all | solution.py:452
  16.4 3.5 %edges.1 = (f32[16,192,128]{2,1,0:T(8,128)}, f32[192,128]{1,0:T(8,128)}, f32[192,128]{1,0:T(8,128)}, f32[192,128]{1,0:T(8,128)}, f32[192,128]{1,0:T(8,128)}) custom-call(f32[2880,128]{1,0:T(8,128)} %bitcast.23, s32[16,128]{1,0:T(8,128)} %mask_ref.5, f32[16,128]{1,0:T(8,128)} %fx_ref.5, f32[16,128]{1,0:T(8,128)} %fy_ref.5), custom_call_target="tpu_custom_call" | custom-call | tf_op jit(solution)/shard_map/edges/pallas_call | solution.py:176
  20.0 2.3 %collective-permute-start = (f32[192,128]{1,0:T(8,128)}, f32[192,128]{1,0:T(8,128)S(1)}, u32[]{:S(2)}, u32[]{:S(2)}) collective-permute-start(f32[192,128]{1,0:T(8,128)} %get-tuple-element.48), channel_id=1, source_target_pairs={{16,0},{32,16},{48,32},{64,48},{80,64},{96,80},{112,96},{17,1},{33... | collective-permute-start | bytes 294920 | tf_op jit(solution)/shard_map/ppermute | solution.py:427
  22.2 3.3 %collective-permute-start.1 = (f32[192,128]{1,0:T(8,128)}, f32[192,128]{1,0:T(8,128)S(1)}, u32[]{:S(2)}, u32[]{:S(2)}) collective-permute-start(f32[192,128]{1,0:T(8,128)} %get-tuple-element.49), channel_id=1, source_target_pairs={{0,16},{16,32},{32,48},{48,64},{64,80},{80,96},{96,112},{1,17},{17... | collective-permute-start | bytes 294920 | tf_op jit(solution)/shard_map/ppermute | solution.py:428
  25.5 4.2 %collective-permute-start.2 = (f32[192,128]{1,0:T(8,128)}, f32[192,128]{1,0:T(8,128)S(1)}, u32[]{:S(2)}, u32[]{:S(2)}) collective-permute-start(f32[192,128]{1,0:T(8,128)} %get-tuple-element.50), channel_id=1, source_target_pairs={{1,0},{2,1},{3,2},{4,3},{5,4},{6,5},{7,6},{8,7},{9,8},{10,9},{11,1... | collective-permute-start | bytes 294920 | tf_op jit(solution)/shard_map/ppermute | solution.py:429
  29.7 1.9 %collective-permute-start.3 = (f32[192,128]{1,0:T(8,128)}, f32[192,128]{1,0:T(8,128)S(1)}, u32[]{:S(2)}, u32[]{:S(2)}) collective-permute-start(f32[192,128]{1,0:T(8,128)} %get-tuple-element.51), channel_id=1, source_target_pairs={{0,1},{1,2},{2,3},{3,4},{4,5},{5,6},{6,7},{7,8},{8,9},{9,10},{10,1... | collective-permute-start | bytes 294920 | tf_op jit(solution)/shard_map/ppermute | solution.py:430
  31.7 5.2 %pack0.1 = bf16[128,48,128]{2,1,0:T(8,128)(2,1)} custom-call(s32[1,128]{1,0:T(1,128)} %counts_ref.3, bf16[360,4096]{1,0:T(8,128)(2,1)} %bitcast.19), custom_call_target="tpu_custom_call" | custom-call | tf_op jit(solution)/shard_map/pack0/pallas_call | solution.py:85
  36.9 2.2 %weights.1 = (bf16[512,192]{1,0:T(8,128)(2,1)}, bf16[512,256]{1,0:T(8,128)(2,1)}, bf16[128,256]{1,0:T(8,128)(2,1)}, bf16[256,192]{1,0:T(8,128)(2,1)}, bf16[512,2...) custom-call(f32[180,256]{1,0:T(8,128)} %w1_ref.1, f32[1,256]{1,0:T(1,128)} %bitcast.27, f32[256,256]{1,0:T(8,128)} %w2_ref, ...), custom_call_target="tpu_custom_call" | custom-call | tf_op jit(solution)/shard_map/weights/pallas_call | solution.py:132
  39.2 0.5 copy-done.3
  39.9 4.4 %stencil1.1.refs_14_ = f32[16,192,128]{2,1,0:T(8,128)} custom-call(f32[16,192,128]{2,1,0:T(8,128)} %get-tuple-element.46.lam_ref.refs_3_, s32[16,128]{1,0:T(8,128)} %mask_ref.5, f32[16,128]{1,0:T(8,128)} %fx_ref.5, f32[16,128]{1,0:T(8,128)} %fy_ref.5, f32[192,128]{1,0:T(8,128)} %copy-done.3, f32[192,128]{1,0:T(8,128)} %copy-done.4, f32[192,128]{1,0:T(8,128)} %copy-done.5, ...), custom_call_target="tpu_custom_call" | custom-call | tf_op jit(solution)/shard_map/stencil1/pallas_call | solution.py:215
  44.3 1.1 copy-done.1
  45.4 10.7 %all-to-all-start.1 = ((bf16[128,48,128]{2,1,0:T(8,128)(2,1)}), bf16[128,48,128]{2,1,0:T(8,128)(2,1)S(1)}, u32[]{:S(2)}, u32[]{:S(2)}) async-start(bf16[128,48,128]{2,1,0:T(8,128)(2,1)} %pack0.1), calls=%async_computation.1 | async-start | bytes 3145728 | tf_op jit(solution)/shard_map/all_to_all | solution.py:461
  56.2 0.7 copy.23.refs_11_
  56.9 0.8 copy.22.refs_10_
  57.7 13.8 %closure1.1 = (f32[16,192,128]{2,1,0:T(8,128)}, f32[512,256]{1,0:T(8,128)}, f32[192,128]{1,0:T(8,128)}, f32[192,128]{1,0:T(8,128)}, f32[192,128]{1,0:T(8,128)}, /*index=5*/f32[192,128]{1,0:T(8,128)}) custom-call(s32[16,128]{1,0:T(8,128)} %refs_0_.3, s32[16,128]{1,0:T(8,128)} %mask_ref.5, bf16[128,48,128]{2,1,0:T(8,128)(2,1)} %copy-done.1, ...), custom_call_target="tpu_custom_call" | custom-call | tf_op jit(solution)/shard_map/closure1/pallas_call | solution.py:372
  71.5 8.1 %all-to-all-done.1.refs_2_ = bf16[128,48,128]{2,1,0:T(8,128)(2,1)S(1)} async-done(((bf16[128,48,128]{2,1,0:T(8,128)(2,1)}), bf16[128,48,128]{2,1,0:T(8,128)(2,1)S(1)}, u32[]{:S(2)}, u32[]{:S(2)}) %all-to-all-start.1) | async-done | bytes 1572896 | tf_op jit(solution)/shard_map/all_to_all | solution.py:461
  79.6 1.1 copy-done
  80.7 13.4 %closure0.1 = (f32[16,192,128]{2,1,0:T(8,128)}, f32[1024,128]{1,0:T(8,128)}) custom-call(s32[16,128]{1,0:T(8,128)} %refs_0_.3, s32[16,128]{1,0:T(8,128)} %mask_ref.5, bf16[128,48,128]{2,1,0:T(8,128)(2,1)} %copy-done, f32[16,192,128]{2,1,0:T(8,128)} %get-tuple-element.66.refs_3_.lam_ref, bf16[512,192]{1,0:T(8,128)(2,1)} %get-tuple-element.59.refs_4_, ...), custom_call_target="tpu_custom_call" | custom-call | tf_op jit(solution)/shard_map/closure0/pallas_call | solution.py:372
  94.2 18.9 %all_to_all.32 = f32[128,8,128]{2,1,0:T(8,128)} all-to-all(f32[128,8,128]{2,1,0:T(8,128)} %bitcast.25), channel_id=1, replica_groups=mesh['gx'=8,'gy'=16] {'gx','gy'}, dimensions={0} | all-to-all | bytes 1048576 | tf_op jit(solution)/shard_map/all_to_all | solution.py:406
  113.1 2.0 %sum.1 = f32[1024,128]{1,0:T(8,128)} custom-call(f32[1024,128]{1,0:T(8,128)} %bitcast.22), custom_call_target="tpu_custom_call" | custom-call | tf_op jit(solution)/shard_map/sum/pallas_call | solution.py:407
  115.1 5.8 %all-to-all-start.3 = ((f32[128,8,128]{2,1,0:T(8,128)}), f32[128,8,128]{2,1,0:T(8,128)S(1)}, u32[]{:S(2)}, u32[]{:S(2)}) async-start(f32[128,8,128]{2,1,0:T(8,128)} %bitcast.21), calls=%async_computation.3 | async-start | bytes 1048576 | tf_op jit(solution)/shard_map/all_to_all | solution.py:410
  120.9 2.3 %collective-permute-start.4 = (f32[192,128]{1,0:T(8,128)S(1)}, f32[192,128]{1,0:T(8,128)S(1)}, u32[]{:S(2)}, u32[]{:S(2)}) collective-permute-start(f32[192,128]{1,0:T(8,128)S(1)} %copy-done.15), channel_id=1, source_target_pairs={{16,0},{32,16},{48,32},{64,48},{80,64},{96,80},{112,96},{17,1},{33... | collective-permute-start | bytes 294920 | tf_op jit(solution)/shard_map/ppermute | solution.py:427
  123.2 3.3 %collective-permute-start.5 = (f32[192,128]{1,0:T(8,128)S(1)}, f32[192,128]{1,0:T(8,128)S(1)}, u32[]{:S(2)}, u32[]{:S(2)}) collective-permute-start(f32[192,128]{1,0:T(8,128)S(1)} %copy-done.14), channel_id=1, source_target_pairs={{0,16},{16,32},{32,48},{48,64},{64,80},{80,96},{96,112},{1,17},{17... | collective-permute-start | bytes 294920 | tf_op jit(solution)/shard_map/ppermute | solution.py:428
  126.5 4.1 %collective-permute-start.6 = (f32[192,128]{1,0:T(8,128)S(1)}, f32[192,128]{1,0:T(8,128)S(1)}, u32[]{:S(2)}, u32[]{:S(2)}) collective-permute-start(f32[192,128]{1,0:T(8,128)S(1)} %copy-done.13), channel_id=1, source_target_pairs={{1,0},{2,1},{3,2},{4,3},{5,4},{6,5},{7,6},{8,7},{9,8},{10,9},{11,1... | collective-permute-start | bytes 294920 | tf_op jit(solution)/shard_map/ppermute | solution.py:429
  130.6 1.9 %collective-permute-start.7 = (f32[192,128]{1,0:T(8,128)S(1)}, f32[192,128]{1,0:T(8,128)S(1)}, u32[]{:S(2)}, u32[]{:S(2)}) collective-permute-start(f32[192,128]{1,0:T(8,128)S(1)} %copy-done.12), channel_id=1, source_target_pairs={{0,1},{1,2},{2,3},{3,4},{4,5},{5,6},{6,7},{7,8},{8,9},{9,10},{10,1... | collective-permute-start | bytes 294920 | tf_op jit(solution)/shard_map/ppermute | solution.py:430
  132.6 0.2 collective-permute-done.6.hw_ref
  132.8 6.3 %collective-permute-done.7.he_ref = f32[192,128]{1,0:T(8,128)S(1)} collective-permute-done((f32[192,128]{1,0:T(8,128)S(1)}, f32[192,128]{1,0:T(8,128)S(1)}, u32[]{:S(2)}, u32[]{:S(2)}) %collective-permute-start.7) | collective-permute-done | bytes 98336 | tf_op jit(solution)/shard_map/ppermute | solution.py:430
  139.2 0.6 copy-done.10
  139.8 5.3 %stencil0.1 = f32[2880,128]{1,0:T(8,128)} custom-call(f32[16,192,128]{2,1,0:T(8,128)} %get-tuple-element.66.refs_3_.lam_ref, f32[16,192,128]{2,1,0:T(8,128)} %get-tuple-element.69.down_ref, s32[16,128]{1,0:T(8,128)} %mask_ref.5, f32[16,128]{1,0:T(8,128)} %fx_ref.5, f32[16,128]{1,0:T(8,128)} %fy_ref.5, f32[192,128]{1,0:T(8,128)} %copy-done.7, ...), custom_call_target="tpu_custom_call" | custom-call | tf_op jit(solution)/shard_map/stencil0/pallas_call | solution.py:229
  145.1 0.8 copy-done.2
  145.9 1.9 %unpack.1 = (f32[180,256]{1,0:T(8,128)}, f32[1,256]{1,0:T(1,128)}, f32[256,256]{1,0:T(8,128)}, f32[1,256]{1,0:T(1,128)}, f32[60,256]{1,0:T(8,128)}, /*index=5*/f32[1,60]{1,0:T(1,128)}) custom-call(f32[1024,128]{1,0:T(8,128)} %bitcast.20), custom_call_target="tpu_custom_call" | custom-call | tf_op jit(solution)/shard_map/unpack/pallas_call | solution.py:412
  (38 shorter events, 0.2 us)
Async XLA Ops:
  5.9 38.4 %all-to-all-start = ((bf16[128,48,128]{2,1,0:T(8,128)(2,1)}), bf16[128,48,128]{2,1,0:T(8,128)(2,1)S(1)}, u32[]{:S(2)}, u32[]{:S(2)}) async-start(bf16[128,48,128]{2,1,0:T(8,128)(2,1)} %pack1.1), calls=%async_computation | async-start | bytes 3145728 | tf_op jit(solution)/shard_map/all_to_all | solution.py:452
  20.0 19.2 %collective-permute-start = (f32[192,128]{1,0:T(8,128)}, f32[192,128]{1,0:T(8,128)S(1)}, u32[]{:S(2)}, u32[]{:S(2)}) collective-permute-start(f32[192,128]{1,0:T(8,128)} %get-tuple-element.48), channel_id=1, source_target_pairs={{16,0},{32,16},{48,32},{64,48},{80,64},{96,80},{112,96},{17,1},{33... | collective-permute-start | bytes 294920 | tf_op jit(solution)/shard_map/ppermute | solution.py:427
  22.2 16.9 %collective-permute-start.1 = (f32[192,128]{1,0:T(8,128)}, f32[192,128]{1,0:T(8,128)S(1)}, u32[]{:S(2)}, u32[]{:S(2)}) collective-permute-start(f32[192,128]{1,0:T(8,128)} %get-tuple-element.49), channel_id=1, source_target_pairs={{0,16},{16,32},{32,48},{48,64},{64,80},{80,96},{96,112},{1,17},{17... | collective-permute-start | bytes 294920 | tf_op jit(solution)/shard_map/ppermute | solution.py:428
  25.5 13.6 %collective-permute-start.2 = (f32[192,128]{1,0:T(8,128)}, f32[192,128]{1,0:T(8,128)S(1)}, u32[]{:S(2)}, u32[]{:S(2)}) collective-permute-start(f32[192,128]{1,0:T(8,128)} %get-tuple-element.50), channel_id=1, source_target_pairs={{1,0},{2,1},{3,2},{4,3},{5,4},{6,5},{7,6},{8,7},{9,8},{10,9},{11,1... | collective-permute-start | bytes 294920 | tf_op jit(solution)/shard_map/ppermute | solution.py:429
  29.7 9.5 %collective-permute-start.3 = (f32[192,128]{1,0:T(8,128)}, f32[192,128]{1,0:T(8,128)S(1)}, u32[]{:S(2)}, u32[]{:S(2)}) collective-permute-start(f32[192,128]{1,0:T(8,128)} %get-tuple-element.51), channel_id=1, source_target_pairs={{0,1},{1,2},{2,3},{3,4},{4,5},{5,6},{6,7},{7,8},{8,9},{9,10},{10,1... | collective-permute-start | bytes 294920 | tf_op jit(solution)/shard_map/ppermute | solution.py:430
  39.1 0.6 copy-start.3
  39.2 0.7 copy-start.4
  39.2 0.7 copy-start.5
  39.2 0.6 copy-start.6
  44.3 11.9 %copy-start.16 = (f32[60]{0:T(128)S(1)}, f32[60]{0:T(128)}, u32[]{:S(2)}) copy-start(f32[60]{0:T(128)} %param.25) | copy-start | bytes 724
  44.3 12.6 %copy-start.11 = (f32[256]{0:T(256)S(1)}, f32[256]{0:T(256)}, u32[]{:S(2)}) copy-start(f32[256]{0:T(256)} %param.23) | copy-start | bytes 3076
  44.3 1.2 copy-start.1
  45.4 34.2 %all-to-all-start.1 = ((bf16[128,48,128]{2,1,0:T(8,128)(2,1)}), bf16[128,48,128]{2,1,0:T(8,128)(2,1)S(1)}, u32[]{:S(2)}, u32[]{:S(2)}) async-start(bf16[128,48,128]{2,1,0:T(8,128)(2,1)} %pack0.1), calls=%async_computation.1 | async-start | bytes 3145728 | tf_op jit(solution)/shard_map/all_to_all | solution.py:461
  79.6 1.1 copy-start
  94.2 26.7 %copy-start.15 = (f32[192,128]{1,0:T(8,128)S(1)}, f32[192,128]{1,0:T(8,128)}, u32[]{:S(2)}) copy-start(f32[192,128]{1,0:T(8,128)} %get-tuple-element.70) | copy-start | bytes 294916
  94.2 29.0 %copy-start.14 = (f32[192,128]{1,0:T(8,128)S(1)}, f32[192,128]{1,0:T(8,128)}, u32[]{:S(2)}) copy-start(f32[192,128]{1,0:T(8,128)} %get-tuple-element.71) | copy-start | bytes 294916
  94.2 32.3 %copy-start.13 = (f32[192,128]{1,0:T(8,128)S(1)}, f32[192,128]{1,0:T(8,128)}, u32[]{:S(2)}) copy-start(f32[192,128]{1,0:T(8,128)} %get-tuple-element.72) | copy-start | bytes 294916
  94.2 36.4 %copy-start.12 = (f32[192,128]{1,0:T(8,128)S(1)}, f32[192,128]{1,0:T(8,128)}, u32[]{:S(2)}) copy-start(f32[192,128]{1,0:T(8,128)} %get-tuple-element.73) | copy-start | bytes 294916
  115.1 30.0 %all-to-all-start.3 = ((f32[128,8,128]{2,1,0:T(8,128)}), f32[128,8,128]{2,1,0:T(8,128)S(1)}, u32[]{:S(2)}, u32[]{:S(2)}) async-start(f32[128,8,128]{2,1,0:T(8,128)} %bitcast.21), calls=%async_computation.3 | async-start | bytes 1048576 | tf_op jit(solution)/shard_map/all_to_all | solution.py:410
  120.9 11.6 %collective-permute-start.4 = (f32[192,128]{1,0:T(8,128)S(1)}, f32[192,128]{1,0:T(8,128)S(1)}, u32[]{:S(2)}, u32[]{:S(2)}) collective-permute-start(f32[192,128]{1,0:T(8,128)S(1)} %copy-done.15), channel_id=1, source_target_pairs={{16,0},{32,16},{48,32},{64,48},{80,64},{96,80},{112,96},{17,1},{33... | collective-permute-start | bytes 294920 | tf_op jit(solution)/shard_map/ppermute | solution.py:427
  123.2 9.4 %collective-permute-start.5 = (f32[192,128]{1,0:T(8,128)S(1)}, f32[192,128]{1,0:T(8,128)S(1)}, u32[]{:S(2)}, u32[]{:S(2)}) collective-permute-start(f32[192,128]{1,0:T(8,128)S(1)} %copy-done.14), channel_id=1, source_target_pairs={{0,16},{16,32},{32,48},{48,64},{64,80},{80,96},{96,112},{1,17},{17... | collective-permute-start | bytes 294920 | tf_op jit(solution)/shard_map/ppermute | solution.py:428
  126.5 6.3 %collective-permute-start.6 = (f32[192,128]{1,0:T(8,128)S(1)}, f32[192,128]{1,0:T(8,128)S(1)}, u32[]{:S(2)}, u32[]{:S(2)}) collective-permute-start(f32[192,128]{1,0:T(8,128)S(1)} %copy-done.13), channel_id=1, source_target_pairs={{1,0},{2,1},{3,2},{4,3},{5,4},{6,5},{7,6},{8,7},{9,8},{10,9},{11,1... | collective-permute-start | bytes 294920 | tf_op jit(solution)/shard_map/ppermute | solution.py:429
  130.6 8.5 %collective-permute-start.7 = (f32[192,128]{1,0:T(8,128)S(1)}, f32[192,128]{1,0:T(8,128)S(1)}, u32[]{:S(2)}, u32[]{:S(2)}) collective-permute-start(f32[192,128]{1,0:T(8,128)S(1)} %copy-done.12), channel_id=1, source_target_pairs={{0,1},{1,2},{2,3},{3,4},{4,5},{5,6},{6,7},{7,8},{8,9},{9,10},{10,1... | collective-permute-start | bytes 294920 | tf_op jit(solution)/shard_map/ppermute | solution.py:430
  132.6 6.6 %copy-start.7 = (f32[192,128]{1,0:T(8,128)}, f32[192,128]{1,0:T(8,128)S(1)}, u32[]{:S(2)}) copy-start(f32[192,128]{1,0:T(8,128)S(1)} %collective-permute-done.4.hn_ref) | copy-start | bytes 294916
  132.6 6.6 %copy-start.8 = (f32[192,128]{1,0:T(8,128)}, f32[192,128]{1,0:T(8,128)S(1)}, u32[]{:S(2)}) copy-start(f32[192,128]{1,0:T(8,128)S(1)} %collective-permute-done.5.hs_ref) | copy-start | bytes 294916
  132.8 6.4 %copy-start.9 = (f32[192,128]{1,0:T(8,128)}, f32[192,128]{1,0:T(8,128)S(1)}, u32[]{:S(2)}) copy-start(f32[192,128]{1,0:T(8,128)S(1)} %collective-permute-done.6.hw_ref) | copy-start | bytes 294916
  139.2 0.6 copy-start.10
  145.1 0.8 copy-start.2

commit v3 on v2

--- a/solution.py
+++ b/solution.py
@@ -19,14 +19,14 @@
 CY = 128
 DEV = 128
 STORE = 4096
-PLANES = 16
 UNROLL = 8
-COLS = PLANES * CY
+COLS = CX * CY
+
+CLOSURE_MIB = 24
 
 BF = jnp.bfloat16
 F32 = jnp.float32
 NT = (((1,), (1,)), ((), ()))
-PARAMS = pltpu.CompilerParams(vmem_limit_bytes=56 * 2**20)
 
 step_size = 0.25
 flat_mix = 0.25
@@ -44,6 +44,26 @@
 
 def dot_nt(left, right):
     return lax.dot_general(left, right, NT, preferred_element_type=F32)
+
+
+def params(mib):
+    return pltpu.CompilerParams(vmem_limit_bytes=mib * 2**20)
+
+
+def near_shape(*shape, dtype=F32):
+    return pltpu.VMEM(shape, dtype)
+
+
+def call(kernel, name, out_shape, args, scratch=(), mib=4):
+    args = [pltpu.with_memory_space_constraint(a, pltpu.VMEM) for a in args]
+    return pl.pallas_call(
+        kernel,
+        out_shape=out_shape,
+        in_specs=[pl.BlockSpec(memory_space=pltpu.VMEM)] * len(args),
+        scratch_shapes=list(scratch),
+        compiler_params=params(mib),
+        name=name,
+    )(*args)
 
 
 def pack_kernel(moment, counts_ref, stored_ref, out_ref, near, padded, sem):
@@ -84,7 +104,7 @@
 def pack(moment, counts, stored_t):
     return pl.pallas_call(
         functools.partial(pack_kernel, moment),
-        out_shape=jax.ShapeDtypeStruct((DEV, SLOT + HALF, 128), BF),
+        out_shape=pltpu.HBM((DEV, SLOT + HALF, 128), BF),
         in_specs=[pl.BlockSpec(memory_space=pltpu.SMEM), pl.BlockSpec(memory_space=pl.ANY)],
         out_specs=pl.BlockSpec(memory_space=pltpu.VMEM),
         scratch_shapes=[
@@ -92,12 +112,13 @@
             pltpu.VMEM((FEATS, STORE), BF),
             pltpu.SemaphoreType.DMA,
         ],
-        compiler_params=PARAMS,
+        compiler_params=params(8),
         name=f"pack{moment}",
-    )(counts, stored_t)
-
-
-def weights_kernel(w1_ref, b1_ref, w2_ref, w3t_ref, f1_ref, f2_ref, f3_ref, r3_ref, r2_ref, r1_ref, wide, tall):
+    )(*(pltpu.with_memory_space_constraint(a, pltpu.HBM) for a in (counts, stored_t)))
+
+
+def weights_kernel(w1_ref, b1_ref, w2_ref, b2_ref, w3t_ref, b3_ref, *refs):
+    f1_ref, f2_ref, f3_ref, r3_ref, r2_ref, r1_ref, c2_ref, c3_ref, wide, tall = refs
     wide[...] = jnp.zeros_like(wide)
     for t in range(TRACERS):
         wide[t * PAD : t * PAD + NZ, :] = w1_ref[t * NZ : (t + 1) * NZ, :]
@@ -125,20 +146,19 @@
     lane = lax.broadcasted_iota(jnp.int32, high.shape, 1)
     middle = (lane >= PAD) & (lane < 2 * PAD)
     r3_ref[...] = jnp.where(middle, low.astype(F32), high.astype(F32)).astype(BF)
-
-
-def weights(w1, b1, w2, w3t):
+    c2_ref[...] = jnp.broadcast_to(b2_ref[...], (8, HID)).T[:, :1]
+    c3_ref[...] = jnp.zeros_like(c3_ref)
+    c3_ref[:NZ, :] = jnp.broadcast_to(b3_ref[...], (8, NZ)).T[:, :1]
+
+
+def weights(*args):
     shapes = ((2 * HID, FEATS), (2 * HID, HID), (2 * PAD, HID), (HID, FEATS), (2 * HID, HID), (2 * FEATS, HID))
-    return pl.pallas_call(
-        weights_kernel,
-        out_shape=tuple(jax.ShapeDtypeStruct(s, BF) for s in shapes),
-        scratch_shapes=[pltpu.VMEM((FEATS, HID), F32), pltpu.VMEM((FEATS, HID), F32)],
-        compiler_params=PARAMS,
-        name="weights",
-    )(w1, b1, w2, w3t)
-
-
-def edge_plane(x, plane, mask_row, fx_row, fy_row, ew_ref, ee_ref):
+    outs = tuple(near_shape(*shape, dtype=BF) for shape in shapes) + (near_shape(HID, 1), near_shape(PAD, 1))
+    scratch = [pltpu.VMEM((FEATS, HID), F32), pltpu.VMEM((FEATS, HID), F32)]
+    return call(weights_kernel, "weights", outs, args, scratch)
+
+
+def edge_plane(x, plane, mask_row, fy_row, ew_ref, ee_ref):
     weighted = plane * mask_row
     lane = lax.broadcasted_iota(jnp.int32, plane.shape, 1)
     west = pltpu.roll(weighted * (flat_mix + 0.5 * fy_row), x, 1)
@@ -163,22 +183,17 @@
         for t in range(TRACERS):
             planes_ref[x, t * PAD : t * PAD + NZ, :] = raw_ref[pl.ds(t * NZ * CX + x, NZ, stride=CX), :]
         mask_row = mask_ref[x : x + 1, :].astype(F32)
-        edge_plane(x, planes_ref[x], mask_row, None, fy_ref[x : x + 1, :], ew_ref, ee_ref)
+        edge_plane(x, planes_ref[x], mask_row, fy_ref[x : x + 1, :], ew_ref, ee_ref)
     en_ref[...] = north_edge(planes_ref[0], mask_ref[0:1, :].astype(F32), fx_ref[0:1, :])
     es_ref[...] = south_edge(planes_ref[CX - 1], mask_ref[CX - 1 :, :].astype(F32), fx_ref[CX - 1 :, :])
 
 
-EDGE = jax.ShapeDtypeStruct((FEATS, CY), F32)
-PLANE = jax.ShapeDtypeStruct((CX, FEATS, CY), F32)
-
-
-def edges(raw, mask, fx, fy):
-    return pl.pallas_call(
-        edges_kernel,
-        out_shape=(PLANE, EDGE, EDGE, EDGE, EDGE),
-        compiler_params=PARAMS,
-        name="edges",
-    )(raw, mask, fx, fy)
+EDGE = near_shape(FEATS, CY)
+PLANE = near_shape(CX, FEATS, CY)
+
+
+def edges(*args):
+    return call(edges_kernel, "edges", (PLANE, EDGE, EDGE, EDGE, EDGE), args)
 
 
 def stencil_plane(x, lam_ref, mask_ref, fx_ref, fy_ref, hn_ref, hs_ref, hw_ref, he_ref):
@@ -212,9 +227,7 @@
 
 
 def first_stencil(lam, mask, fx, fy, halos):
-    return pl.pallas_call(first_kernel, out_shape=PLANE, compiler_params=PARAMS, name="stencil1")(
-        lam, mask, fx, fy, *halos
-    )
+    return call(first_kernel, "stencil1", PLANE, (lam, mask, fx, fy, *halos))
 
 
 def last_kernel(lam_ref, down_ref, mask_ref, fx_ref, fy_ref, hn_ref, hs_ref, hw_ref, he_ref, out_ref):
@@ -226,12 +239,8 @@
 
 
 def last_stencil(lam, down, mask, fx, fy, halos):
-    return pl.pallas_call(
-        last_kernel,
-        out_shape=jax.ShapeDtypeStruct((TRACERS * NZ * CX, CY), F32),
-        compiler_params=PARAMS,
-        name="stencil0",
-    )(lam, down, mask, fx, fy, *halos)
+    out = jax.ShapeDtypeStruct((TRACERS * NZ * CX, CY), F32)
+    return call(last_kernel, "stencil0", out, (lam, down, mask, fx, fy, *halos))
 
 
 def closure_kernel(first, *refs):
@@ -244,32 +253,26 @@
         before_ref, out_ref, grads_ref = refs[:3]
         refs = refs[3:]
     rows_ref, total = refs
-    block = pl.program_id(0)
-
-    @pl.when(block == 0)
-    def _():
-        for half in range(2):
-            for g in range(DEV // 8):
-                at = half * (STORE // 2) + g * 128
-                main = [got_ref[8 * g + i, half * HALF : (half + 1) * HALF, :] for i in range(8)]
-                rows_ref[: 2 * PAD, at : at + 128] = jnp.concatenate(main, axis=0).T
+    for half in range(2):
         for g in range(DEV // 8):
-            rest = [got_ref[8 * g + i, SLOT:, :] for i in range(8)]
-            both = jnp.concatenate(rest, axis=0).T
-            rows_ref[2 * PAD :, g * 128 : (g + 1) * 128] = both[:PAD]
-            at = STORE // 2 + g * 128
-            rows_ref[2 * PAD :, at : at + 128] = both[PAD:]
-        if first:
-            total[...] = jnp.zeros_like(total)
-            ew_ref[...] = jnp.zeros_like(ew_ref)
-            ee_ref[...] = jnp.zeros_like(ee_ref)
-        else:
-            total[...] = before_ref[...]
-
-    x0 = block * PLANES
+            at = half * (STORE // 2) + g * 128
+            main = [got_ref[8 * g + i, half * HALF : (half + 1) * HALF, :] for i in range(8)]
+            rows_ref[: 2 * PAD, at : at + 128] = jnp.concatenate(main, axis=0).T
+    for g in range(DEV // 8):
+        rest = [got_ref[8 * g + i, SLOT:, :] for i in range(8)]
+        both = jnp.concatenate(rest, axis=0).T
+        rows_ref[2 * PAD :, g * 128 : (g + 1) * 128] = both[:PAD]
+        at = STORE // 2 + g * 128
+        rows_ref[2 * PAD :, at : at + 128] = both[PAD:]
+    if first:
+        total[...] = jnp.zeros_like(total)
+        ew_ref[...] = jnp.zeros_like(ew_ref)
+        ee_ref[...] = jnp.zeros_like(ee_ref)
+    else:
+        total[...] = before_ref[...]
 
     def wide(ref):
-        return jnp.concatenate([ref[pl.ds(x0 + i, 1), :] for i in range(PLANES)], axis=1)
+        return jnp.concatenate([ref[i : i + 1, :] for i in range(CX)], axis=1)
 
     owner = wide(owner_ref)
     at = ((owner >> 4) & 1) * (STORE // 2) + (owner >> 5) * HALF + (owner & (HALF - 1))
@@ -298,7 +301,7 @@
     direct = []
     for t in range(TRACERS):
         lo, hi = t * PAD, (t + 1) * PAD
-        mu = jnp.concatenate([lam_ref[i, lo:hi, :] for i in range(PLANES)], axis=1) * mask_row
+        mu = jnp.concatenate([lam_ref[i, lo:hi, :] for i in range(CX)], axis=1) * mask_row
         gap = mu - pltpu.roll(mu, PAD - 1, 0)
         column = picked[lo:hi]
         slope = slope + gap * (pltpu.roll(column, PAD - 1, 0) - column)
@@ -326,7 +329,7 @@
     both = dot_nt(ones, d3_both)
     total[NZ + 2 : NZ + 3, :PAD] += both[:1, :PAD] + both[:1, PAD:]
 
-    for i in range(PLANES):
+    for i in range(CX):
         part = slice(i * CY, (i + 1) * CY)
         for t in range(TRACERS):
             lo, hi = t * PAD, (t + 1) * PAD
@@ -336,49 +339,29 @@
             else:
                 out_ref[i, lo:hi, :] = down
         if first:
-            x = x0 + i
-            edge_plane(
-                x, out_ref[i], mask_ref[pl.ds(x, 1), :].astype(F32), None, fy_ref[pl.ds(x, 1), :], ew_ref, ee_ref
-            )
-
+            edge_plane(i, out_ref[i], mask_ref[i : i + 1, :].astype(F32), fy_ref[i : i + 1, :], ew_ref, ee_ref)
     if first:
-
-        @pl.when(block == 0)
-        def _():
-            en_ref[...] = north_edge(out_ref[0], mask_ref[0:1, :].astype(F32), fx_ref[0:1, :])
-
-    @pl.when(block == CX // PLANES - 1)
-    def _():
-        if first:
-            es_ref[...] = south_edge(out_ref[PLANES - 1], mask_ref[CX - 1 :, :].astype(F32), fx_ref[CX - 1 :, :])
-            grads_ref[...] = total[...]
-        else:
-            grads_ref[: 2 * HID, :] = total[:, :128]
-            grads_ref[2 * HID :, :] = total[:, 128:]
-
-
-def closure(first, owners, mask, got, lam, split_weights, b2, b3, *extra):
-    whole = pl.BlockSpec(memory_space=pltpu.VMEM)
-    planes = pl.BlockSpec((PLANES, FEATS, CY), lambda b: (b, 0, 0))
-    in_specs = [whole, whole, whole, planes] + [whole] * 8
+        en_ref[...] = north_edge(out_ref[0], mask_ref[0:1, :].astype(F32), fx_ref[0:1, :])
+        es_ref[...] = south_edge(out_ref[CX - 1], mask_ref[CX - 1 :, :].astype(F32), fx_ref[CX - 1 :, :])
+        grads_ref[...] = total[...]
+    else:
+        grads_ref[: 2 * HID, :] = total[:, :128]
+        grads_ref[2 * HID :, :] = total[:, 128:]
+
+
+def closure(first, owners, mask, got, lam, split_weights, *extra):
     if first:
-        in_specs += [whole, whole, planes]
-        out_shape = (PLANE, jax.ShapeDtypeStruct((2 * HID, HID), F32), EDGE, EDGE, EDGE, EDGE)
-        out_specs = (planes,) + (whole,) * 5
-    else:
-        in_specs += [whole]
-        out_shape = (PLANE, jax.ShapeDtypeStruct((4 * HID, 128), F32))
-        out_specs = (planes, whole)
-    return pl.pallas_call(
+        out_shape = (PLANE, near_shape(2 * HID, HID), EDGE, EDGE, EDGE, EDGE)
+    else:
+        out_shape = (PLANE, near_shape(4 * HID, 128))
+    return call(
         functools.partial(closure_kernel, first),
-        grid=(CX // PLANES,),
-        out_shape=out_shape,
-        in_specs=in_specs,
-        out_specs=out_specs,
-        scratch_shapes=[pltpu.VMEM((FEATS, STORE), BF), pltpu.VMEM((2 * HID, HID), F32)],
-        compiler_params=PARAMS,
-        name="closure1" if first else "closure0",
-    )(owners, mask, got, lam, *split_weights, b2, b3, *extra)
+        "closure1" if first else "closure0",
+        out_shape,
+        (owners, mask, got, lam, *split_weights, *extra),
+        [pltpu.VMEM((FEATS, STORE), BF), pltpu.VMEM((2 * HID, HID), F32)],
+        CLOSURE_MIB,
+    )
 
 
 def sum_kernel(parts_ref, out_ref):
@@ -402,19 +385,15 @@
     b3_ref[...] = sums_ref[NZ + 2 : NZ + 3, :NZ] * scale
 
 
-def reduce_params(packed, count):
+def reduce_params(packed, count, halos):
     parts = lax.all_to_all(packed, ("gx", "gy"), split_axis=0, concat_axis=0, tiled=True)
-    spread = pl.pallas_call(
-        sum_kernel, out_shape=jax.ShapeDtypeStruct(packed.shape, F32), compiler_params=PARAMS, name="sum"
-    )(parts)
+    parts, _ = lax.optimization_barrier((parts, halos))
+    spread = call(sum_kernel, "sum", near_shape(*packed.shape), (parts,))
     sums = lax.all_to_all(spread, ("gx", "gy"), split_axis=0, concat_axis=0, tiled=True)
     shapes = ((TRACERS * NZ, HID), (1, HID), (HID, HID), (1, HID), (NZ, HID), (1, NZ))
-    return pl.pallas_call(
-        functools.partial(unpack_kernel, step_size / float(np.sqrt(count))),
-        out_shape=tuple(jax.ShapeDtypeStruct(s, F32) for s in shapes),
-        compiler_params=PARAMS,
-        name="unpack",
-    )(sums)
+    scale = step_size / float(np.sqrt(count))
+    outs = tuple(jax.ShapeDtypeStruct(shape, F32) for shape in shapes)
+    return call(functools.partial(unpack_kernel, scale), "unpack", outs, (sums,))
 
 
 def exchange(north, south, west, east):
@@ -448,25 +427,24 @@
 ):
     stored_t = stored[0].T
     late = pack(1, counts, stored_t)
-    stored_t, costate, weight_mid, late = lax.optimization_barrier((stored_t, costate, weight_mid, late))
+    stored_t, late = lax.optimization_barrier((stored_t, late))
     late = lax.all_to_all(late, ("gx", "gy"), split_axis=0, concat_axis=0, tiled=True)
     early = pack(0, counts, stored_t)
-    split_weights = weights(weight_in, bias_in[None, :], weight_mid, weight_out.T)
-    b2 = bias_mid[:, None]
-    b3 = jnp.pad(bias_out, (0, PAD - NZ))[:, None]
+    costate, weight_mid, early = lax.optimization_barrier((costate, weight_mid, early))
+    early = lax.all_to_all(early, ("gx", "gy"), split_axis=0, concat_axis=0, tiled=True)
+    split_weights = weights(
+        weight_in, bias_in[None, :], weight_mid, bias_mid[None, :], weight_out.T, bias_out[None, :]
+    )
     planes, *sides = edges(costate.reshape(TRACERS * NZ * CX, CY), land_mask, flow_x, flow_y)
     halos = exchange(*sides)
     base = first_stencil(planes, land_mask, flow_x, flow_y, halos)
-    early, base, split_weights = lax.optimization_barrier((early, base, split_weights))
-    early = lax.all_to_all(early, ("gx", "gy"), split_axis=0, concat_axis=0, tiled=True)
-    lam, grads, *sides = closure(
-        True, owners, land_mask, late, planes, split_weights, b2, b3, flow_x, flow_y, base
-    )
+    lam, grads, *sides = closure(True, owners, land_mask, late, planes, split_weights, flow_x, flow_y, base)
+    down, packed = closure(False, owners, land_mask, early, lam, split_weights, grads)
+    *sides, packed = lax.optimization_barrier((*sides, packed))
     halos = exchange(*sides)
-    down, packed = closure(False, owners, land_mask, early, lam, split_weights, b2, b3, grads)
     adjoint = last_stencil(lam, down, land_mask, flow_x, flow_y, halos)
     count = CX * CY * lax.axis_size("gx") * lax.axis_size("gy")
-    g1, gb1, g2, gb2, g3, gb3 = reduce_params(packed, count)
+    g1, gb1, g2, gb2, g3, gb3 = reduce_params(packed, count, halos)
     return (adjoint.reshape(costate.shape), g1, gb1[0], g2, gb2[0], g3.T, gb3[0])
 
 

time: 149 us -> 155 us (1.040)
  the two profiles are of different devices: /device:TPU:33 before, /device:TPU:1 now
where the time goes in v3:
time: 155 us; the launch traced here: 154 us
  starting transfers between devices  60.2 us (39%)
  Pallas kernels  39.4 us (25%)
  waiting for transfers between devices  33.2 us (21%)
  local copies, waits for them, and re-layouts  20 us (13%)
    pallas_call x8, Pallas kernels, call(): pl.pallas_call(kernel, out_shape=out_shape, in_specs=[pl.BlockSpec(memory...  28.9 us
    unnamed x74, local copies, waits for them, and re-layouts  20 us
    all_to_all x1, waiting for transfers between devices, on_device(): lax.all_to_all(late, ('gx', 'gy'), split_axis=0, concat_axis=0, tiled=True)  18.8 us
    all_to_all x1, starting transfers between devices, reduce_params(): lax.all_to_all(spread, ('gx', 'gy'), split_axis=0, concat_axis=0, tiled=T...  11.9 us
    all_to_all x1, starting transfers between devices, on_device(): lax.all_to_all(late, ('gx', 'gy'), split_axis=0, concat_axis=0, tiled=True)  11.5 us
    pallas_call x2, Pallas kernels, pack(): pl.pallas_call(functools.partial(pack_kernel, moment), out_shape=pltpu.HB...  10.5 us
    all_to_all x1, starting transfers between devices, reduce_params(): lax.all_to_all(packed, ('gx', 'gy'), split_axis=0, concat_axis=0, tiled=T...  10.1 us
    all_to_all x1, waiting for transfers between devices, reduce_params(): lax.all_to_all(spread, ('gx', 'gy'), split_axis=0, concat_axis=0, tiled=T...  9.33 us
  transfers between devices with their start and end apart: 12, of which 6 were waited for; matrix products, arithmetic and copies ran while one was open for 0% of the time, Pallas kernels for 14%

profile of v3, /device:TPU:1, one launch (start us, length us, event | category | flops | bytes accessed | tf_op | source)
XLA Modules:
  0.0 153.7 jit_solution(11657093875352601577)
XLA Ops:
  0.6 5.2 %pack1.1 = bf16[128,48,128]{2,1,0:T(8,128)(2,1)} custom-call(s32[1,128]{1,0:T(1,128)} %counts_ref.3, bf16[360,4096]{1,0:T(8,128)(2,1)} %bitcast.25), custom_call_target="tpu_custom_call" | custom-call | tf_op jit(solution)/shard_map/pack1/pallas_call | solution.py:105
  5.9 11.5 %all-to-all-start = ((bf16[128,48,128]{2,1,0:T(8,128)(2,1)}), bf16[128,48,128]{2,1,0:T(8,128)(2,1)S(1)}, u32[]{:S(2)}, u32[]{:S(2)}) async-start(bf16[128,48,128]{2,1,0:T(8,128)(2,1)} %pack1.1), calls=%async_computation | async-start | bytes 3145728 | tf_op jit(solution)/shard_map/all_to_all | solution.py:431
  17.4 5.2 %pack0.1 = bf16[128,48,128]{2,1,0:T(8,128)(2,1)} custom-call(s32[1,128]{1,0:T(1,128)} %counts_ref.3, bf16[360,4096]{1,0:T(8,128)(2,1)} %bitcast.26), custom_call_target="tpu_custom_call" | custom-call | tf_op jit(solution)/shard_map/pack0/pallas_call | solution.py:105
  22.7 18.8 %all-to-all-done.refs_2_ = bf16[128,48,128]{2,1,0:T(8,128)(2,1)S(1)} async-done(((bf16[128,48,128]{2,1,0:T(8,128)(2,1)}), bf16[128,48,128]{2,1,0:T(8,128)(2,1)S(1)}, u32[]{:S(2)}, u32[]{:S(2)}) %all-to-all-start) | async-done | bytes 1572896 | tf_op jit(solution)/shard_map/all_to_all | solution.py:431
  41.5 4.8 %all-to-all-start.1 = ((bf16[128,48,128]{2,1,0:T(8,128)(2,1)}), bf16[128,48,128]{2,1,0:T(8,128)(2,1)S(1)}, u32[]{:S(2)}, u32[]{:S(2)}) async-start(bf16[128,48,128]{2,1,0:T(8,128)(2,1)} %pack0.1), calls=%async_computation.1 | async-start | bytes 3145728 | tf_op jit(solution)/shard_map/all_to_all | solution.py:434
  46.4 1.4 copy-done.4
  47.8 1.1 edges.1
  48.8 3.1 %collective-permute-start = (f32[192,128]{1,0:T(8,128)S(1)}, f32[192,128]{1,0:T(8,128)S(1)}, u32[]{:S(2)}, u32[]{:S(2)}) collective-permute-start(f32[192,128]{1,0:T(8,128)S(1)} %get-tuple-element.58), channel_id=1, source_target_pairs={{16,0},{32,16},{48,32},{64,48},{80,64},{96,80},{112,96},{17,1},{33... | collective-permute-start | bytes 294920 | tf_op jit(solution)/shard_map/ppermute | solution.py:406
  51.9 2.4 %collective-permute-start.1 = (f32[192,128]{1,0:T(8,128)S(1)}, f32[192,128]{1,0:T(8,128)S(1)}, u32[]{:S(2)}, u32[]{:S(2)}) collective-permute-start(f32[192,128]{1,0:T(8,128)S(1)} %get-tuple-element.59), channel_id=1, source_target_pairs={{0,16},{16,32},{32,48},{48,64},{64,80},{80,96},{96,112},{1,17},{17... | collective-permute-start | bytes 294920 | tf_op jit(solution)/shard_map/ppermute | solution.py:407
  54.4 1.3 collective-permute-start.2
  55.7 4.2 %collective-permute-start.3 = (f32[192,128]{1,0:T(8,128)S(1)}, f32[192,128]{1,0:T(8,128)S(1)}, u32[]{:S(2)}, u32[]{:S(2)}) collective-permute-start(f32[192,128]{1,0:T(8,128)S(1)} %get-tuple-element.61), channel_id=1, source_target_pairs={{0,1},{1,2},{2,3},{3,4},{4,5},{5,6},{6,7},{7,8},{8,9},{9,10},{10,1... | collective-permute-start | bytes 294920 | tf_op jit(solution)/shard_map/ppermute | solution.py:409
  59.9 0.9 copy-done.18
  65.0 1.8 %collective-permute-done.2.hw_ref = f32[192,128]{1,0:T(8,128)S(1)} collective-permute-done((f32[192,128]{1,0:T(8,128)S(1)}, f32[192,128]{1,0:T(8,128)S(1)}, u32[]{:S(2)}, u32[]{:S(2)}) %collective-permute-start.2) | collective-permute-done | bytes 98336 | tf_op jit(solution)/shard_map/ppermute | solution.py:408
  66.8 1.7 %stencil1.1.refs_14_ = f32[16,192,128]{2,1,0:T(8,128)S(1)} custom-call(f32[16,192,128]{2,1,0:T(8,128)S(1)} %get-tuple-element.48.lam_ref.refs_3_, s32[16,128]{1,0:T(8,128)S(1)} %copy-done.19, f32[16,128]{1,0:T(8,128)S(1)} %copy-done.23, f32[16,128]{1,0:T(8,128)S(1)} %copy-done.25, f32[192,128]{1,0:T(8,128)S(1)} %collective-permute-done.hn_ref, ...), custom_call_target="tpu_custom_call" | custom-call | tf_op jit(solution)/shard_map/stencil1/pallas_call | solution.py:59
  68.6 10.6 %closure1.1 = (f32[16,192,128]{2,1,0:T(8,128)S(1)}, f32[512,256]{1,0:T(8,128)S(1)}, f32[192,128]{1,0:T(8,128)S(1)}, f32[192,128]{1,0:T(8,128)S(1)}, f32[192,128]{1,0:T(8,128)S(1)}, /*index=5*/f32[192,128]{1,0:T(8,128)S(1)}) custom-call(s32[16,128]{1,0:T(8,128)S(1)} %copy-done.28, s32[16,128]{1,0:T(8,128)S(1)} %copy-done.19, ...), custom_call_target="tpu_custom_call" | custom-call | tf_op jit(solution)/shard_map/closure1/pallas_call | solution.py:59
  82.5 0.9 copy-done.6
  83.5 0.9 copy-done.8
  85.4 1.0 copy-done.12
  89.6 10.1 %closure0.1 = (f32[16,192,128]{2,1,0:T(8,128)S(1)}, f32[1024,128]{1,0:T(8,128)S(1)}) custom-call(s32[16,128]{1,0:T(8,128)S(1)} %copy-done.29, s32[16,128]{1,0:T(8,128)S(1)} %copy-done.19, bf16[128,48,128]{2,1,0:T(8,128)(2,1)S(1)} %all-to-all-done.1.refs_2_, f32[16,192,128]{2,1,0:T(8,128)S(1)} %get-tuple-element.62.refs_3_.lam_ref, ...), custom_call_target="tpu_custom_call" | custom-call | tf_op jit(solution)/shard_map/closure0/pallas_call | solution.py:59
  99.7 1.2 copy-done.2
  101.7 10.1 %all-to-all-start.2 = ((f32[128,8,128]{2,1,0:T(8,128)}), f32[128,8,128]{2,1,0:T(8,128)S(1)}, u32[]{:S(2)}, u32[]{:S(2)}) async-start(f32[128,8,128]{2,1,0:T(8,128)} %bitcast.20), calls=%async_computation.2 | async-start | bytes 1048576 | tf_op jit(solution)/shard_map/all_to_all | solution.py:389
  111.8 3.0 %collective-permute-start.4 = (f32[192,128]{1,0:T(8,128)}, f32[192,128]{1,0:T(8,128)S(1)}, u32[]{:S(2)}, u32[]{:S(2)}) collective-permute-start(f32[192,128]{1,0:T(8,128)} %copy-done.36), channel_id=1, source_target_pairs={{16,0},{32,16},{48,32},{64,48},{80,64},{96,80},{112,96},{17,1},{33... | collective-permute-start | bytes 294920 | tf_op jit(solution)/shard_map/ppermute | solution.py:406
  114.8 2.6 %collective-permute-start.5 = (f32[192,128]{1,0:T(8,128)}, f32[192,128]{1,0:T(8,128)S(1)}, u32[]{:S(2)}, u32[]{:S(2)}) collective-permute-start(f32[192,128]{1,0:T(8,128)} %copy-done.35), channel_id=1, source_target_pairs={{0,16},{16,32},{32,48},{48,64},{64,80},{80,96},{96,112},{1,17},{17... | collective-permute-start | bytes 294920 | tf_op jit(solution)/shard_map/ppermute | solution.py:407
  117.4 1.3 collective-permute-start.6
  118.7 4.0 %collective-permute-start.7 = (f32[192,128]{1,0:T(8,128)}, f32[192,128]{1,0:T(8,128)S(1)}, u32[]{:S(2)}, u32[]{:S(2)}) collective-permute-start(f32[192,128]{1,0:T(8,128)} %copy-done.33), channel_id=1, source_target_pairs={{0,1},{1,2},{2,3},{3,4},{4,5},{5,6},{6,7},{7,8},{8,9},{9,10},{10,1... | collective-permute-start | bytes 294920 | tf_op jit(solution)/shard_map/ppermute | solution.py:409
  122.7 1.3 collective-permute-done.6.hw_ref
  124.0 1.1 collective-permute-done.7.he_ref
  125.9 1.0 sum.1
  126.9 11.9 %all-to-all-start.3 = ((f32[128,8,128]{2,1,0:T(8,128)}), f32[128,8,128]{2,1,0:T(8,128)S(1)}, u32[]{:S(2)}, u32[]{:S(2)}) async-start(f32[128,8,128]{2,1,0:T(8,128)} %bitcast.11), calls=%async_computation.3 | async-start | bytes 1048576 | tf_op jit(solution)/shard_map/all_to_all | solution.py:392
  138.8 1.4 copy-done.3
  140.2 3.4 %stencil0.1 = f32[2880,128]{1,0:T(8,128)} custom-call(f32[16,192,128]{2,1,0:T(8,128)S(1)} %get-tuple-element.62.refs_3_.lam_ref, f32[16,192,128]{2,1,0:T(8,128)S(1)} %copy-done.3, s32[16,128]{1,0:T(8,128)S(1)} %copy-done.19, f32[16,128]{1,0:T(8,128)S(1)} %copy-done.23, f32[16,128]{1,0:T(8,128)S(1)} %copy-done.26, ...), custom_call_target="tpu_custom_call" | custom-call | tf_op jit(solution)/shard_map/stencil0/pallas_call | solution.py:59
  143.6 9.3 %all-to-all-done.3 = f32[128,8,128]{2,1,0:T(8,128)S(1)} async-done(((f32[128,8,128]{2,1,0:T(8,128)}), f32[128,8,128]{2,1,0:T(8,128)S(1)}, u32[]{:S(2)}, u32[]{:S(2)}) %all-to-all-start.3) | async-done | bytes 524320 | tf_op jit(solution)/shard_map/all_to_all | solution.py:392
  (76 shorter events, 14.1 us)
Async XLA Ops:
  5.9 35.6 %all-to-all-start = ((bf16[128,48,128]{2,1,0:T(8,128)(2,1)}), bf16[128,48,128]{2,1,0:T(8,128)(2,1)S(1)}, u32[]{:S(2)}, u32[]{:S(2)}) async-start(bf16[128,48,128]{2,1,0:T(8,128)(2,1)} %pack1.1), calls=%async_computation | async-start | bytes 3145728 | tf_op jit(solution)/shard_map/all_to_all | solution.py:431
  22.6 23.7 %copy-start.19 = (s32[16,128]{1,0:T(8,128)S(1)}, s32[16,128]{1,0:T(8,128)}, u32[]{:S(2)}) copy-start(s32[16,128]{1,0:T(8,128)} %mask_ref.5) | copy-start | bytes 24580
  22.7 23.7 %copy-start.23 = (f32[16,128]{1,0:T(8,128)S(1)}, f32[16,128]{1,0:T(8,128)}, u32[]{:S(2)}) copy-start(f32[16,128]{1,0:T(8,128)} %fx_ref.5) | copy-start | bytes 24580
  22.7 23.7 %copy-start.24 = (f32[16,128]{1,0:T(8,128)S(1)}, f32[16,128]{1,0:T(8,128)}, u32[]{:S(2)}) copy-start(f32[16,128]{1,0:T(8,128)} %fy_ref.5) | copy-start | bytes 24580
  41.5 4.8 %copy-start = (bf16[128,48,128]{2,1,0:T(8,128)(2,1)}, bf16[128,48,128]{2,1,0:T(8,128)(2,1)S(1)}, u32[]{:S(2)}) copy-start(bf16[128,48,128]{2,1,0:T(8,128)(2,1)S(1)} %all-to-all-done.refs_2_) | copy-start | bytes 4718596
  41.5 41.0 %all-to-all-start.1 = ((bf16[128,48,128]{2,1,0:T(8,128)(2,1)}), bf16[128,48,128]{2,1,0:T(8,128)(2,1)S(1)}, u32[]{:S(2)}, u32[]{:S(2)}) async-start(bf16[128,48,128]{2,1,0:T(8,128)(2,1)} %pack0.1), calls=%async_computation.1 | async-start | bytes 3145728 | tf_op jit(solution)/shard_map/all_to_all | solution.py:434
  46.4 1.4 copy-start.4
  47.8 19.0 %copy-start.25 = (f32[16,128]{1,0:T(8,128)S(1)}, f32[16,128]{1,0:T(8,128)}, u32[]{:S(2)}) copy-start(f32[16,128]{1,0:T(8,128)} %fy_ref.5) | copy-start | bytes 24580
  48.8 16.2 %collective-permute-start = (f32[192,128]{1,0:T(8,128)S(1)}, f32[192,128]{1,0:T(8,128)S(1)}, u32[]{:S(2)}, u32[]{:S(2)}) collective-permute-start(f32[192,128]{1,0:T(8,128)S(1)} %get-tuple-element.58), channel_id=1, source_target_pairs={{16,0},{32,16},{48,32},{64,48},{80,64},{96,80},{112,96},{17,1},{33... | collective-permute-start | bytes 294920 | tf_op jit(solution)/shard_map/ppermute | solution.py:406
  51.9 13.1 %collective-permute-start.1 = (f32[192,128]{1,0:T(8,128)S(1)}, f32[192,128]{1,0:T(8,128)S(1)}, u32[]{:S(2)}, u32[]{:S(2)}) collective-permute-start(f32[192,128]{1,0:T(8,128)S(1)} %get-tuple-element.59), channel_id=1, source_target_pairs={{0,16},{16,32},{32,48},{48,64},{64,80},{80,96},{96,112},{1,17},{17... | collective-permute-start | bytes 294920 | tf_op jit(solution)/shard_map/ppermute | solution.py:407
  54.4 12.4 %collective-permute-start.2 = (f32[192,128]{1,0:T(8,128)S(1)}, f32[192,128]{1,0:T(8,128)S(1)}, u32[]{:S(2)}, u32[]{:S(2)}) collective-permute-start(f32[192,128]{1,0:T(8,128)S(1)} %get-tuple-element.60), channel_id=1, source_target_pairs={{1,0},{2,1},{3,2},{4,3},{5,4},{6,5},{7,6},{8,7},{9,8},{10,9},{11,1... | collective-permute-start | bytes 294920 | tf_op jit(solution)/shard_map/ppermute | solution.py:408
  55.7 11.1 %collective-permute-start.3 = (f32[192,128]{1,0:T(8,128)S(1)}, f32[192,128]{1,0:T(8,128)S(1)}, u32[]{:S(2)}, u32[]{:S(2)}) collective-permute-start(f32[192,128]{1,0:T(8,128)S(1)} %get-tuple-element.61), channel_id=1, source_target_pairs={{0,1},{1,2},{2,3},{3,4},{4,5},{5,6},{6,7},{7,8},{8,9},{9,10},{10,1... | collective-permute-start | bytes 294920 | tf_op jit(solution)/shard_map/ppermute | solution.py:409
  59.9 1.0 copy-start.18
  64.9 3.6 %copy-start.5 = (bf16[512,256]{1,0:T(8,128)(2,1)}, bf16[512,256]{1,0:T(8,128)(2,1)S(1)}, u32[]{:S(2)}) copy-start(bf16[512,256]{1,0:T(8,128)(2,1)S(1)} %get-tuple-element.51.refs_5_) | copy-start | bytes 786436
  64.9 3.6 %copy-start.7 = (bf16[512,256]{1,0:T(8,128)(2,1)}, bf16[512,256]{1,0:T(8,128)(2,1)S(1)}, u32[]{:S(2)}) copy-start(bf16[512,256]{1,0:T(8,128)(2,1)S(1)} %get-tuple-element.54.refs_8_) | copy-start | bytes 786436
  65.0 3.6 %copy-start.9 = (bf16[384,256]{1,0:T(8,128)(2,1)}, bf16[384,256]{1,0:T(8,128)(2,1)S(1)}, u32[]{:S(2)}) copy-start(bf16[384,256]{1,0:T(8,128)(2,1)S(1)} %get-tuple-element.55.refs_9_) | copy-start | bytes 589828
  65.0 3.6 %copy-start.13 = (f32[256,1]{1,0:T(8,128)}, f32[256,1]{1,0:T(8,128)S(1)}, u32[]{:S(2)}) copy-start(f32[256,1]{1,0:T(8,128)S(1)} %get-tuple-element.56.refs_10_) | copy-start | bytes 3076
  65.0 3.6 %copy-start.16 = (bf16[128,256]{1,0:T(8,128)(2,1)}, bf16[128,256]{1,0:T(8,128)(2,1)S(1)}, u32[]{:S(2)}) copy-start(bf16[128,256]{1,0:T(8,128)(2,1)S(1)} %get-tuple-element.52.refs_6_) | copy-start | bytes 196612
  65.0 3.6 %copy-start.21 = (f32[64,1]{1,0:T(8,128)}, f32[64,1]{1,0:T(8,128)S(1)}, u32[]{:S(2)}) copy-start(f32[64,1]{1,0:T(8,128)S(1)} %get-tuple-element.57.refs_11_) | copy-start | bytes 772
  66.8 1.8 %copy-start.1 = (bf16[128,48,128]{2,1,0:T(8,128)(2,1)S(1)}, bf16[128,48,128]{2,1,0:T(8,128)(2,1)}, u32[]{:S(2)}) copy-start(bf16[128,48,128]{2,1,0:T(8,128)(2,1)} %copy-done) | copy-start | bytes 4718596
  66.8 1.8 %copy-start.28 = (s32[16,128]{1,0:T(8,128)S(1)}, s32[16,128]{1,0:T(8,128)}, u32[]{:S(2)}) copy-start(s32[16,128]{1,0:T(8,128)} %refs_0_.3) | copy-start | bytes 24580
  82.5 1.0 copy-start.6
  85.4 1.0 copy-start.12
  99.7 1.2 copy-start.2
  101.7 37.1 %copy-start.26 = (f32[16,128]{1,0:T(8,128)S(1)}, f32[16,128]{1,0:T(8,128)}, u32[]{:S(2)}) copy-start(f32[16,128]{1,0:T(8,128)} %fy_ref.5) | copy-start | bytes 24580
  101.7 24.2 %all-to-all-start.2 = ((f32[128,8,128]{2,1,0:T(8,128)}), f32[128,8,128]{2,1,0:T(8,128)S(1)}, u32[]{:S(2)}, u32[]{:S(2)}) async-start(f32[128,8,128]{2,1,0:T(8,128)} %bitcast.20), calls=%async_computation.2 | async-start | bytes 1048576 | tf_op jit(solution)/shard_map/all_to_all | solution.py:389
  111.8 10.9 %collective-permute-start.4 = (f32[192,128]{1,0:T(8,128)}, f32[192,128]{1,0:T(8,128)S(1)}, u32[]{:S(2)}, u32[]{:S(2)}) collective-permute-start(f32[192,128]{1,0:T(8,128)} %copy-done.36), channel_id=1, source_target_pairs={{16,0},{32,16},{48,32},{64,48},{80,64},{96,80},{112,96},{17,1},{33... | collective-permute-start | bytes 294920 | tf_op jit(solution)/shard_map/ppermute | solution.py:406
  114.8 7.9 %collective-permute-start.5 = (f32[192,128]{1,0:T(8,128)}, f32[192,128]{1,0:T(8,128)S(1)}, u32[]{:S(2)}, u32[]{:S(2)}) collective-permute-start(f32[192,128]{1,0:T(8,128)} %copy-done.35), channel_id=1, source_target_pairs={{0,16},{16,32},{32,48},{48,64},{64,80},{80,96},{96,112},{1,17},{17... | collective-permute-start | bytes 294920 | tf_op jit(solution)/shard_map/ppermute | solution.py:407
  117.4 6.6 %collective-permute-start.6 = (f32[192,128]{1,0:T(8,128)}, f32[192,128]{1,0:T(8,128)S(1)}, u32[]{:S(2)}, u32[]{:S(2)}) collective-permute-start(f32[192,128]{1,0:T(8,128)} %copy-done.34), channel_id=1, source_target_pairs={{1,0},{2,1},{3,2},{4,3},{5,4},{6,5},{7,6},{8,7},{9,8},{10,9},{11,1... | collective-permute-start | bytes 294920 | tf_op jit(solution)/shard_map/ppermute | solution.py:408
  118.7 6.5 %collective-permute-start.7 = (f32[192,128]{1,0:T(8,128)}, f32[192,128]{1,0:T(8,128)S(1)}, u32[]{:S(2)}, u32[]{:S(2)}) collective-permute-start(f32[192,128]{1,0:T(8,128)} %copy-done.33), channel_id=1, source_target_pairs={{0,1},{1,2},{2,3},{3,4},{4,5},{5,6},{6,7},{7,8},{8,9},{9,10},{10,1... | collective-permute-start | bytes 294920 | tf_op jit(solution)/shard_map/ppermute | solution.py:409
  126.9 26.1 %all-to-all-start.3 = ((f32[128,8,128]{2,1,0:T(8,128)}), f32[128,8,128]{2,1,0:T(8,128)S(1)}, u32[]{:S(2)}, u32[]{:S(2)}) async-start(f32[128,8,128]{2,1,0:T(8,128)} %bitcast.11), calls=%async_computation.3 | async-start | bytes 1048576 | tf_op jit(solution)/shard_map/all_to_all | solution.py:392
  138.8 1.4 copy-start.3
  (17 other events, 13.0 us)

commit v4 on v3

--- a/solution.py
+++ b/solution.py
@@ -15,6 +15,7 @@
 HID = 256
 SLOT = 32
 HALF = SLOT // 2
+BLOCK = SLOT + HALF
 CX = 16
 CY = 128
 DEV = 128
@@ -66,18 +67,20 @@
     )(*args)
 
 
-def pack_kernel(moment, counts_ref, stored_ref, out_ref, near, padded, sem):
-    top = moment * TRACERS * NZ // 8 * 8
-    copy = pltpu.make_async_copy(stored_ref.at[top : top + near.shape[0], :], near, sem)
-    copy.start()
+def pack_kernel(counts_ref, stored_ref, out_ref, near, padded, rows_out, in_sems, out_sem):
+    cut = (FEATS - TRACERS * (PAD - NZ) + 7) // 8 * 8
+    parts = (slice(0, cut), slice(cut, 2 * TRACERS * NZ))
+    copies = [pltpu.make_async_copy(stored_ref.at[p, :], near.at[p, :], in_sems.at[i]) for i, p in enumerate(parts)]
+    for copy in copies:
+        copy.start()
     lane = lax.broadcasted_iota(jnp.int32, (SLOT, 256), 1)
     offset = lane - lax.broadcasted_iota(jnp.int32, (SLOT, 256), 0)
-    for t in range(TRACERS):
-        padded[t * PAD + NZ : (t + 1) * PAD, :] = jnp.zeros((PAD - NZ, STORE), BF)
-    copy.wait()
-    skip = moment * TRACERS * NZ - top
-    for t in range(TRACERS):
-        padded[t * PAD : t * PAD + NZ, :] = near[skip + t * NZ : skip + (t + 1) * NZ, :]
+    for block in range(2 * TRACERS):
+        padded[block * PAD + NZ : (block + 1) * PAD, :] = jnp.zeros((PAD - NZ, STORE), BF)
+    for moment in range(2):
+        copies[moment].wait()
+        for block in range(moment * TRACERS, (moment + 1) * TRACERS):
+            padded[block * PAD : block * PAD + NZ, :] = near[block * NZ : (block + 1) * NZ, :]
 
     def group(g, start):
         base = pl.multiple_of(jnp.minimum((start // 128) * 128, STORE - 256), 128)
@@ -87,33 +90,48 @@
             start = start + counts_ref[0, 4 * g + i]
         rows = dot_nt(jnp.concatenate(hots, axis=0), padded[:, pl.ds(base, 256)])
         for i in range(4):
-            mine = rows[i * SLOT : (i + 1) * SLOT]
-            rest = jnp.concatenate([mine[:HALF, 2 * PAD :], mine[HALF:, 2 * PAD :]], axis=1)
-            out_ref[4 * g + i, :SLOT, :] = mine[:, : 2 * PAD].astype(BF)
-            out_ref[4 * g + i, SLOT:, :] = rest.astype(BF)
+            for moment in range(2):
+                at, first = moment * BLOCK, moment * FEATS
+                mine = rows[i * SLOT : (i + 1) * SLOT, first : first + FEATS]
+                rest = jnp.concatenate([mine[:HALF, 2 * PAD :], mine[HALF:, 2 * PAD :]], axis=1)
+                rows_out[4 * g + i, at : at + SLOT, :] = mine[:, : 2 * PAD].astype(BF)
+                rows_out[4 * g + i, at + SLOT : at + BLOCK, :] = rest.astype(BF)
         return start
+
+    def leave(j):
+        tiles = pl.ds(j * 4 * UNROLL, 4 * UNROLL)
+        return pltpu.make_async_copy(rows_out.at[tiles], out_ref.at[tiles], out_sem.at[j])
+
+    start = jnp.int32(0)
+    steps = DEV // 4 // UNROLL
 
     def groups(j, start):
         for u in range(UNROLL):
             start = group(j * UNROLL + u, start)
+        leave(j).start()
         return start
 
-    lax.fori_loop(0, DEV // 4 // UNROLL, groups, jnp.int32(0))
-
-
-def pack(moment, counts, stored_t):
+    lax.fori_loop(0, steps, groups, start)
+    for j in range(steps):
+        leave(j).wait()
+
+
+def pack(counts, stored_t):
+    anywhere = pl.BlockSpec(memory_space=pl.ANY)
     return pl.pallas_call(
-        functools.partial(pack_kernel, moment),
-        out_shape=pltpu.HBM((DEV, SLOT + HALF, 128), BF),
-        in_specs=[pl.BlockSpec(memory_space=pltpu.SMEM), pl.BlockSpec(memory_space=pl.ANY)],
-        out_specs=pl.BlockSpec(memory_space=pltpu.VMEM),
+        pack_kernel,
+        out_shape=pltpu.HBM((DEV, 2 * BLOCK, 128), BF),
+        in_specs=[pl.BlockSpec(memory_space=pltpu.SMEM), anywhere],
+        out_specs=anywhere,
         scratch_shapes=[
-            pltpu.VMEM((TRACERS * NZ + 4, STORE), BF),
-            pltpu.VMEM((FEATS, STORE), BF),
-            pltpu.SemaphoreType.DMA,
+            pltpu.VMEM((2 * TRACERS * NZ, STORE), BF),
+            pltpu.VMEM((2 * FEATS, STORE), BF),
+            pltpu.VMEM((DEV, 2 * BLOCK, 128), BF),
+            pltpu.SemaphoreType.DMA((2,)),
+            pltpu.SemaphoreType.DMA((DEV // 4 // UNROLL,)),
         ],
-        compiler_params=params(8),
-        name=f"pack{moment}",
+        compiler_params=params(24),
+        name="pack",
     )(*(pltpu.with_memory_space_constraint(a, pltpu.HBM) for a in (counts, stored_t)))
 
 
@@ -243,33 +261,20 @@
     return call(last_kernel, "stencil0", out, (lam, down, mask, fx, fy, *halos))
 
 
-def closure_kernel(first, *refs):
-    (owner_ref, mask_ref, got_ref, lam_ref, f1_ref, f2_ref, f3_ref, r3_ref, r2_ref, r1_ref, b2_ref, b3_ref) = refs[:12]
-    refs = refs[12:]
-    if first:
-        fx_ref, fy_ref, base_ref, out_ref, grads_ref, en_ref, es_ref, ew_ref, ee_ref = refs[:9]
-        refs = refs[9:]
-    else:
-        before_ref, out_ref, grads_ref = refs[:3]
-        refs = refs[3:]
-    rows_ref, total = refs
+def closure_step(first, got_ref, owner_ref, mask_ref, lam_ref, weight_refs, base_ref, out_ref, rows_ref, total):
+    f1_ref, f2_ref, f3_ref, r3_ref, r2_ref, r1_ref, b2_ref, b3_ref = weight_refs
     for half in range(2):
         for g in range(DEV // 8):
             at = half * (STORE // 2) + g * 128
-            main = [got_ref[8 * g + i, half * HALF : (half + 1) * HALF, :] for i in range(8)]
+            lo = first + half * HALF
+            main = [got_ref[8 * g + i, lo : lo + HALF, :] for i in range(8)]
             rows_ref[: 2 * PAD, at : at + 128] = jnp.concatenate(main, axis=0).T
     for g in range(DEV // 8):
-        rest = [got_ref[8 * g + i, SLOT:, :] for i in range(8)]
+        rest = [got_ref[8 * g + i, first + SLOT : first + BLOCK, :] for i in range(8)]
         both = jnp.concatenate(rest, axis=0).T
         rows_ref[2 * PAD :, g * 128 : (g + 1) * 128] = both[:PAD]
         at = STORE // 2 + g * 128
         rows_ref[2 * PAD :, at : at + 128] = both[PAD:]
-    if first:
-        total[...] = jnp.zeros_like(total)
-        ew_ref[...] = jnp.zeros_like(ew_ref)
-        ee_ref[...] = jnp.zeros_like(ee_ref)
-    else:
-        total[...] = before_ref[...]
 
     def wide(ref):
         return jnp.concatenate([ref[i : i + 1, :] for i in range(CX)], axis=1)
@@ -334,34 +339,34 @@
         for t in range(TRACERS):
             lo, hi = t * PAD, (t + 1) * PAD
             down = d0[lo:hi, part] + direct[t][:, part]
-            if first:
+            if base_ref is not None:
                 out_ref[i, lo:hi, :] = base_ref[i, lo:hi, :] + step_size * down
             else:
                 out_ref[i, lo:hi, :] = down
-        if first:
-            edge_plane(i, out_ref[i], mask_ref[i : i + 1, :].astype(F32), fy_ref[i : i + 1, :], ew_ref, ee_ref)
-    if first:
-        en_ref[...] = north_edge(out_ref[0], mask_ref[0:1, :].astype(F32), fx_ref[0:1, :])
-        es_ref[...] = south_edge(out_ref[CX - 1], mask_ref[CX - 1 :, :].astype(F32), fx_ref[CX - 1 :, :])
-        grads_ref[...] = total[...]
-    else:
-        grads_ref[: 2 * HID, :] = total[:, :128]
-        grads_ref[2 * HID :, :] = total[:, 128:]
-
-
-def closure(first, owners, mask, got, lam, split_weights, *extra):
-    if first:
-        out_shape = (PLANE, near_shape(2 * HID, HID), EDGE, EDGE, EDGE, EDGE)
-    else:
-        out_shape = (PLANE, near_shape(4 * HID, 128))
-    return call(
-        functools.partial(closure_kernel, first),
-        "closure1" if first else "closure0",
-        out_shape,
-        (owners, mask, got, lam, *split_weights, *extra),
-        [pltpu.VMEM((FEATS, STORE), BF), pltpu.VMEM((2 * HID, HID), F32)],
-        CLOSURE_MIB,
-    )
+
+
+def closure_kernel(got_ref, owner_ref, mask_ref, fx_ref, fy_ref, planes_ref, base_ref, *refs):
+    weight_refs, refs = refs[:8], refs[8:]
+    lam_ref, down_ref, grads_ref, en_ref, es_ref, ew_ref, ee_ref, late_ref, early_ref, total = refs
+    total[...] = jnp.zeros_like(total)
+    ew_ref[...] = jnp.zeros_like(ew_ref)
+    ee_ref[...] = jnp.zeros_like(ee_ref)
+    step = functools.partial(closure_step, got_ref=got_ref, owner_ref=owner_ref, mask_ref=mask_ref, total=total)
+    step(BLOCK, lam_ref=planes_ref, weight_refs=weight_refs, base_ref=base_ref, out_ref=lam_ref, rows_ref=late_ref)
+    for x in range(CX):
+        edge_plane(x, lam_ref[x], mask_ref[x : x + 1, :].astype(F32), fy_ref[x : x + 1, :], ew_ref, ee_ref)
+    en_ref[...] = north_edge(lam_ref[0], mask_ref[0:1, :].astype(F32), fx_ref[0:1, :])
+    es_ref[...] = south_edge(lam_ref[CX - 1], mask_ref[CX - 1 :, :].astype(F32), fx_ref[CX - 1 :, :])
+    step(0, lam_ref=lam_ref, weight_refs=weight_refs, base_ref=None, out_ref=down_ref, rows_ref=early_ref)
+    grads_ref[: 2 * HID, :] = total[:, :128]
+    grads_ref[2 * HID :, :] = total[:, 128:]
+
+
+def closure(*args):
+    outs = (PLANE, PLANE, near_shape(4 * HID, 128), EDGE, EDGE, EDGE, EDGE)
+    rows = pltpu.VMEM((FEATS, STORE), BF)
+    scratch = [rows, rows, pltpu.VMEM((2 * HID, HID), F32)]
+    return call(closure_kernel, "closure", outs, args, scratch, CLOSURE_MIB)
 
 
 def sum_kernel(parts_ref, out_ref):
@@ -385,10 +390,14 @@
     b3_ref[...] = sums_ref[NZ + 2 : NZ + 3, :NZ] * scale
 
 
-def reduce_params(packed, count, halos):
+def reduce_params(packed, tied):
     parts = lax.all_to_all(packed, ("gx", "gy"), split_axis=0, concat_axis=0, tiled=True)
-    parts, _ = lax.optimization_barrier((parts, halos))
+    parts, _ = lax.optimization_barrier((parts, tied))
     spread = call(sum_kernel, "sum", near_shape(*packed.shape), (parts,))
+    return spread
+
+
+def finish_params(spread, count):
     sums = lax.all_to_all(spread, ("gx", "gy"), split_axis=0, concat_axis=0, tiled=True)
     shapes = ((TRACERS * NZ, HID), (1, HID), (HID, HID), (1, HID), (NZ, HID), (1, NZ))
     scale = step_size / float(np.sqrt(count))
@@ -396,18 +405,10 @@
     return call(functools.partial(unpack_kernel, scale), "unpack", outs, (sums,))
 
 
-def exchange(north, south, west, east):
-    gx, gy = lax.axis_size("gx"), lax.axis_size("gy")
-    down_x = [(i + 1, i) for i in range(gx - 1)]
-    up_x = [(i, i + 1) for i in range(gx - 1)]
-    down_y = [(i + 1, i) for i in range(gy - 1)]
-    up_y = [(i, i + 1) for i in range(gy - 1)]
-    return (
-        lax.ppermute(north, "gx", down_x),
-        lax.ppermute(south, "gx", up_x),
-        lax.ppermute(west, "gy", down_y),
-        lax.ppermute(east, "gy", up_y),
-    )
+def exchange(axis, before, after):
+    up = [(i, i + 1) for i in range(lax.axis_size(axis) - 1)]
+    down = [(j, i) for i, j in up]
+    return lax.ppermute(before, axis, down), lax.ppermute(after, axis, up)
 
 
 def on_device(
@@ -425,26 +426,27 @@
     weight_out,
     bias_out,
 ):
-    stored_t = stored[0].T
-    late = pack(1, counts, stored_t)
-    stored_t, late = lax.optimization_barrier((stored_t, late))
-    late = lax.all_to_all(late, ("gx", "gy"), split_axis=0, concat_axis=0, tiled=True)
-    early = pack(0, counts, stored_t)
-    costate, weight_mid, early = lax.optimization_barrier((costate, weight_mid, early))
-    early = lax.all_to_all(early, ("gx", "gy"), split_axis=0, concat_axis=0, tiled=True)
+    payload = pack(counts, stored[0].T)
+    costate, weight_mid, payload = lax.optimization_barrier((costate, weight_mid, payload))
+    got = lax.all_to_all(payload, ("gx", "gy"), split_axis=0, concat_axis=0, tiled=True)
     split_weights = weights(
         weight_in, bias_in[None, :], weight_mid, bias_mid[None, :], weight_out.T, bias_out[None, :]
     )
-    planes, *sides = edges(costate.reshape(TRACERS * NZ * CX, CY), land_mask, flow_x, flow_y)
-    halos = exchange(*sides)
+    planes, north, south, west, east = edges(
+        costate.reshape(TRACERS * NZ * CX, CY), land_mask, flow_x, flow_y
+    )
+    halos = exchange("gx", north, south) + exchange("gy", west, east)
     base = first_stencil(planes, land_mask, flow_x, flow_y, halos)
-    lam, grads, *sides = closure(True, owners, land_mask, late, planes, split_weights, flow_x, flow_y, base)
-    down, packed = closure(False, owners, land_mask, early, lam, split_weights, grads)
-    *sides, packed = lax.optimization_barrier((*sides, packed))
-    halos = exchange(*sides)
-    adjoint = last_stencil(lam, down, land_mask, flow_x, flow_y, halos)
+    lam, down, packed, north, south, west, east = closure(
+        got, owners, land_mask, flow_x, flow_y, planes, base, *split_weights
+    )
+    halos_x = exchange("gx", north, south)
+    spread = reduce_params(packed, halos_x)
+    west, east, spread = lax.optimization_barrier((west, east, spread))
+    halos_y = exchange("gy", west, east)
+    adjoint = last_stencil(lam, down, land_mask, flow_x, flow_y, halos_x + halos_y)
     count = CX * CY * lax.axis_size("gx") * lax.axis_size("gy")
-    g1, gb1, g2, gb2, g3, gb3 = reduce_params(packed, count, halos)
+    g1, gb1, g2, gb2, g3, gb3 = finish_params(spread, count)
     return (adjoint.reshape(costate.shape), g1, gb1[0], g2, gb2[0], g3.T, gb3[0])
 
 

time: 155 us -> 146 us (0.942)
  the two profiles are of different devices: /device:TPU:1 before, /device:TPU:32 now
where the time goes in v4:
time: 146 us; the launch traced here: 145 us
  starting transfers between devices  44.4 us (30%)
  Pallas kernels  37.8 us (26%)
  waiting for transfers between devices  34.4 us (24%)
  local copies, waits for them, and re-layouts  27.2 us (19%)
    pallas_call x7, Pallas kernels, call(): pl.pallas_call(kernel, out_shape=out_shape, in_specs=[pl.BlockSpec(memory...  31.6 us
    unnamed x82, local copies, waits for them, and re-layouts  27.2 us
    ppermute x8, waiting for transfers between devices, exchange(): return (lax.ppermute(before, axis, down), lax.ppermute(after, axis, up))  26.6 us
    ppermute x8, starting transfers between devices, exchange(): return (lax.ppermute(before, axis, down), lax.ppermute(after, axis, up))  21.5 us
    all_to_all x1, starting transfers between devices, on_device(): lax.all_to_all(payload, ('gx', 'gy'), split_axis=0, concat_axis=0, tiled=...  10.2 us
    all_to_all x1, waiting for transfers between devices, reduce_params(): lax.all_to_all(packed, ('gx', 'gy'), split_axis=0, concat_axis=0, tiled=T...  7.89 us
    all_to_all x1, starting transfers between devices, reduce_params(): lax.all_to_all(packed, ('gx', 'gy'), split_axis=0, concat_axis=0, tiled=T...  7.77 us
    pallas_call x1, Pallas kernels, pack(): pl.pallas_call(pack_kernel, out_shape=pltpu.HBM((DEV, 2 * BLOCK, 128), BF...  6.16 us
  transfers between devices with their start and end apart: 11, of which 6 were waited for; matrix products, arithmetic and copies ran while one was open for 0% of the time, Pallas kernels for 5%

profile of v4, /device:TPU:32, one launch (start us, length us, event | category | flops | bytes accessed | tf_op | source)
XLA Modules:
  0.0 144.7 jit_solution(10303622504452820983)
XLA Ops:
  0.6 6.2 %pack.1 = bf16[128,96,128]{2,1,0:T(8,128)(2,1)} custom-call(s32[1,128]{1,0:T(1,128)} %counts_ref.1, bf16[360,4096]{1,0:T(8,128)(2,1)} %bitcast.25), custom_call_target="tpu_custom_call" | custom-call | tf_op jit(solution)/shard_map/pack/pallas_call | solution.py:121
  6.8 10.2 %all-to-all-start = ((bf16[128,96,128]{2,1,0:T(8,128)(2,1)}), bf16[128,96,128]{2,1,0:T(8,128)(2,1)S(1)}, u32[]{:S(2)}, u32[]{:S(2)}) async-start(bf16[128,96,128]{2,1,0:T(8,128)(2,1)} %pack.1), calls=%async_computation | async-start | bytes 6291456 | tf_op jit(solution)/shard_map/all_to_all | solution.py:431
  17.1 1.4 copy-done.8
  18.5 1.1 edges.1
  19.6 1.3 collective-permute-start
  20.9 3.0 %collective-permute-start.1 = (f32[192,128]{1,0:T(8,128)S(1)}, f32[192,128]{1,0:T(8,128)S(1)}, u32[]{:S(2)}, u32[]{:S(2)}) collective-permute-start(f32[192,128]{1,0:T(8,128)S(1)} %get-tuple-element.44), channel_id=1, source_target_pairs={{0,16},{16,32},{32,48},{48,64},{64,80},{80,96},{96,112},{1,17},{17... | collective-permute-start | bytes 294920 | tf_op jit(solution)/shard_map/ppermute | solution.py:411
  23.9 4.5 %collective-permute-start.2 = (f32[192,128]{1,0:T(8,128)S(1)}, f32[192,128]{1,0:T(8,128)S(1)}, u32[]{:S(2)}, u32[]{:S(2)}) collective-permute-start(f32[192,128]{1,0:T(8,128)S(1)} %get-tuple-element.45), channel_id=1, source_target_pairs={{1,0},{2,1},{3,2},{4,3},{5,4},{6,5},{7,6},{8,7},{9,8},{10,9},{11,1... | collective-permute-start | bytes 294920 | tf_op jit(solution)/shard_map/ppermute | solution.py:411
  28.4 2.1 %collective-permute-start.3 = (f32[192,128]{1,0:T(8,128)S(1)}, f32[192,128]{1,0:T(8,128)S(1)}, u32[]{:S(2)}, u32[]{:S(2)}) collective-permute-start(f32[192,128]{1,0:T(8,128)S(1)} %get-tuple-element.46), channel_id=1, source_target_pairs={{0,1},{1,2},{2,3},{3,4},{4,5},{5,6},{6,7},{7,8},{8,9},{9,10},{10,1... | collective-permute-start | bytes 294920 | tf_op jit(solution)/shard_map/ppermute | solution.py:411
  37.7 17.0 %collective-permute-done.2.hw_ref = f32[192,128]{1,0:T(8,128)S(1)} collective-permute-done((f32[192,128]{1,0:T(8,128)S(1)}, f32[192,128]{1,0:T(8,128)S(1)}, u32[]{:S(2)}, u32[]{:S(2)}) %collective-permute-start.2) | collective-permute-done | bytes 98336 | tf_op jit(solution)/shard_map/ppermute | solution.py:411
  54.7 1.7 %collective-permute-done.3.he_ref = f32[192,128]{1,0:T(8,128)S(1)} collective-permute-done((f32[192,128]{1,0:T(8,128)S(1)}, f32[192,128]{1,0:T(8,128)S(1)}, u32[]{:S(2)}, u32[]{:S(2)}) %collective-permute-start.3) | collective-permute-done | bytes 98336 | tf_op jit(solution)/shard_map/ppermute | solution.py:411
  56.4 1.8 %stencil1.1.base_ref = f32[16,192,128]{2,1,0:T(8,128)S(1)} custom-call(f32[16,192,128]{2,1,0:T(8,128)S(1)} %get-tuple-element.42.lam_ref.planes_ref, s32[16,128]{1,0:T(8,128)S(1)} %copy-done.20, f32[16,128]{1,0:T(8,128)S(1)} %copy-done.21, f32[16,128]{1,0:T(8,128)S(1)} %copy-done.23, f32[192,128]{1,0:T(8,128)S(1)} %collective-permute-done.hn_ref, ...), custom_call_target="tpu_custom_call" | custom-call | tf_op jit(solution)/shard_map/stencil1/pallas_call | solution.py:60
  58.3 1.2 copy-done
  59.4 1.2 copy-done.2
  60.6 1.4 copy-done.1
  62.0 1.4 copy-done.3
  63.4 0.9 copy-done.12
  64.4 0.9 copy-done.14
  70.1 23.3 %closure.1 = (f32[16,192,128]{2,1,0:T(8,128)S(1)}, f32[16,192,128]{2,1,0:T(8,128)S(1)}, f32[1024,128]{1,0:T(8,128)S(1)}, f32[192,128]{1,0:T(8,128)S(1)}, f32[192...) custom-call(bf16[128,96,128]{2,1,0:T(8,128)(2,1)S(1)} %all-to-all-done.got_ref, ...), custom_call_target="tpu_custom_call" | custom-call | tf_op jit(solution)/shard_map/closure/pallas_call | solution.py:60
  93.4 1.2 copy-done.4
  94.6 1.1 copy-done.6
  99.1 7.8 %all-to-all-start.1 = ((f32[128,8,128]{2,1,0:T(8,128)}), f32[128,8,128]{2,1,0:T(8,128)S(1)}, u32[]{:S(2)}, u32[]{:S(2)}) async-start(f32[128,8,128]{2,1,0:T(8,128)} %bitcast.20), calls=%async_computation.1 | async-start | bytes 1048576 | tf_op jit(solution)/shard_map/all_to_all | solution.py:394
  106.9 1.3 collective-permute-start.4
  108.2 3.0 %collective-permute-start.5 = (f32[192,128]{1,0:T(8,128)}, f32[192,128]{1,0:T(8,128)S(1)}, u32[]{:S(2)}, u32[]{:S(2)}) collective-permute-start(f32[192,128]{1,0:T(8,128)} %copy-done.39), channel_id=1, source_target_pairs={{0,16},{16,32},{32,48},{48,64},{64,80},{80,96},{96,112},{1,17},{17... | collective-permute-start | bytes 294920 | tf_op jit(solution)/shard_map/ppermute | solution.py:411
  111.2 1.1 collective-permute-done.5.hs_ref
  112.3 7.9 %all-to-all-done.1 = f32[128,8,128]{2,1,0:T(8,128)S(1)} async-done(((f32[128,8,128]{2,1,0:T(8,128)}), f32[128,8,128]{2,1,0:T(8,128)S(1)}, u32[]{:S(2)}, u32[]{:S(2)}) %all-to-all-start.1) | async-done | bytes 524320 | tf_op jit(solution)/shard_map/all_to_all | solution.py:394
  121.2 4.9 %all-to-all-start.2 = ((f32[128,8,128]{2,1,0:T(8,128)}), f32[128,8,128]{2,1,0:T(8,128)S(1)}, u32[]{:S(2)}, u32[]{:S(2)}) async-start(f32[128,8,128]{2,1,0:T(8,128)} %bitcast.10), calls=%async_computation.2 | async-start | bytes 1048576 | tf_op jit(solution)/shard_map/all_to_all | solution.py:401
  126.0 4.4 %collective-permute-start.6 = (f32[192,128]{1,0:T(8,128)S(1)}, f32[192,128]{1,0:T(8,128)S(1)}, u32[]{:S(2)}, u32[]{:S(2)}) collective-permute-start(f32[192,128]{1,0:T(8,128)S(1)} %copy-done.38), channel_id=1, source_target_pairs={{1,0},{2,1},{3,2},{4,3},{5,4},{6,5},{7,6},{8,7},{9,8},{10,9},{11,1... | collective-permute-start | bytes 294920 | tf_op jit(solution)/shard_map/ppermute | solution.py:411
  130.4 1.9 %collective-permute-start.7 = (f32[192,128]{1,0:T(8,128)S(1)}, f32[192,128]{1,0:T(8,128)S(1)}, u32[]{:S(2)}, u32[]{:S(2)}) collective-permute-start(f32[192,128]{1,0:T(8,128)S(1)} %copy-done.36), channel_id=1, source_target_pairs={{0,1},{1,2},{2,3},{3,4},{4,5},{5,6},{6,7},{7,8},{8,9},{9,10},{10,1... | collective-permute-start | bytes 294920 | tf_op jit(solution)/shard_map/ppermute | solution.py:411
  132.4 3.2 %collective-permute-done.6.hw_ref = f32[192,128]{1,0:T(8,128)S(1)} collective-permute-done((f32[192,128]{1,0:T(8,128)S(1)}, f32[192,128]{1,0:T(8,128)S(1)}, u32[]{:S(2)}, u32[]{:S(2)}) %collective-permute-start.6) | collective-permute-done | bytes 98336 | tf_op jit(solution)/shard_map/ppermute | solution.py:411
  135.6 3.5 %collective-permute-done.7.he_ref = f32[192,128]{1,0:T(8,128)S(1)} collective-permute-done((f32[192,128]{1,0:T(8,128)S(1)}, f32[192,128]{1,0:T(8,128)S(1)}, u32[]{:S(2)}, u32[]{:S(2)}) %collective-permute-start.7) | collective-permute-done | bytes 98336 | tf_op jit(solution)/shard_map/ppermute | solution.py:411
  139.1 1.4 copy-done.7
  140.5 3.4 %stencil0.1 = f32[2880,128]{1,0:T(8,128)} custom-call(f32[16,192,128]{2,1,0:T(8,128)S(1)} %copy-done.5, f32[16,192,128]{2,1,0:T(8,128)S(1)} %copy-done.7, s32[16,128]{1,0:T(8,128)S(1)} %copy-done.20, f32[16,128]{1,0:T(8,128)S(1)} %copy-done.21, f32[16,128]{1,0:T(8,128)S(1)} %copy-done.25, f32[192,128]{1,0:T(8,128)S(1)} %collective-permute-done.4.hn_ref, ...), custom_call_target="tpu_custom_call" | custom-call | tf_op jit(solution)/shard_map/stencil0/pallas_call | solution.py:60
  (80 shorter events, 17.2 us)
Async XLA Ops:
  6.8 10.3 %copy-start.20 = (s32[16,128]{1,0:T(8,128)S(1)}, s32[16,128]{1,0:T(8,128)}, u32[]{:S(2)}) copy-start(s32[16,128]{1,0:T(8,128)} %mask_ref.7) | copy-start | bytes 24580
  6.8 10.3 %copy-start.21 = (f32[16,128]{1,0:T(8,128)S(1)}, f32[16,128]{1,0:T(8,128)}, u32[]{:S(2)}) copy-start(f32[16,128]{1,0:T(8,128)} %fx_ref.7) | copy-start | bytes 24580
  6.8 10.3 %copy-start.22 = (f32[16,128]{1,0:T(8,128)S(1)}, f32[16,128]{1,0:T(8,128)}, u32[]{:S(2)}) copy-start(f32[16,128]{1,0:T(8,128)} %fy_ref.7) | copy-start | bytes 24580
  6.8 53.7 %all-to-all-start = ((bf16[128,96,128]{2,1,0:T(8,128)(2,1)}), bf16[128,96,128]{2,1,0:T(8,128)(2,1)S(1)}, u32[]{:S(2)}, u32[]{:S(2)}) async-start(bf16[128,96,128]{2,1,0:T(8,128)(2,1)} %pack.1), calls=%async_computation | async-start | bytes 6291456 | tf_op jit(solution)/shard_map/all_to_all | solution.py:431
  17.1 1.4 copy-start.8
  18.5 12.0 %copy-start.10 = (f32[256,256]{1,0:T(8,128)S(1)}, f32[256,256]{1,0:T(8,128)}, u32[]{:S(2)}) copy-start(f32[256,256]{1,0:T(8,128)} %w2_ref) | copy-start | bytes 786436
  18.5 12.0 %copy-start.17 = (f32[180,256]{1,0:T(8,128)S(1)}, f32[180,256]{1,0:T(8,128)}, u32[]{:S(2)}) copy-start(f32[180,256]{1,0:T(8,128)} %w1_ref.1) | copy-start | bytes 552964
  18.5 37.9 %copy-start.23 = (f32[16,128]{1,0:T(8,128)S(1)}, f32[16,128]{1,0:T(8,128)}, u32[]{:S(2)}) copy-start(f32[16,128]{1,0:T(8,128)} %fy_ref.7) | copy-start | bytes 24580
  19.6 18.1 %collective-permute-start = (f32[192,128]{1,0:T(8,128)S(1)}, f32[192,128]{1,0:T(8,128)S(1)}, u32[]{:S(2)}, u32[]{:S(2)}) collective-permute-start(f32[192,128]{1,0:T(8,128)S(1)} %get-tuple-element.43), channel_id=1, source_target_pairs={{16,0},{32,16},{48,32},{64,48},{80,64},{96,80},{112,96},{17,1},{33... | collective-permute-start | bytes 294920 | tf_op jit(solution)/shard_map/ppermute | solution.py:411
  20.9 16.8 %collective-permute-start.1 = (f32[192,128]{1,0:T(8,128)S(1)}, f32[192,128]{1,0:T(8,128)S(1)}, u32[]{:S(2)}, u32[]{:S(2)}) collective-permute-start(f32[192,128]{1,0:T(8,128)S(1)} %get-tuple-element.44), channel_id=1, source_target_pairs={{0,16},{16,32},{32,48},{48,64},{64,80},{80,96},{96,112},{1,17},{17... | collective-permute-start | bytes 294920 | tf_op jit(solution)/shard_map/ppermute | solution.py:411
  23.9 30.8 %collective-permute-start.2 = (f32[192,128]{1,0:T(8,128)S(1)}, f32[192,128]{1,0:T(8,128)S(1)}, u32[]{:S(2)}, u32[]{:S(2)}) collective-permute-start(f32[192,128]{1,0:T(8,128)S(1)} %get-tuple-element.45), channel_id=1, source_target_pairs={{1,0},{2,1},{3,2},{4,3},{5,4},{6,5},{7,6},{8,7},{9,8},{10,9},{11,1... | collective-permute-start | bytes 294920 | tf_op jit(solution)/shard_map/ppermute | solution.py:411
  28.4 28.0 %collective-permute-start.3 = (f32[192,128]{1,0:T(8,128)S(1)}, f32[192,128]{1,0:T(8,128)S(1)}, u32[]{:S(2)}, u32[]{:S(2)}) collective-permute-start(f32[192,128]{1,0:T(8,128)S(1)} %get-tuple-element.46), channel_id=1, source_target_pairs={{0,1},{1,2},{2,3},{3,4},{4,5},{5,6},{6,7},{7,8},{8,9},{9,10},{10,1... | collective-permute-start | bytes 294920 | tf_op jit(solution)/shard_map/ppermute | solution.py:411
  58.2 1.2 copy-start
  59.4 1.2 copy-start.2
  60.6 1.4 copy-start.1
  62.0 1.4 copy-start.3
  63.4 0.9 copy-start.12
  64.4 0.9 copy-start.14
  65.3 0.9 copy-start.16
  93.4 1.2 copy-start.4
  94.6 1.1 copy-start.6
  99.1 27.0 %copy-start.38 = (f32[192,128]{1,0:T(8,128)S(1)}, f32[192,128]{1,0:T(8,128)}, u32[]{:S(2)}) copy-start(f32[192,128]{1,0:T(8,128)} %copy-done.37) | copy-start | bytes 294916
  99.1 31.4 %copy-start.36 = (f32[192,128]{1,0:T(8,128)S(1)}, f32[192,128]{1,0:T(8,128)}, u32[]{:S(2)}) copy-start(f32[192,128]{1,0:T(8,128)} %copy-done.35) | copy-start | bytes 294916
  99.1 40.0 %copy-start.5 = (f32[16,192,128]{2,1,0:T(8,128)S(1)}, f32[16,192,128]{2,1,0:T(8,128)}, u32[]{:S(2)}) copy-start(f32[16,192,128]{2,1,0:T(8,128)} %copy-done.4) | copy-start | bytes 4718596
  99.1 40.0 %copy-start.25 = (f32[16,128]{1,0:T(8,128)S(1)}, f32[16,128]{1,0:T(8,128)}, u32[]{:S(2)}) copy-start(f32[16,128]{1,0:T(8,128)} %fy_ref.7) | copy-start | bytes 24580
  99.1 21.1 %all-to-all-start.1 = ((f32[128,8,128]{2,1,0:T(8,128)}), f32[128,8,128]{2,1,0:T(8,128)S(1)}, u32[]{:S(2)}, u32[]{:S(2)}) async-start(f32[128,8,128]{2,1,0:T(8,128)} %bitcast.20), calls=%async_computation.1 | async-start | bytes 1048576 | tf_op jit(solution)/shard_map/all_to_all | solution.py:394
  106.9 4.3 %collective-permute-start.4 = (f32[192,128]{1,0:T(8,128)}, f32[192,128]{1,0:T(8,128)S(1)}, u32[]{:S(2)}, u32[]{:S(2)}) collective-permute-start(f32[192,128]{1,0:T(8,128)} %copy-done.40), channel_id=1, source_target_pairs={{16,0},{32,16},{48,32},{64,48},{80,64},{96,80},{112,96},{17,1},{33... | collective-permute-start | bytes 294920 | tf_op jit(solution)/shard_map/ppermute | solution.py:411
  108.2 4.2 %collective-permute-start.5 = (f32[192,128]{1,0:T(8,128)}, f32[192,128]{1,0:T(8,128)S(1)}, u32[]{:S(2)}, u32[]{:S(2)}) collective-permute-start(f32[192,128]{1,0:T(8,128)} %copy-done.39), channel_id=1, source_target_pairs={{0,16},{16,32},{32,48},{48,64},{64,80},{80,96},{96,112},{1,17},{17... | collective-permute-start | bytes 294920 | tf_op jit(solution)/shard_map/ppermute | solution.py:411
  121.2 22.7 %all-to-all-start.2 = ((f32[128,8,128]{2,1,0:T(8,128)}), f32[128,8,128]{2,1,0:T(8,128)S(1)}, u32[]{:S(2)}, u32[]{:S(2)}) async-start(f32[128,8,128]{2,1,0:T(8,128)} %bitcast.10), calls=%async_computation.2 | async-start | bytes 1048576 | tf_op jit(solution)/shard_map/all_to_all | solution.py:401
  126.0 9.5 %collective-permute-start.6 = (f32[192,128]{1,0:T(8,128)S(1)}, f32[192,128]{1,0:T(8,128)S(1)}, u32[]{:S(2)}, u32[]{:S(2)}) collective-permute-start(f32[192,128]{1,0:T(8,128)S(1)} %copy-done.38), channel_id=1, source_target_pairs={{1,0},{2,1},{3,2},{4,3},{5,4},{6,5},{7,6},{8,7},{9,8},{10,9},{11,1... | collective-permute-start | bytes 294920 | tf_op jit(solution)/shard_map/ppermute | solution.py:411
  130.4 8.6 %collective-permute-start.7 = (f32[192,128]{1,0:T(8,128)S(1)}, f32[192,128]{1,0:T(8,128)S(1)}, u32[]{:S(2)}, u32[]{:S(2)}) collective-permute-start(f32[192,128]{1,0:T(8,128)S(1)} %copy-done.36), channel_id=1, source_target_pairs={{0,1},{1,2},{2,3},{3,4},{4,5},{5,6},{6,7},{7,8},{8,9},{9,10},{10,1... | collective-permute-start | bytes 294920 | tf_op jit(solution)/shard_map/ppermute | solution.py:411
  139.1 1.4 copy-start.7
  (20 other events, 14.1 us)

commit v5 on v4

--- a/solution.py
+++ b/solution.py
@@ -51,20 +51,28 @@
     return pltpu.CompilerParams(vmem_limit_bytes=mib * 2**20)
 
 
-def near_shape(*shape, dtype=F32):
+def near(*shape, dtype=F32):
     return pltpu.VMEM(shape, dtype)
 
 
-def call(kernel, name, out_shape, args, scratch=(), mib=4):
+def far(*shape, dtype=F32):
+    return pltpu.HBM(shape, dtype)
+
+
+def call(kernel, name, outs, args, copied=(), scratch=(), mib=4):
     args = [pltpu.with_memory_space_constraint(a, pltpu.VMEM) for a in args]
+    copied = [pltpu.with_memory_space_constraint(a, pltpu.HBM) for a in copied]
+    inside = pl.BlockSpec(memory_space=pltpu.VMEM)
+    anywhere = pl.BlockSpec(memory_space=pl.ANY)
     return pl.pallas_call(
         kernel,
-        out_shape=out_shape,
-        in_specs=[pl.BlockSpec(memory_space=pltpu.VMEM)] * len(args),
+        out_shape=tuple(out[0] if isinstance(out, list) else out for out in outs),
+        in_specs=[inside] * len(args) + [anywhere] * len(copied),
+        out_specs=tuple(anywhere if isinstance(out, list) else inside for out in outs),
         scratch_shapes=list(scratch),
         compiler_params=params(mib),
         name=name,
-    )(*args)
+    )(*args, *copied)
 
 
 def pack_kernel(counts_ref, stored_ref, out_ref, near, padded, rows_out, in_sems, out_sem):
@@ -169,11 +177,12 @@
     c3_ref[:NZ, :] = jnp.broadcast_to(b3_ref[...], (8, NZ)).T[:, :1]
 
 
+WEIGHTS = ((2 * HID, FEATS), (2 * HID, HID), (2 * PAD, HID), (HID, FEATS), (2 * HID, HID), (2 * FEATS, HID))
+
+
 def weights(*args):
-    shapes = ((2 * HID, FEATS), (2 * HID, HID), (2 * PAD, HID), (HID, FEATS), (2 * HID, HID), (2 * FEATS, HID))
-    outs = tuple(near_shape(*shape, dtype=BF) for shape in shapes) + (near_shape(HID, 1), near_shape(PAD, 1))
-    scratch = [pltpu.VMEM((FEATS, HID), F32), pltpu.VMEM((FEATS, HID), F32)]
-    return call(weights_kernel, "weights", outs, args, scratch)
+    outs = tuple(far(*shape, dtype=BF) for shape in WEIGHTS) + (far(HID, 1), far(PAD, 1))
+    return call(weights_kernel, "weights", outs, args, scratch=[near(FEATS, HID), near(FEATS, HID)])
 
 
 def edge_plane(x, plane, mask_row, fy_row, ew_ref, ee_ref):
@@ -193,75 +202,86 @@
     return plane * mask_row * (flat_mix - 0.5 * fx_row)
 
 
-def edges_kernel(raw_ref, mask_ref, fx_ref, fy_ref, planes_ref, en_ref, es_ref, ew_ref, ee_ref):
-    planes_ref[...] = jnp.zeros_like(planes_ref)
+def row(ref, x):
+    return ref[x : x + 1, :].astype(F32)
+
+
+def local_plane(x, lam_ref, mask_ref, fx_ref, fy_ref):
+    weighted = lam_ref[x] * row(mask_ref, x)
+    lane = lax.broadcasted_iota(jnp.int32, weighted.shape, 1)
+    fy = row(fy_ref, x)
+    west = pltpu.roll(weighted * (flat_mix + 0.5 * fy), CY - 1, 1)
+    east = pltpu.roll(weighted * (flat_mix - 0.5 * fy), 1, 1)
+    total = jnp.where(lane == CY - 1, 0.0, west) + jnp.where(lane == 0, 0.0, east) - weighted
+    if x < CX - 1:
+        total = total + north_edge(lam_ref[x + 1], row(mask_ref, x + 1), row(fx_ref, x + 1))
+    if x > 0:
+        total = total + south_edge(lam_ref[x - 1], row(mask_ref, x - 1), row(fx_ref, x - 1))
+    return total
+
+
+def halo_plane(x, hn_ref, hs_ref, hw_ref, he_ref):
+    lane = lax.broadcasted_iota(jnp.int32, hn_ref.shape, 1)
+    total = jnp.where(lane == CY - 1, pltpu.roll(hw_ref[...], CY - 1 - x, 1), 0.0)
+    east = he_ref[...] if x == 0 else pltpu.roll(he_ref[...], CY - x, 1)
+    total = total + jnp.where(lane == 0, east, 0.0)
+    if x == 0:
+        total = total + hs_ref[...]
+    if x == CX - 1:
+        total = total + hn_ref[...]
+    return total
+
+
+def put_edges(lam_ref, mask_ref, fx_ref, fy_ref, en_ref, es_ref, ew_ref, ee_ref):
     ew_ref[...] = jnp.zeros_like(ew_ref)
     ee_ref[...] = jnp.zeros_like(ee_ref)
     for x in range(CX):
+        edge_plane(x, lam_ref[x], row(mask_ref, x), row(fy_ref, x), ew_ref, ee_ref)
+    en_ref[...] = north_edge(lam_ref[0], row(mask_ref, 0), row(fx_ref, 0))
+    es_ref[...] = south_edge(lam_ref[CX - 1], row(mask_ref, CX - 1), row(fx_ref, CX - 1))
+
+
+def edges_kernel(raw_ref, mask_ref, fx_ref, fy_ref, planes_ref, base_ref, en_ref, es_ref, ew_ref, ee_ref):
+    planes_ref[...] = jnp.zeros_like(planes_ref)
+    for x in range(CX):
         for t in range(TRACERS):
             planes_ref[x, t * PAD : t * PAD + NZ, :] = raw_ref[pl.ds(t * NZ * CX + x, NZ, stride=CX), :]
-        mask_row = mask_ref[x : x + 1, :].astype(F32)
-        edge_plane(x, planes_ref[x], mask_row, fy_ref[x : x + 1, :], ew_ref, ee_ref)
-    en_ref[...] = north_edge(planes_ref[0], mask_ref[0:1, :].astype(F32), fx_ref[0:1, :])
-    es_ref[...] = south_edge(planes_ref[CX - 1], mask_ref[CX - 1 :, :].astype(F32), fx_ref[CX - 1 :, :])
-
-
-EDGE = near_shape(FEATS, CY)
-PLANE = near_shape(CX, FEATS, CY)
+    put_edges(planes_ref, mask_ref, fx_ref, fy_ref, en_ref, es_ref, ew_ref, ee_ref)
+    for x in range(CX):
+        base_ref[x] = planes_ref[x] + step_size * local_plane(x, planes_ref, mask_ref, fx_ref, fy_ref)
+
+
+EDGE = far(FEATS, CY)
+PLANE = (CX, FEATS, CY)
 
 
 def edges(*args):
-    return call(edges_kernel, "edges", (PLANE, EDGE, EDGE, EDGE, EDGE), args)
-
-
-def stencil_plane(x, lam_ref, mask_ref, fx_ref, fy_ref, hn_ref, hs_ref, hw_ref, he_ref):
-    def row(ref, at):
-        return ref[at : at + 1, :].astype(F32)
-
-    plane = lam_ref[x]
-    weighted = plane * row(mask_ref, x)
-    if x < CX - 1:
-        total = north_edge(lam_ref[x + 1], row(mask_ref, x + 1), row(fx_ref, x + 1))
-    else:
-        total = hn_ref[...]
-    if x > 0:
-        total = total + south_edge(lam_ref[x - 1], row(mask_ref, x - 1), row(fx_ref, x - 1))
-    else:
-        total = total + hs_ref[...]
-    lane = lax.broadcasted_iota(jnp.int32, plane.shape, 1)
-    fy = row(fy_ref, x)
-    west = pltpu.roll(weighted * (flat_mix + 0.5 * fy), CY - 1, 1)
-    total = total + jnp.where(lane == CY - 1, pltpu.roll(hw_ref[...], CY - 1 - x, 1), west)
-    east = pltpu.roll(weighted * (flat_mix - 0.5 * fy), 1, 1)
-    from_east = he_ref[...] if x == 0 else pltpu.roll(he_ref[...], CY - x, 1)
-    total = total + jnp.where(lane == 0, from_east, east)
-    return plane, total - weighted
-
-
-def first_kernel(lam_ref, mask_ref, fx_ref, fy_ref, hn_ref, hs_ref, hw_ref, he_ref, out_ref):
+    return call(edges_kernel, "edges", (far(*PLANE), far(*PLANE), EDGE, EDGE, EDGE, EDGE), args)
+
+
+def last_kernel(mask_ref, fx_ref, fy_ref, hn_ref, hs_ref, hw_ref, he_ref, lam_far, down_far, out_ref, lam, down, sems):
+    copies = [
+        pltpu.make_async_copy(lam_far, lam, sems.at[0]),
+        pltpu.make_async_copy(down_far, down, sems.at[1]),
+    ]
+    for copy in copies:
+        copy.start()
+    for copy in copies:
+        copy.wait()
     for x in range(CX):
-        plane, total = stencil_plane(x, lam_ref, mask_ref, fx_ref, fy_ref, hn_ref, hs_ref, hw_ref, he_ref)
-        out_ref[x] = plane + step_size * total
-
-
-def first_stencil(lam, mask, fx, fy, halos):
-    return call(first_kernel, "stencil1", PLANE, (lam, mask, fx, fy, *halos))
-
-
-def last_kernel(lam_ref, down_ref, mask_ref, fx_ref, fy_ref, hn_ref, hs_ref, hw_ref, he_ref, out_ref):
-    for x in range(CX):
-        plane, total = stencil_plane(x, lam_ref, mask_ref, fx_ref, fy_ref, hn_ref, hs_ref, hw_ref, he_ref)
-        value = plane + step_size * (total + down_ref[x])
+        total = local_plane(x, lam, mask_ref, fx_ref, fy_ref) + halo_plane(x, hn_ref, hs_ref, hw_ref, he_ref)
+        value = lam[x] + step_size * (total + down[x])
         for t in range(TRACERS):
             out_ref[pl.ds(t * NZ * CX + x, NZ, stride=CX), :] = value[t * PAD : t * PAD + NZ]
 
 
-def last_stencil(lam, down, mask, fx, fy, halos):
-    out = jax.ShapeDtypeStruct((TRACERS * NZ * CX, CY), F32)
-    return call(last_kernel, "stencil0", out, (lam, down, mask, fx, fy, *halos))
-
-
-def closure_step(first, got_ref, owner_ref, mask_ref, lam_ref, weight_refs, base_ref, out_ref, rows_ref, total):
+def last_stencil(lam, down, *args):
+    scratch = [near(*PLANE), near(*PLANE), pltpu.SemaphoreType.DMA((2,))]
+    (out,) = call(last_kernel, "stencil0", (far(TRACERS * NZ * CX, CY),), args, (lam, down), scratch, mib=8)
+    return out
+
+
+def closure_step(first, got_ref, owner_ref, mask_ref, lam_ref, weight_refs, out_ref, rows_ref, total, wait):
     f1_ref, f2_ref, f3_ref, r3_ref, r2_ref, r1_ref, b2_ref, b3_ref = weight_refs
     for half in range(2):
         for g in range(DEV // 8):
@@ -290,6 +310,7 @@
     row = lax.broadcasted_iota(jnp.int32, (FEATS, COLS), 0)
     inputs = jnp.where(row == NZ, 1.0, picked).astype(BF)
 
+    wait("weights")
     both = dot(f1_ref[...], inputs)
     h1 = jnp.tanh(both[:HID] + both[HID:])
     h1_high, h1_low = split(h1)
@@ -301,6 +322,7 @@
     inner = lax.broadcasted_iota(jnp.int32, (PAD, COLS), 0) < NZ - 1
     kappa = jnp.where(inner, kappa_top * sig, 0.0)
 
+    wait("lam")
     mask_row = wide(mask_ref).astype(F32)
     slope = jnp.zeros((PAD, COLS), F32)
     direct = []
@@ -322,6 +344,13 @@
     both = dot(r1_ref[...], d1_high)
     d0 = both[:FEATS] + both[FEATS:] + dot(r1_ref[:FEATS], d1_low)
 
+    for i in range(CX):
+        part = slice(i * CY, (i + 1) * CY)
+        for t in range(TRACERS):
+            lo, hi = t * PAD, (t + 1) * PAD
+            out_ref[i, lo:hi, :] = d0[lo:hi, part] + direct[t][:, part]
+    wait("out")
+
     ones = jnp.ones((16, COLS), BF)
     total[:FEATS, :] += dot_nt(inputs, d1_high) + dot_nt(inputs, d1_low)
     both = dot_nt(jnp.concatenate([h1_high, h1_low, ones], axis=0), d2_high)
@@ -334,39 +363,80 @@
     both = dot_nt(ones, d3_both)
     total[NZ + 2 : NZ + 3, :PAD] += both[:1, :PAD] + both[:1, PAD:]
 
-    for i in range(CX):
-        part = slice(i * CY, (i + 1) * CY)
-        for t in range(TRACERS):
-            lo, hi = t * PAD, (t + 1) * PAD
-            down = d0[lo:hi, part] + direct[t][:, part]
-            if base_ref is not None:
-                out_ref[i, lo:hi, :] = base_ref[i, lo:hi, :] + step_size * down
-            else:
-                out_ref[i, lo:hi, :] = down
-
-
-def closure_kernel(got_ref, owner_ref, mask_ref, fx_ref, fy_ref, planes_ref, base_ref, *refs):
-    weight_refs, refs = refs[:8], refs[8:]
-    lam_ref, down_ref, grads_ref, en_ref, es_ref, ew_ref, ee_ref, late_ref, early_ref, total = refs
+
+def bring(refs, copies, sems):
+    started = {}
+    for i, (name, source, target) in enumerate(copies):
+        started.setdefault(name, []).append(pltpu.make_async_copy(source, target, sems.at[i]))
+        started[name][-1].start()
+
+    def wait(name):
+        for copy in started.pop(name, ()):
+            copy.wait()
+
+    return wait
+
+
+def late_kernel(got_ref, owner_ref, mask_ref, *refs):
+    sources, (out_ref, total), refs = refs[:10], refs[10:12], refs[12:]
+    targets, (rows_ref, down, sems) = refs[:10], refs[10:]
+    names = ("weights",) * 8 + ("lam", "base")
+    wait = bring(refs, zip(names, sources, targets), sems)
+    planes, base = targets[8:]
     total[...] = jnp.zeros_like(total)
-    ew_ref[...] = jnp.zeros_like(ew_ref)
-    ee_ref[...] = jnp.zeros_like(ee_ref)
-    step = functools.partial(closure_step, got_ref=got_ref, owner_ref=owner_ref, mask_ref=mask_ref, total=total)
-    step(BLOCK, lam_ref=planes_ref, weight_refs=weight_refs, base_ref=base_ref, out_ref=lam_ref, rows_ref=late_ref)
+
+    def then(name):
+        wait(name)
+        if name == "out":
+            wait("base")
+            for x in range(CX):
+                out_ref[x] = base[x] + step_size * down[x]
+
+    closure_step(BLOCK, got_ref, owner_ref, mask_ref, planes, targets[:8], down, rows_ref, total, then)
+
+
+def early_kernel(got_ref, owner_ref, mask_ref, fx_ref, fy_ref, part_ref, before_ref, *refs):
+    halos, sources, refs = refs[:4], refs[4:12], refs[12:]
+    (lam_far, down_far, grads_ref), sides, refs = refs[:3], refs[3:7], refs[7:]
+    targets, (rows_ref, lam, down, total, sems, out_sems) = refs[:8], refs[8:]
+    wait = bring(refs, zip(("weights",) * 8, sources, targets), sems)
     for x in range(CX):
-        edge_plane(x, lam_ref[x], mask_ref[x : x + 1, :].astype(F32), fy_ref[x : x + 1, :], ew_ref, ee_ref)
-    en_ref[...] = north_edge(lam_ref[0], mask_ref[0:1, :].astype(F32), fx_ref[0:1, :])
-    es_ref[...] = south_edge(lam_ref[CX - 1], mask_ref[CX - 1 :, :].astype(F32), fx_ref[CX - 1 :, :])
-    step(0, lam_ref=lam_ref, weight_refs=weight_refs, base_ref=None, out_ref=down_ref, rows_ref=early_ref)
+        lam[x] = part_ref[x] + step_size * halo_plane(x, *halos)
+    lam_copy = pltpu.make_async_copy(lam, lam_far, out_sems.at[0])
+    lam_copy.start()
+    down_copy = pltpu.make_async_copy(down, down_far, out_sems.at[1])
+    put_edges(lam, mask_ref, fx_ref, fy_ref, *sides)
+    total[...] = before_ref[...]
+
+    def then(name):
+        wait(name)
+        if name == "out":
+            down_copy.start()
+
+    closure_step(0, got_ref, owner_ref, mask_ref, lam, targets, down, rows_ref, total, then)
     grads_ref[: 2 * HID, :] = total[:, :128]
     grads_ref[2 * HID :, :] = total[:, 128:]
-
-
-def closure(*args):
-    outs = (PLANE, PLANE, near_shape(4 * HID, 128), EDGE, EDGE, EDGE, EDGE)
-    rows = pltpu.VMEM((FEATS, STORE), BF)
-    scratch = [rows, rows, pltpu.VMEM((2 * HID, HID), F32)]
-    return call(closure_kernel, "closure", outs, args, scratch, CLOSURE_MIB)
+    lam_copy.wait()
+    down_copy.wait()
+
+
+WEIGHT_SCRATCH = [near(*shape, dtype=BF) for shape in WEIGHTS] + [near(HID, 1), near(PAD, 1)]
+ROWS = near(FEATS, STORE, dtype=BF)
+TOTAL = near(2 * HID, HID)
+
+
+def late_closure(got, owners, mask, split_weights, planes, base):
+    scratch = WEIGHT_SCRATCH + [near(*PLANE), near(*PLANE), ROWS, near(*PLANE), pltpu.SemaphoreType.DMA((10,))]
+    copied = (*split_weights, planes, base)
+    return call(late_kernel, "closure1", (near(*PLANE), TOTAL), (got, owners, mask), copied, scratch, CLOSURE_MIB)
+
+
+def early_closure(got, owners, mask, fx, fy, part, before, halos, split_weights):
+    outs = ([far(*PLANE)], [far(*PLANE)], far(4 * HID, 128), EDGE, EDGE, EDGE, EDGE)
+    scratch = WEIGHT_SCRATCH + [ROWS, near(*PLANE), near(*PLANE), TOTAL]
+    scratch += [pltpu.SemaphoreType.DMA((8,)), pltpu.SemaphoreType.DMA((2,))]
+    args = (got, owners, mask, fx, fy, part, before, *halos)
+    return call(early_kernel, "closure0", outs, args, split_weights, scratch, CLOSURE_MIB)
 
 
 def sum_kernel(parts_ref, out_ref):
@@ -393,7 +463,7 @@
 def reduce_params(packed, tied):
     parts = lax.all_to_all(packed, ("gx", "gy"), split_axis=0, concat_axis=0, tiled=True)
     parts, _ = lax.optimization_barrier((parts, tied))
-    spread = call(sum_kernel, "sum", near_shape(*packed.shape), (parts,))
+    (spread,) = call(sum_kernel, "sum", (far(*packed.shape),), (parts,))
     return spread
 
 
@@ -401,7 +471,7 @@
     sums = lax.all_to_all(spread, ("gx", "gy"), split_axis=0, concat_axis=0, tiled=True)
     shapes = ((TRACERS * NZ, HID), (1, HID), (HID, HID), (1, HID), (NZ, HID), (1, NZ))
     scale = step_size / float(np.sqrt(count))
-    outs = tuple(jax.ShapeDtypeStruct(shape, F32) for shape in shapes)
+    outs = tuple(far(*shape) for shape in shapes)
     return call(functools.partial(unpack_kernel, scale), "unpack", outs, (sums,))
 
 
@@ -432,19 +502,19 @@
     split_weights = weights(
         weight_in, bias_in[None, :], weight_mid, bias_mid[None, :], weight_out.T, bias_out[None, :]
     )
-    planes, north, south, west, east = edges(
+    planes, base, north, south, west, east = edges(
         costate.reshape(TRACERS * NZ * CX, CY), land_mask, flow_x, flow_y
     )
     halos = exchange("gx", north, south) + exchange("gy", west, east)
-    base = first_stencil(planes, land_mask, flow_x, flow_y, halos)
-    lam, down, packed, north, south, west, east = closure(
-        got, owners, land_mask, flow_x, flow_y, planes, base, *split_weights
+    part, grads = late_closure(got, owners, land_mask, split_weights, planes, base)
+    lam, down, packed, north, south, west, east = early_closure(
+        got, owners, land_mask, flow_x, flow_y, part, grads, halos, split_weights
     )
     halos_x = exchange("gx", north, south)
     spread = reduce_params(packed, halos_x)
     west, east, spread = lax.optimization_barrier((west, east, spread))
     halos_y = exchange("gy", west, east)
-    adjoint = last_stencil(lam, down, land_mask, flow_x, flow_y, halos_x + halos_y)
+    adjoint = last_stencil(lam, down, land_mask, flow_x, flow_y, *halos_x, *halos_y)
     count = CX * CY * lax.axis_size("gx") * lax.axis_size("gy")
     g1, gb1, g2, gb2, g3, gb3 = finish_params(spread, count)
     return (adjoint.reshape(costate.shape), g1, gb1[0], g2, gb2[0], g3.T, gb3[0])

time: 146 us -> 127 us (0.87)
  local copies, waits for them, and re-layouts: 27.2 us -> 4.96 us
  Pallas kernels: 37.8 us -> 41.1 us
  waiting for transfers between devices: 34.4 us -> 36.5 us
  starting transfers between devices: 44.4 us -> 42.5 us
    unnamed x82 -> x30, local copies, waits for them, and re-layouts: 27.2 us -> 4.96 us
    all_to_all x1, waiting for transfers between devices: 0.01 us -> 20.8 us  [on_device(): lax.all_to_all(payload, ('gx', 'gy'), split_axis=0, concat_axis=0, tiled=...]
    ppermute x8, waiting for transfers between devices: 26.6 us -> 7.83 us  [exchange(): return (lax.ppermute(before, axis, down), lax.ppermute(after, axis, up))]
    pallas_call x7, Pallas kernels: 31.6 us -> 35 us  [call(): pl.pallas_call(kernel, out_shape=tuple((out[0] if isinstance(out, list) e...]
    all_to_all x1, starting transfers between devices: 7.77 us -> 5.96 us  [reduce_params(): lax.all_to_all(packed, ('gx', 'gy'), split_axis=0, concat_axis=0, tiled=T...]
  transfers between devices with their start and end apart: 11 -> 11, of which waited for: 6 -> 5; matrix products, arithmetic and copies ran while one was open for 0% -> 0% of each run, Pallas kernels for 5% -> 17%
where the time goes in v5:
time: 127 us; the launch traced here: 126 us
  starting transfers between devices  42.5 us (33%)
  Pallas kernels  41.1 us (32%)
  waiting for transfers between devices  36.5 us (29%)
  local copies, waits for them, and re-layouts  4.96 us (4%)
    pallas_call x7, Pallas kernels, call(): pl.pallas_call(kernel, out_shape=tuple((out[0] if isinstance(out, list) e...  35 us
    ppermute x8, starting transfers between devices, exchange(): return (lax.ppermute(before, axis, down), lax.ppermute(after, axis, up))  21.5 us
    all_to_all x1, waiting for transfers between devices, on_device(): lax.all_to_all(payload, ('gx', 'gy'), split_axis=0, concat_axis=0, tiled=...  20.8 us
    all_to_all x1, starting transfers between devices, on_device(): lax.all_to_all(payload, ('gx', 'gy'), split_axis=0, concat_axis=0, tiled=...  10.2 us
    all_to_all x1, waiting for transfers between devices, reduce_params(): lax.all_to_all(packed, ('gx', 'gy'), split_axis=0, concat_axis=0, tiled=T...  7.89 us
    ppermute x8, waiting for transfers between devices, exchange(): return (lax.ppermute(before, axis, down), lax.ppermute(after, axis, up))  7.83 us
    pallas_call x1, Pallas kernels, pack(): pl.pallas_call(pack_kernel, out_shape=pltpu.HBM((DEV, 2 * BLOCK, 128), BF...  6.16 us
    all_to_all x1, starting transfers between devices, reduce_params(): lax.all_to_all(packed, ('gx', 'gy'), split_axis=0, concat_axis=0, tiled=T...  5.96 us
  transfers between devices with their start and end apart: 11, of which 5 were waited for; matrix products, arithmetic and copies ran while one was open for 0% of the time, Pallas kernels for 17%

profile of v5, /device:TPU:32, one launch (start us, length us, event | category | flops | bytes accessed | tf_op | source)
XLA Modules:
  0.0 126.0 jit_solution(18288449460567096664)
XLA Ops:
  0.6 6.2 %pack.1 = bf16[128,96,128]{2,1,0:T(8,128)(2,1)} custom-call(s32[1,128]{1,0:T(1,128)} %counts_ref.1, bf16[360,4096]{1,0:T(8,128)(2,1)} %bitcast.24), custom_call_target="tpu_custom_call" | custom-call | tf_op jit(solution)/shard_map/pack/pallas_call | solution.py:129
  6.8 0.0 copy-start.4
  6.8 0.0 copy-start.5
  6.8 10.2 %all-to-all-start = ((bf16[128,96,128]{2,1,0:T(8,128)(2,1)}), bf16[128,96,128]{2,1,0:T(8,128)(2,1)S(1)}, u32[]{:S(2)}, u32[]{:S(2)}) async-start(bf16[128,96,128]{2,1,0:T(8,128)(2,1)} %pack.1), calls=%async_computation | async-start | bytes 6291456 | tf_op jit(solution)/shard_map/all_to_all | solution.py:501
  17.1 1.4 %copy-done = f32[3,60,16,128]{3,2,1,0:T(8,128)S(1)} copy-done((f32[3,60,16,128]{3,2,1,0:T(8,128)S(1)}, f32[3,60,16,128]{3,2,1,0:T(8,128)}, u32[]{:S(2)}) %copy-start) | copy-done | bytes 1474584
  18.5 3.1 %edges.1 = (f32[16,192,128]{2,1,0:T(8,128)}, f32[16,192,128]{2,1,0:T(8,128)}, f32[192,128]{1,0:T(8,128)}, f32[192,128]{1,0:T(8,128)}, f32[192,128]{1,0:T(8,128)}, /*index=5*/f32[192,128]{1,0:T(8,128)}) custom-call(f32[2880,128]{1,0:T(8,128)S(1)} %bitcast.19, s32[16,128]{1,0:T(8,128)S(1)} %copy-done.3, f32[16,128]{1,0:T(8,128)S(1)} %copy-done.4, ...), custom_call_target="tpu_custom_call" | custom-call | tf_op jit(solution)/shard_map/edges/pallas_call | solution.py:67
  21.6 1.3 %collective-permute-start = (f32[192,128]{1,0:T(8,128)}, f32[192,128]{1,0:T(8,128)S(1)}, u32[]{:S(2)}, u32[]{:S(2)}) collective-permute-start(f32[192,128]{1,0:T(8,128)} %get-tuple-element.58), channel_id=1, source_target_pairs={{16,0},{32,16},{48,32},{64,48},{80,64},{96,80},{112,96},{17,1},{33... | collective-permute-start | bytes 294920 | tf_op jit(solution)/shard_map/ppermute | solution.py:481
  22.9 3.0 %collective-permute-start.1 = (f32[192,128]{1,0:T(8,128)}, f32[192,128]{1,0:T(8,128)S(1)}, u32[]{:S(2)}, u32[]{:S(2)}) collective-permute-start(f32[192,128]{1,0:T(8,128)} %get-tuple-element.59), channel_id=1, source_target_pairs={{0,16},{16,32},{32,48},{48,64},{64,80},{80,96},{96,112},{1,17},{17... | collective-permute-start | bytes 294920 | tf_op jit(solution)/shard_map/ppermute | solution.py:481
  25.9 4.5 %collective-permute-start.2 = (f32[192,128]{1,0:T(8,128)}, f32[192,128]{1,0:T(8,128)S(1)}, u32[]{:S(2)}, u32[]{:S(2)}) collective-permute-start(f32[192,128]{1,0:T(8,128)} %get-tuple-element.60), channel_id=1, source_target_pairs={{1,0},{2,1},{3,2},{4,3},{5,4},{6,5},{7,6},{8,7},{9,8},{10,9},{11,1... | collective-permute-start | bytes 294920 | tf_op jit(solution)/shard_map/ppermute | solution.py:481
  30.4 2.1 %collective-permute-start.3 = (f32[192,128]{1,0:T(8,128)}, f32[192,128]{1,0:T(8,128)S(1)}, u32[]{:S(2)}, u32[]{:S(2)}) collective-permute-start(f32[192,128]{1,0:T(8,128)} %get-tuple-element.61), channel_id=1, source_target_pairs={{0,1},{1,2},{2,3},{3,4},{4,5},{5,6},{6,7},{7,8},{8,9},{9,10},{10,1... | collective-permute-start | bytes 294920 | tf_op jit(solution)/shard_map/ppermute | solution.py:481
  32.5 0.8 copy-done.8
  33.4 0.7 copy-done.10
  34.0 0.7 copy-done.11
  34.7 0.7 copy-done.12
  35.4 1.2 weights.1
  36.6 20.8 %all-to-all-done.got_ref = bf16[128,96,128]{2,1,0:T(8,128)(2,1)S(1)} async-done(((bf16[128,96,128]{2,1,0:T(8,128)(2,1)}), bf16[128,96,128]{2,1,0:T(8,128)(2,1)S(1)}, u32[]{:S(2)}, u32[]{:S(2)}) %all-to-all-start) | async-done | bytes 3145760 | tf_op jit(solution)/shard_map/all_to_all | solution.py:501
  57.3 0.7 copy-done.9
  58.0 11.8 %closure1.1 = (f32[16,192,128]{2,1,0:T(8,128)S(1)}, f32[512,256]{1,0:T(8,128)S(1)}) custom-call(bf16[128,96,128]{2,1,0:T(8,128)(2,1)S(1)} %all-to-all-done.got_ref, s32[16,128]{1,0:T(8,128)S(1)} %copy-done.9, s32[16,128]{1,0:T(8,128)S(1)} %copy-done.3, bf16[512,192]{1,0:T(8,128)(2,1)} %get-tuple-element.45.refs_0_.refs_4_, ...), custom_call_target="tpu_custom_call" | custom-call | tf_op jit(solution)/shard_map/closure1/pallas_call | solution.py:67
  69.9 11.8 %closure0.1 = (f32[16,192,128]{2,1,0:T(8,128)}, f32[16,192,128]{2,1,0:T(8,128)}, f32[1024,128]{1,0:T(8,128)}, f32[192,128]{1,0:T(8,128)}, f32[192,128]{1,0:T(8,1...) custom-call(bf16[128,96,128]{2,1,0:T(8,128)(2,1)S(1)} %all-to-all-done.got_ref, s32[16,128]{1,0:T(8,128)S(1)} %copy-done.9, ...), custom_call_target="tpu_custom_call" | custom-call | tf_op jit(solution)/shard_map/closure0/pallas_call | solution.py:67
  81.7 6.0 %all-to-all-start.1 = ((f32[128,8,128]{2,1,0:T(8,128)}), f32[128,8,128]{2,1,0:T(8,128)S(1)}, u32[]{:S(2)}, u32[]{:S(2)}) async-start(f32[128,8,128]{2,1,0:T(8,128)} %bitcast.27), calls=%async_computation.1 | async-start | bytes 1048576 | tf_op jit(solution)/shard_map/all_to_all | solution.py:464
  87.7 1.3 %collective-permute-start.4 = (f32[192,128]{1,0:T(8,128)}, f32[192,128]{1,0:T(8,128)S(1)}, u32[]{:S(2)}, u32[]{:S(2)}) collective-permute-start(f32[192,128]{1,0:T(8,128)} %get-tuple-element.62), channel_id=1, source_target_pairs={{16,0},{32,16},{48,32},{64,48},{80,64},{96,80},{112,96},{17,1},{33... | collective-permute-start | bytes 294920 | tf_op jit(solution)/shard_map/ppermute | solution.py:481
  89.0 3.0 %collective-permute-start.5 = (f32[192,128]{1,0:T(8,128)}, f32[192,128]{1,0:T(8,128)S(1)}, u32[]{:S(2)}, u32[]{:S(2)}) collective-permute-start(f32[192,128]{1,0:T(8,128)} %get-tuple-element.63), channel_id=1, source_target_pairs={{0,16},{16,32},{32,48},{48,64},{64,80},{80,96},{96,112},{1,17},{17... | collective-permute-start | bytes 294920 | tf_op jit(solution)/shard_map/ppermute | solution.py:481
  92.1 1.1 collective-permute-done.5.hs_ref
  93.2 7.9 %all-to-all-done.1 = f32[128,8,128]{2,1,0:T(8,128)S(1)} async-done(((f32[128,8,128]{2,1,0:T(8,128)}), f32[128,8,128]{2,1,0:T(8,128)S(1)}, u32[]{:S(2)}, u32[]{:S(2)}) %all-to-all-start.1) | async-done | bytes 524320 | tf_op jit(solution)/shard_map/all_to_all | solution.py:464
  101.1 1.0 sum.1
  102.0 4.9 %all-to-all-start.2 = ((f32[128,8,128]{2,1,0:T(8,128)}), f32[128,8,128]{2,1,0:T(8,128)S(1)}, u32[]{:S(2)}, u32[]{:S(2)}) async-start(f32[128,8,128]{2,1,0:T(8,128)} %bitcast.25), calls=%async_computation.2 | async-start | bytes 1048576 | tf_op jit(solution)/shard_map/all_to_all | solution.py:471
  106.9 4.4 %collective-permute-start.6 = (f32[192,128]{1,0:T(8,128)S(1)}, f32[192,128]{1,0:T(8,128)S(1)}, u32[]{:S(2)}, u32[]{:S(2)}) collective-permute-start(f32[192,128]{1,0:T(8,128)S(1)} %copy-done.14), channel_id=1, source_target_pairs={{1,0},{2,1},{3,2},{4,3},{5,4},{6,5},{7,6},{8,7},{9,8},{10,9},{11,1... | collective-permute-start | bytes 294920 | tf_op jit(solution)/shard_map/ppermute | solution.py:481
  111.3 1.9 %collective-permute-start.7 = (f32[192,128]{1,0:T(8,128)S(1)}, f32[192,128]{1,0:T(8,128)S(1)}, u32[]{:S(2)}, u32[]{:S(2)}) collective-permute-start(f32[192,128]{1,0:T(8,128)S(1)} %copy-done.13), channel_id=1, source_target_pairs={{0,1},{1,2},{2,3},{3,4},{4,5},{5,6},{6,7},{7,8},{8,9},{9,10},{10,1... | collective-permute-start | bytes 294920 | tf_op jit(solution)/shard_map/ppermute | solution.py:481
  113.2 3.2 %collective-permute-done.6.hw_ref = f32[192,128]{1,0:T(8,128)S(1)} collective-permute-done((f32[192,128]{1,0:T(8,128)S(1)}, f32[192,128]{1,0:T(8,128)S(1)}, u32[]{:S(2)}, u32[]{:S(2)}) %collective-permute-start.6) | collective-permute-done | bytes 98336 | tf_op jit(solution)/shard_map/ppermute | solution.py:481
  116.4 3.5 %collective-permute-done.7.he_ref = f32[192,128]{1,0:T(8,128)S(1)} collective-permute-done((f32[192,128]{1,0:T(8,128)S(1)}, f32[192,128]{1,0:T(8,128)S(1)}, u32[]{:S(2)}, u32[]{:S(2)}) %collective-permute-start.7) | collective-permute-done | bytes 98336 | tf_op jit(solution)/shard_map/ppermute | solution.py:481
  119.9 5.3 %stencil0.1 = f32[2880,128]{1,0:T(8,128)} custom-call(s32[16,128]{1,0:T(8,128)S(1)} %copy-done.3, f32[16,128]{1,0:T(8,128)S(1)} %copy-done.4, f32[16,128]{1,0:T(8,128)S(1)} %copy-done.7, f32[192,128]{1,0:T(8,128)S(1)} %collective-permute-done.4.hn_ref, f32[192,128]{1,0:T(8,128)S(1)} %collective-permute-done.5.hs_ref, ...), custom_call_target="tpu_custom_call" | custom-call | tf_op jit(solution)/shard_map/stencil0/pallas_call | solution.py:67
  125.2 0.8 unpack.1
  (28 shorter events, 0.1 us)
Async XLA Ops:
  6.8 10.3 %copy-start.3 = (s32[16,128]{1,0:T(8,128)S(1)}, s32[16,128]{1,0:T(8,128)}, u32[]{:S(2)}) copy-start(s32[16,128]{1,0:T(8,128)} %mask_ref.7) | copy-start | bytes 24580
  6.8 10.3 %copy-start.4 = (f32[16,128]{1,0:T(8,128)S(1)}, f32[16,128]{1,0:T(8,128)}, u32[]{:S(2)}) copy-start(f32[16,128]{1,0:T(8,128)} %fx_ref.5) | copy-start | bytes 24580
  6.8 10.3 %copy-start.5 = (f32[16,128]{1,0:T(8,128)S(1)}, f32[16,128]{1,0:T(8,128)}, u32[]{:S(2)}) copy-start(f32[16,128]{1,0:T(8,128)} %fy_ref.5) | copy-start | bytes 24580
  6.8 50.5 %all-to-all-start = ((bf16[128,96,128]{2,1,0:T(8,128)(2,1)}), bf16[128,96,128]{2,1,0:T(8,128)(2,1)S(1)}, u32[]{:S(2)}, u32[]{:S(2)}) async-start(bf16[128,96,128]{2,1,0:T(8,128)(2,1)} %pack.1), calls=%async_computation | async-start | bytes 6291456 | tf_op jit(solution)/shard_map/all_to_all | solution.py:501
  17.1 1.4 %copy-start = (f32[3,60,16,128]{3,2,1,0:T(8,128)S(1)}, f32[3,60,16,128]{3,2,1,0:T(8,128)}, u32[]{:S(2)}) copy-start(f32[3,60,16,128]{3,2,1,0:T(8,128)} %param.19) | copy-start | bytes 4423684
  18.5 14.0 %copy-start.1 = (f32[256,256]{1,0:T(8,128)S(1)}, f32[256,256]{1,0:T(8,128)}, u32[]{:S(2)}) copy-start(f32[256,256]{1,0:T(8,128)} %w2_ref) | copy-start | bytes 786436
  18.5 14.0 %copy-start.2 = (f32[180,256]{1,0:T(8,128)S(1)}, f32[180,256]{1,0:T(8,128)}, u32[]{:S(2)}) copy-start(f32[180,256]{1,0:T(8,128)} %w1_ref.1) | copy-start | bytes 552964
  21.6 48.3 %collective-permute-start = (f32[192,128]{1,0:T(8,128)}, f32[192,128]{1,0:T(8,128)S(1)}, u32[]{:S(2)}, u32[]{:S(2)}) collective-permute-start(f32[192,128]{1,0:T(8,128)} %get-tuple-element.58), channel_id=1, source_target_pairs={{16,0},{32,16},{48,32},{64,48},{80,64},{96,80},{112,96},{17,1},{33... | collective-permute-start | bytes 294920 | tf_op jit(solution)/shard_map/ppermute | solution.py:481
  22.9 47.0 %collective-permute-start.1 = (f32[192,128]{1,0:T(8,128)}, f32[192,128]{1,0:T(8,128)S(1)}, u32[]{:S(2)}, u32[]{:S(2)}) collective-permute-start(f32[192,128]{1,0:T(8,128)} %get-tuple-element.59), channel_id=1, source_target_pairs={{0,16},{16,32},{32,48},{48,64},{64,80},{80,96},{96,112},{1,17},{17... | collective-permute-start | bytes 294920 | tf_op jit(solution)/shard_map/ppermute | solution.py:481
  25.9 43.9 %collective-permute-start.2 = (f32[192,128]{1,0:T(8,128)}, f32[192,128]{1,0:T(8,128)S(1)}, u32[]{:S(2)}, u32[]{:S(2)}) collective-permute-start(f32[192,128]{1,0:T(8,128)} %get-tuple-element.60), channel_id=1, source_target_pairs={{1,0},{2,1},{3,2},{4,3},{5,4},{6,5},{7,6},{8,7},{9,8},{10,9},{11,1... | collective-permute-start | bytes 294920 | tf_op jit(solution)/shard_map/ppermute | solution.py:481
  30.4 39.5 %collective-permute-start.3 = (f32[192,128]{1,0:T(8,128)}, f32[192,128]{1,0:T(8,128)S(1)}, u32[]{:S(2)}, u32[]{:S(2)}) collective-permute-start(f32[192,128]{1,0:T(8,128)} %get-tuple-element.61), channel_id=1, source_target_pairs={{0,1},{1,2},{2,3},{3,4},{4,5},{5,6},{6,7},{7,8},{8,9},{9,10},{10,1... | collective-permute-start | bytes 294920 | tf_op jit(solution)/shard_map/ppermute | solution.py:481
  32.5 0.8 copy-start.8
  33.4 0.7 copy-start.10
  34.0 0.7 copy-start.11
  34.7 0.7 copy-start.12
  57.3 0.7 copy-start.9
  58.0 11.8 %copy-start.6 = (f32[16,128]{1,0:T(8,128)S(1)}, f32[16,128]{1,0:T(8,128)}, u32[]{:S(2)}) copy-start(f32[16,128]{1,0:T(8,128)} %fy_ref.5) | copy-start | bytes 24580
  81.7 25.2 %copy-start.14 = (f32[192,128]{1,0:T(8,128)S(1)}, f32[192,128]{1,0:T(8,128)}, u32[]{:S(2)}) copy-start(f32[192,128]{1,0:T(8,128)} %get-tuple-element.68) | copy-start | bytes 294916
  81.7 29.6 %copy-start.13 = (f32[192,128]{1,0:T(8,128)S(1)}, f32[192,128]{1,0:T(8,128)}, u32[]{:S(2)}) copy-start(f32[192,128]{1,0:T(8,128)} %get-tuple-element.69) | copy-start | bytes 294916
  81.7 38.2 %copy-start.7 = (f32[16,128]{1,0:T(8,128)S(1)}, f32[16,128]{1,0:T(8,128)}, u32[]{:S(2)}) copy-start(f32[16,128]{1,0:T(8,128)} %fy_ref.5) | copy-start | bytes 24580
  81.7 19.3 %all-to-all-start.1 = ((f32[128,8,128]{2,1,0:T(8,128)}), f32[128,8,128]{2,1,0:T(8,128)S(1)}, u32[]{:S(2)}, u32[]{:S(2)}) async-start(f32[128,8,128]{2,1,0:T(8,128)} %bitcast.27), calls=%async_computation.1 | async-start | bytes 1048576 | tf_op jit(solution)/shard_map/all_to_all | solution.py:464
  87.7 4.3 %collective-permute-start.4 = (f32[192,128]{1,0:T(8,128)}, f32[192,128]{1,0:T(8,128)S(1)}, u32[]{:S(2)}, u32[]{:S(2)}) collective-permute-start(f32[192,128]{1,0:T(8,128)} %get-tuple-element.62), channel_id=1, source_target_pairs={{16,0},{32,16},{48,32},{64,48},{80,64},{96,80},{112,96},{17,1},{33... | collective-permute-start | bytes 294920 | tf_op jit(solution)/shard_map/ppermute | solution.py:481
  89.0 4.2 %collective-permute-start.5 = (f32[192,128]{1,0:T(8,128)}, f32[192,128]{1,0:T(8,128)S(1)}, u32[]{:S(2)}, u32[]{:S(2)}) collective-permute-start(f32[192,128]{1,0:T(8,128)} %get-tuple-element.63), channel_id=1, source_target_pairs={{0,16},{16,32},{32,48},{48,64},{64,80},{80,96},{96,112},{1,17},{17... | collective-permute-start | bytes 294920 | tf_op jit(solution)/shard_map/ppermute | solution.py:481
  102.0 23.2 %all-to-all-start.2 = ((f32[128,8,128]{2,1,0:T(8,128)}), f32[128,8,128]{2,1,0:T(8,128)S(1)}, u32[]{:S(2)}, u32[]{:S(2)}) async-start(f32[128,8,128]{2,1,0:T(8,128)} %bitcast.25), calls=%async_computation.2 | async-start | bytes 1048576 | tf_op jit(solution)/shard_map/all_to_all | solution.py:471
  106.9 9.5 %collective-permute-start.6 = (f32[192,128]{1,0:T(8,128)S(1)}, f32[192,128]{1,0:T(8,128)S(1)}, u32[]{:S(2)}, u32[]{:S(2)}) collective-permute-start(f32[192,128]{1,0:T(8,128)S(1)} %copy-done.14), channel_id=1, source_target_pairs={{1,0},{2,1},{3,2},{4,3},{5,4},{6,5},{7,6},{8,7},{9,8},{10,9},{11,1... | collective-permute-start | bytes 294920 | tf_op jit(solution)/shard_map/ppermute | solution.py:481
  111.3 8.6 %collective-permute-start.7 = (f32[192,128]{1,0:T(8,128)S(1)}, f32[192,128]{1,0:T(8,128)S(1)}, u32[]{:S(2)}, u32[]{:S(2)}) collective-permute-start(f32[192,128]{1,0:T(8,128)S(1)} %copy-done.13), channel_id=1, source_target_pairs={{0,1},{1,2},{2,3},{3,4},{4,5},{5,6},{6,7},{7,8},{8,9},{9,10},{10,1... | collective-permute-start | bytes 294920 | tf_op jit(solution)/shard_map/ppermute | solution.py:481

commit v6 on v5

--- a/solution.py
+++ b/solution.py
@@ -20,7 +20,7 @@
 CY = 128
 DEV = 128
 STORE = 4096
-UNROLL = 8
+UNROLL = 16
 COLS = CX * CY
 
 CLOSURE_MIB = 24
@@ -51,6 +51,19 @@
     return pltpu.CompilerParams(vmem_limit_bytes=mib * 2**20)
 
 
+def bring(copies, sems):
+    started = {}
+    for i, (name, source, target) in enumerate(copies):
+        started.setdefault(name, []).append(pltpu.make_async_copy(source, target, sems.at[i]))
+        started[name][-1].start()
+
+    def wait(name):
+        for copy in started.pop(name, ()):
+            copy.wait()
+
+    return wait
+
+
 def near(*shape, dtype=F32):
     return pltpu.VMEM(shape, dtype)
 
@@ -59,7 +72,7 @@
     return pltpu.HBM(shape, dtype)
 
 
-def call(kernel, name, outs, args, copied=(), scratch=(), mib=4):
+def call(kernel, name, outs, args, copied=(), scratch=(), mib=4, aliases={}):
     args = [pltpu.with_memory_space_constraint(a, pltpu.VMEM) for a in args]
     copied = [pltpu.with_memory_space_constraint(a, pltpu.HBM) for a in copied]
     inside = pl.BlockSpec(memory_space=pltpu.VMEM)
@@ -70,6 +83,7 @@
         in_specs=[inside] * len(args) + [anywhere] * len(copied),
         out_specs=tuple(anywhere if isinstance(out, list) else inside for out in outs),
         scratch_shapes=list(scratch),
+        input_output_aliases=aliases,
         compiler_params=params(mib),
         name=name,
     )(*args, *copied)
@@ -220,16 +234,11 @@
     return total
 
 
-def halo_plane(x, hn_ref, hs_ref, hw_ref, he_ref):
-    lane = lax.broadcasted_iota(jnp.int32, hn_ref.shape, 1)
-    total = jnp.where(lane == CY - 1, pltpu.roll(hw_ref[...], CY - 1 - x, 1), 0.0)
+def halo_lanes(x, hw_ref, he_ref):
+    lane = lax.broadcasted_iota(jnp.int32, hw_ref.shape, 1)
     east = he_ref[...] if x == 0 else pltpu.roll(he_ref[...], CY - x, 1)
-    total = total + jnp.where(lane == 0, east, 0.0)
-    if x == 0:
-        total = total + hs_ref[...]
-    if x == CX - 1:
-        total = total + hn_ref[...]
-    return total
+    west = pltpu.roll(hw_ref[...], CY - 1 - x, 1)
+    return jnp.where(lane == CY - 1, west, 0.0) + jnp.where(lane == 0, east, 0.0)
 
 
 def put_edges(lam_ref, mask_ref, fx_ref, fy_ref, en_ref, es_ref, ew_ref, ee_ref):
@@ -259,17 +268,11 @@
     return call(edges_kernel, "edges", (far(*PLANE), far(*PLANE), EDGE, EDGE, EDGE, EDGE), args)
 
 
-def last_kernel(mask_ref, fx_ref, fy_ref, hn_ref, hs_ref, hw_ref, he_ref, lam_far, down_far, out_ref, lam, down, sems):
-    copies = [
-        pltpu.make_async_copy(lam_far, lam, sems.at[0]),
-        pltpu.make_async_copy(down_far, down, sems.at[1]),
-    ]
-    for copy in copies:
-        copy.start()
-    for copy in copies:
-        copy.wait()
+def last_kernel(mask_ref, fx_ref, fy_ref, hw_ref, he_ref, lam_far, down_far, out_ref, lam, down, sems):
+    wait = bring(((0, lam_far, lam), (0, down_far, down)), sems)
+    wait(0)
     for x in range(CX):
-        total = local_plane(x, lam, mask_ref, fx_ref, fy_ref) + halo_plane(x, hn_ref, hs_ref, hw_ref, he_ref)
+        total = local_plane(x, lam, mask_ref, fx_ref, fy_ref) + halo_lanes(x, hw_ref, he_ref)
         value = lam[x] + step_size * (total + down[x])
         for t in range(TRACERS):
             out_ref[pl.ds(t * NZ * CX + x, NZ, stride=CX), :] = value[t * PAD : t * PAD + NZ]
@@ -277,7 +280,19 @@
 
 def last_stencil(lam, down, *args):
     scratch = [near(*PLANE), near(*PLANE), pltpu.SemaphoreType.DMA((2,))]
-    (out,) = call(last_kernel, "stencil0", (far(TRACERS * NZ * CX, CY),), args, (lam, down), scratch, mib=8)
+    (out,) = call(last_kernel, "stencil0", (near(TRACERS * NZ * CX, CY),), args, (lam, down), scratch, mib=8)
+    return out
+
+
+def rows_kernel(part_ref, hn_ref, hs_ref, out_ref):
+    for x, halo_ref in ((0, hs_ref), (CX - 1, hn_ref)):
+        for t in range(TRACERS):
+            rows = pl.ds(t * NZ * CX + x, NZ, stride=CX)
+            out_ref[rows, :] = part_ref[rows, :] + step_size * halo_ref[t * PAD : t * PAD + NZ, :]
+
+
+def add_rows(part, hn, hs):
+    (out,) = call(rows_kernel, "rows0", (near(*part.shape),), (part, hn, hs), aliases={0: 0})
     return out
 
 
@@ -299,6 +314,7 @@
     def wide(ref):
         return jnp.concatenate([ref[i : i + 1, :] for i in range(CX)], axis=1)
 
+    wait("tile")
     owner = wide(owner_ref)
     at = ((owner >> 4) & 1) * (STORE // 2) + (owner >> 5) * HALF + (owner & (HALF - 1))
     level = lax.broadcasted_iota(jnp.int32, (256, COLS), 0)
@@ -364,25 +380,13 @@
     total[NZ + 2 : NZ + 3, :PAD] += both[:1, :PAD] + both[:1, PAD:]
 
 
-def bring(refs, copies, sems):
-    started = {}
-    for i, (name, source, target) in enumerate(copies):
-        started.setdefault(name, []).append(pltpu.make_async_copy(source, target, sems.at[i]))
-        started[name][-1].start()
-
-    def wait(name):
-        for copy in started.pop(name, ()):
-            copy.wait()
-
-    return wait
-
-
-def late_kernel(got_ref, owner_ref, mask_ref, *refs):
-    sources, (out_ref, total), refs = refs[:10], refs[10:12], refs[12:]
-    targets, (rows_ref, down, sems) = refs[:10], refs[10:]
-    names = ("weights",) * 8 + ("lam", "base")
-    wait = bring(refs, zip(names, sources, targets), sems)
-    planes, base = targets[8:]
+def late_kernel(got_ref, *refs):
+    sources, (out_ref, total), refs = refs[:12], refs[12:14], refs[14:]
+    targets, (rows_ref, down, sems) = refs[:12], refs[12:]
+    names = ("tile", "tile") + ("weights",) * 8 + ("lam", "base")
+    wait = bring(zip(names, sources, targets), sems)
+    owner, mask, *split_weights = targets[:10]
+    planes, base = targets[10:]
     total[...] = jnp.zeros_like(total)
 
     def then(name):
@@ -392,16 +396,22 @@
             for x in range(CX):
                 out_ref[x] = base[x] + step_size * down[x]
 
-    closure_step(BLOCK, got_ref, owner_ref, mask_ref, planes, targets[:8], down, rows_ref, total, then)
+    closure_step(BLOCK, got_ref, owner, mask, planes, split_weights, down, rows_ref, total, then)
 
 
 def early_kernel(got_ref, owner_ref, mask_ref, fx_ref, fy_ref, part_ref, before_ref, *refs):
     halos, sources, refs = refs[:4], refs[4:12], refs[12:]
     (lam_far, down_far, grads_ref), sides, refs = refs[:3], refs[3:7], refs[7:]
     targets, (rows_ref, lam, down, total, sems, out_sems) = refs[:8], refs[8:]
-    wait = bring(refs, zip(("weights",) * 8, sources, targets), sems)
+    wait = bring(zip(("weights",) * 8, sources, targets), sems)
+    hn_ref, hs_ref, hw_ref, he_ref = halos
     for x in range(CX):
-        lam[x] = part_ref[x] + step_size * halo_plane(x, *halos)
+        halo = halo_lanes(x, hw_ref, he_ref)
+        if x == 0:
+            halo = halo + hs_ref[...]
+        if x == CX - 1:
+            halo = halo + hn_ref[...]
+        lam[x] = part_ref[x] + step_size * halo
     lam_copy = pltpu.make_async_copy(lam, lam_far, out_sems.at[0])
     lam_copy.start()
     down_copy = pltpu.make_async_copy(down, down_far, out_sems.at[1])
@@ -425,10 +435,10 @@
 TOTAL = near(2 * HID, HID)
 
 
-def late_closure(got, owners, mask, split_weights, planes, base):
-    scratch = WEIGHT_SCRATCH + [near(*PLANE), near(*PLANE), ROWS, near(*PLANE), pltpu.SemaphoreType.DMA((10,))]
-    copied = (*split_weights, planes, base)
-    return call(late_kernel, "closure1", (near(*PLANE), TOTAL), (got, owners, mask), copied, scratch, CLOSURE_MIB)
+def late_closure(got, *copied):
+    scratch = [near(CX, CY, dtype=jnp.int32)] * 2 + WEIGHT_SCRATCH
+    scratch += [near(*PLANE), near(*PLANE), ROWS, near(*PLANE), pltpu.SemaphoreType.DMA((12,))]
+    return call(late_kernel, "closure1", (near(*PLANE), TOTAL), (got,), copied, scratch, CLOSURE_MIB)
 
 
 def early_closure(got, owners, mask, fx, fy, part, before, halos, split_weights):
@@ -506,15 +516,17 @@
         costate.reshape(TRACERS * NZ * CX, CY), land_mask, flow_x, flow_y
     )
     halos = exchange("gx", north, south) + exchange("gy", west, east)
-    part, grads = late_closure(got, owners, land_mask, split_weights, planes, base)
+    part, grads = late_closure(got, owners, land_mask, *split_weights, planes, base)
     lam, down, packed, north, south, west, east = early_closure(
         got, owners, land_mask, flow_x, flow_y, part, grads, halos, split_weights
     )
+    halos_y = exchange("gy", west, east)
+    spread = reduce_params(packed, halos_y)
+    north, south, spread = lax.optimization_barrier((north, south, spread))
     halos_x = exchange("gx", north, south)
-    spread = reduce_params(packed, halos_x)
-    west, east, spread = lax.optimization_barrier((west, east, spread))
-    halos_y = exchange("gy", west, east)
-    adjoint = last_stencil(lam, down, land_mask, flow_x, flow_y, *halos_x, *halos_y)
+    lam, down, spread = lax.optimization_barrier((lam, down, spread))
+    adjoint = last_stencil(lam, down, land_mask, flow_x, flow_y, *halos_y)
+    adjoint = add_rows(adjoint, *halos_x)
     count = CX * CY * lax.axis_size("gx") * lax.axis_size("gy")
     g1, gb1, g2, gb2, g3, gb3 = finish_params(spread, count)
     return (adjoint.reshape(costate.shape), g1, gb1[0], g2, gb2[0], g3.T, gb3[0])

time: 127 us -> 125 us (0.984)
  the two profiles are of different devices: /device:TPU:32 before, /device:TPU:1 now
where the time goes in v6:
time: 125 us; the launch traced here: 124 us
  starting transfers between devices  45.4 us (36%)
  Pallas kernels  39.5 us (32%)
  waiting for transfers between devices  33.2 us (27%)
  local copies, waits for them, and re-layouts  5.38 us (4%)
    pallas_call x8, Pallas kernels, call(): pl.pallas_call(kernel, out_shape=tuple((out[0] if isinstance(out, list) e...  33.5 us
    ppermute x8, starting transfers between devices, exchange(): return (lax.ppermute(before, axis, down), lax.ppermute(after, axis, up))  21.9 us
    all_to_all x1, waiting for transfers between devices, on_device(): lax.all_to_all(payload, ('gx', 'gy'), split_axis=0, concat_axis=0, tiled=...  21.2 us
    all_to_all x1, starting transfers between devices, on_device(): lax.all_to_all(payload, ('gx', 'gy'), split_axis=0, concat_axis=0, tiled=...  11.5 us
    all_to_all x1, starting transfers between devices, finish_params(): lax.all_to_all(spread, ('gx', 'gy'), split_axis=0, concat_axis=0, tiled=T...  6.67 us
    pallas_call x1, Pallas kernels, pack(): pl.pallas_call(pack_kernel, out_shape=pltpu.HBM((DEV, 2 * BLOCK, 128), BF...  5.96 us
    unnamed x33, local copies, waits for them, and re-layouts  5.38 us
    all_to_all x1, starting transfers between devices, reduce_params(): lax.all_to_all(packed, ('gx', 'gy'), split_axis=0, concat_axis=0, tiled=T...  5.32 us
  transfers between devices with their start and end apart: 11, of which 4 were waited for; matrix products, arithmetic and copies ran while one was open for 1% of the time, Pallas kernels for 16%

profile of v6, /device:TPU:1, one launch (start us, length us, event | category | flops | bytes accessed | tf_op | source)
XLA Modules:
  0.0 124.4 jit_solution(700382972149435914)
XLA Ops:
  0.6 6.0 %pack.1 = bf16[128,96,128]{2,1,0:T(8,128)(2,1)} custom-call(s32[1,128]{1,0:T(1,128)} %counts_ref.1, bf16[360,4096]{1,0:T(8,128)(2,1)} %bitcast.25), custom_call_target="tpu_custom_call" | custom-call | tf_op jit(solution)/shard_map/pack/pallas_call | solution.py:143
  6.6 0.0 copy-start.3
  6.6 0.0 copy-start.5
  6.6 11.5 %all-to-all-start = ((bf16[128,96,128]{2,1,0:T(8,128)(2,1)}), bf16[128,96,128]{2,1,0:T(8,128)(2,1)S(1)}, u32[]{:S(2)}, u32[]{:S(2)}) async-start(bf16[128,96,128]{2,1,0:T(8,128)(2,1)} %pack.1), calls=%async_computation | async-start | bytes 6291456 | tf_op jit(solution)/shard_map/all_to_all | solution.py:511
  18.2 1.4 %copy-done = f32[3,60,16,128]{3,2,1,0:T(8,128)S(1)} copy-done((f32[3,60,16,128]{3,2,1,0:T(8,128)S(1)}, f32[3,60,16,128]{3,2,1,0:T(8,128)}, u32[]{:S(2)}) %copy-start) | copy-done | bytes 1474584
  19.6 3.1 %edges.1 = (f32[16,192,128]{2,1,0:T(8,128)}, f32[16,192,128]{2,1,0:T(8,128)}, f32[192,128]{1,0:T(8,128)}, f32[192,128]{1,0:T(8,128)}, f32[192,128]{1,0:T(8,128)}, /*index=5*/f32[192,128]{1,0:T(8,128)}) custom-call(f32[2880,128]{1,0:T(8,128)S(1)} %bitcast.20, s32[16,128]{1,0:T(8,128)S(1)} %copy-done.3, f32[16,128]{1,0:T(8,128)S(1)} %copy-done.5, ...), custom_call_target="tpu_custom_call" | custom-call | tf_op jit(solution)/shard_map/edges/pallas_call | solution.py:80
  22.7 3.0 %collective-permute-start = (f32[192,128]{1,0:T(8,128)}, f32[192,128]{1,0:T(8,128)S(1)}, u32[]{:S(2)}, u32[]{:S(2)}) collective-permute-start(f32[192,128]{1,0:T(8,128)} %get-tuple-element.61), channel_id=1, source_target_pairs={{16,0},{32,16},{48,32},{64,48},{80,64},{96,80},{112,96},{17,1},{33... | collective-permute-start | bytes 294920 | tf_op jit(solution)/shard_map/ppermute | solution.py:491
  25.6 2.6 %collective-permute-start.1 = (f32[192,128]{1,0:T(8,128)}, f32[192,128]{1,0:T(8,128)S(1)}, u32[]{:S(2)}, u32[]{:S(2)}) collective-permute-start(f32[192,128]{1,0:T(8,128)} %get-tuple-element.62), channel_id=1, source_target_pairs={{0,16},{16,32},{32,48},{48,64},{64,80},{80,96},{96,112},{1,17},{17... | collective-permute-start | bytes 294920 | tf_op jit(solution)/shard_map/ppermute | solution.py:491
  28.2 1.3 %collective-permute-start.2 = (f32[192,128]{1,0:T(8,128)}, f32[192,128]{1,0:T(8,128)S(1)}, u32[]{:S(2)}, u32[]{:S(2)}) collective-permute-start(f32[192,128]{1,0:T(8,128)} %get-tuple-element.63), channel_id=1, source_target_pairs={{1,0},{2,1},{3,2},{4,3},{5,4},{6,5},{7,6},{8,7},{9,8},{10,9},{11,1... | collective-permute-start | bytes 294920 | tf_op jit(solution)/shard_map/ppermute | solution.py:491
  29.5 4.2 %collective-permute-start.3 = (f32[192,128]{1,0:T(8,128)}, f32[192,128]{1,0:T(8,128)S(1)}, u32[]{:S(2)}, u32[]{:S(2)}) collective-permute-start(f32[192,128]{1,0:T(8,128)} %get-tuple-element.64), channel_id=1, source_target_pairs={{0,1},{1,2},{2,3},{3,4},{4,5},{5,6},{6,7},{7,8},{8,9},{9,10},{10,1... | collective-permute-start | bytes 294920 | tf_op jit(solution)/shard_map/ppermute | solution.py:491
  33.8 0.8 copy-done.9
  34.6 0.7 copy-done.11
  35.3 0.7 copy-done.12
  36.0 0.7 copy-done.13
  36.6 1.2 weights.1
  37.8 21.2 %all-to-all-done.got_ref = bf16[128,96,128]{2,1,0:T(8,128)(2,1)S(1)} async-done(((bf16[128,96,128]{2,1,0:T(8,128)(2,1)}), bf16[128,96,128]{2,1,0:T(8,128)(2,1)S(1)}, u32[]{:S(2)}, u32[]{:S(2)}) %all-to-all-start) | async-done | bytes 3145760 | tf_op jit(solution)/shard_map/all_to_all | solution.py:511
  59.1 11.5 %closure1.1 = (f32[16,192,128]{2,1,0:T(8,128)S(1)}, f32[512,256]{1,0:T(8,128)S(1)}) custom-call(bf16[128,96,128]{2,1,0:T(8,128)(2,1)S(1)} %all-to-all-done.got_ref, s32[16,128]{1,0:T(8,128)} %owner_ref.1, s32[16,128]{1,0:T(8,128)} %mask_ref.5, bf16[512,192]{1,0:T(8,128)(2,1)} %get-tuple-element.48.refs_2_.refs_4_, ...), custom_call_target="tpu_custom_call" | custom-call | tf_op jit(solution)/shard_map/closure1/pallas_call | solution.py:80
  70.7 11.6 %closure0.1 = (f32[16,192,128]{2,1,0:T(8,128)}, f32[16,192,128]{2,1,0:T(8,128)}, f32[1024,128]{1,0:T(8,128)}, f32[192,128]{1,0:T(8,128)}, f32[192,128]{1,0:T(8,1...) custom-call(bf16[128,96,128]{2,1,0:T(8,128)(2,1)S(1)} %all-to-all-done.got_ref, s32[16,128]{1,0:T(8,128)S(1)} %copy-done.10, ...), custom_call_target="tpu_custom_call" | custom-call | tf_op jit(solution)/shard_map/closure0/pallas_call | solution.py:80
  82.3 5.3 %all-to-all-start.1 = ((f32[128,8,128]{2,1,0:T(8,128)}), f32[128,8,128]{2,1,0:T(8,128)S(1)}, u32[]{:S(2)}, u32[]{:S(2)}) async-start(f32[128,8,128]{2,1,0:T(8,128)} %bitcast.27), calls=%async_computation.1 | async-start | bytes 1048576 | tf_op jit(solution)/shard_map/all_to_all | solution.py:474
  87.7 1.3 %collective-permute-start.4 = (f32[192,128]{1,0:T(8,128)}, f32[192,128]{1,0:T(8,128)S(1)}, u32[]{:S(2)}, u32[]{:S(2)}) collective-permute-start(f32[192,128]{1,0:T(8,128)} %get-tuple-element.65), channel_id=1, source_target_pairs={{1,0},{2,1},{3,2},{4,3},{5,4},{6,5},{7,6},{8,7},{9,8},{10,9},{11,1... | collective-permute-start | bytes 294920 | tf_op jit(solution)/shard_map/ppermute | solution.py:491
  89.0 4.0 %collective-permute-start.5 = (f32[192,128]{1,0:T(8,128)}, f32[192,128]{1,0:T(8,128)S(1)}, u32[]{:S(2)}, u32[]{:S(2)}) collective-permute-start(f32[192,128]{1,0:T(8,128)} %get-tuple-element.66), channel_id=1, source_target_pairs={{0,1},{1,2},{2,3},{3,4},{4,5},{5,6},{6,7},{7,8},{8,9},{9,10},{10,1... | collective-permute-start | bytes 294920 | tf_op jit(solution)/shard_map/ppermute | solution.py:491
  93.0 3.9 %collective-permute-done.4.hw_ref = f32[192,128]{1,0:T(8,128)S(1)} collective-permute-done((f32[192,128]{1,0:T(8,128)}, f32[192,128]{1,0:T(8,128)S(1)}, u32[]{:S(2)}, u32[]{:S(2)}) %collective-permute-start.4) | collective-permute-done | bytes 98336 | tf_op jit(solution)/shard_map/ppermute | solution.py:491
  96.9 4.9 %all-to-all-done.1 = f32[128,8,128]{2,1,0:T(8,128)S(1)} async-done(((f32[128,8,128]{2,1,0:T(8,128)}), f32[128,8,128]{2,1,0:T(8,128)S(1)}, u32[]{:S(2)}, u32[]{:S(2)}) %all-to-all-start.1) | async-done | bytes 524320 | tf_op jit(solution)/shard_map/all_to_all | solution.py:474
  101.8 1.0 sum.1
  102.8 6.7 %all-to-all-start.2 = ((f32[128,8,128]{2,1,0:T(8,128)}), f32[128,8,128]{2,1,0:T(8,128)S(1)}, u32[]{:S(2)}, u32[]{:S(2)}) async-start(f32[128,8,128]{2,1,0:T(8,128)} %bitcast.26), calls=%async_computation.2 | async-start | bytes 1048576 | tf_op jit(solution)/shard_map/all_to_all | solution.py:481
  109.4 3.0 %collective-permute-start.6 = (f32[192,128]{1,0:T(8,128)S(1)}, f32[192,128]{1,0:T(8,128)S(1)}, u32[]{:S(2)}, u32[]{:S(2)}) collective-permute-start(f32[192,128]{1,0:T(8,128)S(1)} %copy-done.15), channel_id=1, source_target_pairs={{16,0},{32,16},{48,32},{64,48},{80,64},{96,80},{112,96},{17,1},{33... | collective-permute-start | bytes 294920 | tf_op jit(solution)/shard_map/ppermute | solution.py:491
  112.4 2.6 %collective-permute-start.7 = (f32[192,128]{1,0:T(8,128)S(1)}, f32[192,128]{1,0:T(8,128)S(1)}, u32[]{:S(2)}, u32[]{:S(2)}) collective-permute-start(f32[192,128]{1,0:T(8,128)S(1)} %copy-done.14), channel_id=1, source_target_pairs={{0,16},{16,32},{32,48},{48,64},{64,80},{80,96},{96,112},{1,17},{17... | collective-permute-start | bytes 294920 | tf_op jit(solution)/shard_map/ppermute | solution.py:491
  115.0 4.1 %stencil0.1.part_ref = f32[2880,128]{1,0:T(8,128)S(1)} custom-call(s32[16,128]{1,0:T(8,128)S(1)} %copy-done.4, f32[16,128]{1,0:T(8,128)S(1)} %copy-done.5, f32[16,128]{1,0:T(8,128)S(1)} %copy-done.8, f32[192,128]{1,0:T(8,128)S(1)} %collective-permute-done.4.hw_ref, f32[192,128]{1,0:T(8,128)S(1)} %collective-permute-done.5.he_ref, ...), custom_call_target="tpu_custom_call" | custom-call | tf_op jit(solution)/shard_map/stencil0/pallas_call | solution.py:80
  119.1 0.2 rows0.1
  119.3 1.1 copy.22
  120.4 3.1 %all-to-all-done.2 = f32[128,8,128]{2,1,0:T(8,128)S(1)} async-done(((f32[128,8,128]{2,1,0:T(8,128)}), f32[128,8,128]{2,1,0:T(8,128)S(1)}, u32[]{:S(2)}, u32[]{:S(2)}) %all-to-all-start.2) | async-done | bytes 524320 | tf_op jit(solution)/shard_map/all_to_all | solution.py:481
  123.6 0.8 unpack.1
  (32 shorter events, 0.1 us)
Async XLA Ops:
  6.6 11.5 %copy-start.3 = (s32[16,128]{1,0:T(8,128)S(1)}, s32[16,128]{1,0:T(8,128)}, u32[]{:S(2)}) copy-start(s32[16,128]{1,0:T(8,128)} %mask_ref.5) | copy-start | bytes 24580
  6.6 11.5 %copy-start.5 = (f32[16,128]{1,0:T(8,128)S(1)}, f32[16,128]{1,0:T(8,128)}, u32[]{:S(2)}) copy-start(f32[16,128]{1,0:T(8,128)} %fx_ref.5) | copy-start | bytes 24580
  6.6 11.5 %copy-start.6 = (f32[16,128]{1,0:T(8,128)S(1)}, f32[16,128]{1,0:T(8,128)}, u32[]{:S(2)}) copy-start(f32[16,128]{1,0:T(8,128)} %fy_ref.5) | copy-start | bytes 24580
  6.6 52.4 %all-to-all-start = ((bf16[128,96,128]{2,1,0:T(8,128)(2,1)}), bf16[128,96,128]{2,1,0:T(8,128)(2,1)S(1)}, u32[]{:S(2)}, u32[]{:S(2)}) async-start(bf16[128,96,128]{2,1,0:T(8,128)(2,1)} %pack.1), calls=%async_computation | async-start | bytes 6291456 | tf_op jit(solution)/shard_map/all_to_all | solution.py:511
  18.2 1.4 %copy-start = (f32[3,60,16,128]{3,2,1,0:T(8,128)S(1)}, f32[3,60,16,128]{3,2,1,0:T(8,128)}, u32[]{:S(2)}) copy-start(f32[3,60,16,128]{3,2,1,0:T(8,128)} %param.19) | copy-start | bytes 4423684
  19.6 14.2 %copy-start.1 = (f32[256,256]{1,0:T(8,128)S(1)}, f32[256,256]{1,0:T(8,128)}, u32[]{:S(2)}) copy-start(f32[256,256]{1,0:T(8,128)} %w2_ref) | copy-start | bytes 786436
  19.6 14.2 %copy-start.2 = (f32[180,256]{1,0:T(8,128)S(1)}, f32[180,256]{1,0:T(8,128)}, u32[]{:S(2)}) copy-start(f32[180,256]{1,0:T(8,128)} %w1_ref.1) | copy-start | bytes 552964
  22.7 47.9 %collective-permute-start = (f32[192,128]{1,0:T(8,128)}, f32[192,128]{1,0:T(8,128)S(1)}, u32[]{:S(2)}, u32[]{:S(2)}) collective-permute-start(f32[192,128]{1,0:T(8,128)} %get-tuple-element.61), channel_id=1, source_target_pairs={{16,0},{32,16},{48,32},{64,48},{80,64},{96,80},{112,96},{17,1},{33... | collective-permute-start | bytes 294920 | tf_op jit(solution)/shard_map/ppermute | solution.py:491
  25.6 45.0 %collective-permute-start.1 = (f32[192,128]{1,0:T(8,128)}, f32[192,128]{1,0:T(8,128)S(1)}, u32[]{:S(2)}, u32[]{:S(2)}) collective-permute-start(f32[192,128]{1,0:T(8,128)} %get-tuple-element.62), channel_id=1, source_target_pairs={{0,16},{16,32},{32,48},{48,64},{64,80},{80,96},{96,112},{1,17},{17... | collective-permute-start | bytes 294920 | tf_op jit(solution)/shard_map/ppermute | solution.py:491
  28.2 42.4 %collective-permute-start.2 = (f32[192,128]{1,0:T(8,128)}, f32[192,128]{1,0:T(8,128)S(1)}, u32[]{:S(2)}, u32[]{:S(2)}) collective-permute-start(f32[192,128]{1,0:T(8,128)} %get-tuple-element.63), channel_id=1, source_target_pairs={{1,0},{2,1},{3,2},{4,3},{5,4},{6,5},{7,6},{8,7},{9,8},{10,9},{11,1... | collective-permute-start | bytes 294920 | tf_op jit(solution)/shard_map/ppermute | solution.py:491
  29.5 41.1 %collective-permute-start.3 = (f32[192,128]{1,0:T(8,128)}, f32[192,128]{1,0:T(8,128)S(1)}, u32[]{:S(2)}, u32[]{:S(2)}) collective-permute-start(f32[192,128]{1,0:T(8,128)} %get-tuple-element.64), channel_id=1, source_target_pairs={{0,1},{1,2},{2,3},{3,4},{4,5},{5,6},{6,7},{7,8},{8,9},{9,10},{10,1... | collective-permute-start | bytes 294920 | tf_op jit(solution)/shard_map/ppermute | solution.py:491
  33.8 0.8 copy-start.9
  34.6 0.7 copy-start.11
  35.3 0.7 copy-start.12
  36.0 0.7 copy-start.13
  59.1 11.6 %copy-start.4 = (s32[16,128]{1,0:T(8,128)S(1)}, s32[16,128]{1,0:T(8,128)}, u32[]{:S(2)}) copy-start(s32[16,128]{1,0:T(8,128)} %mask_ref.5) | copy-start | bytes 24580
  59.1 11.6 %copy-start.7 = (f32[16,128]{1,0:T(8,128)S(1)}, f32[16,128]{1,0:T(8,128)}, u32[]{:S(2)}) copy-start(f32[16,128]{1,0:T(8,128)} %fy_ref.5) | copy-start | bytes 24580
  59.1 11.6 %copy-start.10 = (s32[16,128]{1,0:T(8,128)S(1)}, s32[16,128]{1,0:T(8,128)}, u32[]{:S(2)}) copy-start(s32[16,128]{1,0:T(8,128)} %owner_ref.1) | copy-start | bytes 24580
  82.3 27.1 %copy-start.15 = (f32[192,128]{1,0:T(8,128)S(1)}, f32[192,128]{1,0:T(8,128)}, u32[]{:S(2)}) copy-start(f32[192,128]{1,0:T(8,128)} %get-tuple-element.76) | copy-start | bytes 294916
  82.3 30.1 %copy-start.14 = (f32[192,128]{1,0:T(8,128)S(1)}, f32[192,128]{1,0:T(8,128)}, u32[]{:S(2)}) copy-start(f32[192,128]{1,0:T(8,128)} %get-tuple-element.77) | copy-start | bytes 294916
  82.3 32.7 %copy-start.8 = (f32[16,128]{1,0:T(8,128)S(1)}, f32[16,128]{1,0:T(8,128)}, u32[]{:S(2)}) copy-start(f32[16,128]{1,0:T(8,128)} %fy_ref.5) | copy-start | bytes 24580
  82.3 19.5 %all-to-all-start.1 = ((f32[128,8,128]{2,1,0:T(8,128)}), f32[128,8,128]{2,1,0:T(8,128)S(1)}, u32[]{:S(2)}, u32[]{:S(2)}) async-start(f32[128,8,128]{2,1,0:T(8,128)} %bitcast.27), calls=%async_computation.1 | async-start | bytes 1048576 | tf_op jit(solution)/shard_map/all_to_all | solution.py:474
  87.7 9.2 %collective-permute-start.4 = (f32[192,128]{1,0:T(8,128)}, f32[192,128]{1,0:T(8,128)S(1)}, u32[]{:S(2)}, u32[]{:S(2)}) collective-permute-start(f32[192,128]{1,0:T(8,128)} %get-tuple-element.65), channel_id=1, source_target_pairs={{1,0},{2,1},{3,2},{4,3},{5,4},{6,5},{7,6},{8,7},{9,8},{10,9},{11,1... | collective-permute-start | bytes 294920 | tf_op jit(solution)/shard_map/ppermute | solution.py:491
  89.0 7.9 %collective-permute-start.5 = (f32[192,128]{1,0:T(8,128)}, f32[192,128]{1,0:T(8,128)S(1)}, u32[]{:S(2)}, u32[]{:S(2)}) collective-permute-start(f32[192,128]{1,0:T(8,128)} %get-tuple-element.66), channel_id=1, source_target_pairs={{0,1},{1,2},{2,3},{3,4},{4,5},{5,6},{6,7},{7,8},{8,9},{9,10},{10,1... | collective-permute-start | bytes 294920 | tf_op jit(solution)/shard_map/ppermute | solution.py:491
  102.8 20.8 %all-to-all-start.2 = ((f32[128,8,128]{2,1,0:T(8,128)}), f32[128,8,128]{2,1,0:T(8,128)S(1)}, u32[]{:S(2)}, u32[]{:S(2)}) async-start(f32[128,8,128]{2,1,0:T(8,128)} %bitcast.26), calls=%async_computation.2 | async-start | bytes 1048576 | tf_op jit(solution)/shard_map/all_to_all | solution.py:481
  109.4 9.7 %collective-permute-start.6 = (f32[192,128]{1,0:T(8,128)S(1)}, f32[192,128]{1,0:T(8,128)S(1)}, u32[]{:S(2)}, u32[]{:S(2)}) collective-permute-start(f32[192,128]{1,0:T(8,128)S(1)} %copy-done.15), channel_id=1, source_target_pairs={{16,0},{32,16},{48,32},{64,48},{80,64},{96,80},{112,96},{17,1},{33... | collective-permute-start | bytes 294920 | tf_op jit(solution)/shard_map/ppermute | solution.py:491
  112.4 6.7 %collective-permute-start.7 = (f32[192,128]{1,0:T(8,128)S(1)}, f32[192,128]{1,0:T(8,128)S(1)}, u32[]{:S(2)}, u32[]{:S(2)}) collective-permute-start(f32[192,128]{1,0:T(8,128)S(1)} %copy-done.14), channel_id=1, source_target_pairs={{0,16},{16,32},{32,48},{48,64},{64,80},{80,96},{96,112},{1,17},{17... | collective-permute-start | bytes 294920 | tf_op jit(solution)/shard_map/ppermute | solution.py:491

commit v7 on v6

--- a/solution.py
+++ b/solution.py
@@ -399,11 +399,9 @@
     closure_step(BLOCK, got_ref, owner, mask, planes, split_weights, down, rows_ref, total, then)
 
 
-def early_kernel(got_ref, owner_ref, mask_ref, fx_ref, fy_ref, part_ref, before_ref, *refs):
-    halos, sources, refs = refs[:4], refs[4:12], refs[12:]
-    (lam_far, down_far, grads_ref), sides, refs = refs[:3], refs[3:7], refs[7:]
-    targets, (rows_ref, lam, down, total, sems, out_sems) = refs[:8], refs[8:]
-    wait = bring(zip(("weights",) * 8, sources, targets), sems)
+def early_kernel(got_ref, fx_ref, fy_ref, part_ref, before_ref, owner_ref, mask_ref, *refs):
+    split_weights, halos, refs = refs[:8], refs[8:12], refs[12:]
+    (lam_far, down_far, grads_ref), sides, (rows_ref, lam, down, total, out_sems) = refs[:3], refs[3:7], refs[7:]
     hn_ref, hs_ref, hw_ref, he_ref = halos
     for x in range(CX):
         halo = halo_lanes(x, hw_ref, he_ref)
@@ -419,34 +417,32 @@
     total[...] = before_ref[...]
 
     def then(name):
-        wait(name)
         if name == "out":
             down_copy.start()
 
-    closure_step(0, got_ref, owner_ref, mask_ref, lam, targets, down, rows_ref, total, then)
+    closure_step(0, got_ref, owner_ref, mask_ref, lam, split_weights, down, rows_ref, total, then)
     grads_ref[: 2 * HID, :] = total[:, :128]
     grads_ref[2 * HID :, :] = total[:, 128:]
     lam_copy.wait()
     down_copy.wait()
 
 
-WEIGHT_SCRATCH = [near(*shape, dtype=BF) for shape in WEIGHTS] + [near(HID, 1), near(PAD, 1)]
+TILE_WEIGHTS = [near(CX, CY, dtype=jnp.int32)] * 2
+TILE_WEIGHTS += [near(*shape, dtype=BF) for shape in WEIGHTS] + [near(HID, 1), near(PAD, 1)]
 ROWS = near(FEATS, STORE, dtype=BF)
-TOTAL = near(2 * HID, HID)
 
 
 def late_closure(got, *copied):
-    scratch = [near(CX, CY, dtype=jnp.int32)] * 2 + WEIGHT_SCRATCH
-    scratch += [near(*PLANE), near(*PLANE), ROWS, near(*PLANE), pltpu.SemaphoreType.DMA((12,))]
-    return call(late_kernel, "closure1", (near(*PLANE), TOTAL), (got,), copied, scratch, CLOSURE_MIB)
-
-
-def early_closure(got, owners, mask, fx, fy, part, before, halos, split_weights):
+    outs = (near(*PLANE), near(2 * HID, HID), *TILE_WEIGHTS)
+    scratch = [near(*PLANE), near(*PLANE), ROWS, near(*PLANE), pltpu.SemaphoreType.DMA((12,))]
+    return call(late_kernel, "closure1", outs, (got,), copied, scratch, CLOSURE_MIB)
+
+
+def early_closure(got, fx, fy, part, before, brought, halos):
     outs = ([far(*PLANE)], [far(*PLANE)], far(4 * HID, 128), EDGE, EDGE, EDGE, EDGE)
-    scratch = WEIGHT_SCRATCH + [ROWS, near(*PLANE), near(*PLANE), TOTAL]
-    scratch += [pltpu.SemaphoreType.DMA((8,)), pltpu.SemaphoreType.DMA((2,))]
-    args = (got, owners, mask, fx, fy, part, before, *halos)
-    return call(early_kernel, "closure0", outs, args, split_weights, scratch, CLOSURE_MIB)
+    scratch = [ROWS, near(*PLANE), near(*PLANE), near(2 * HID, HID), pltpu.SemaphoreType.DMA((2,))]
+    args = (got, fx, fy, part, before, *brought, *halos)
+    return call(early_kernel, "closure0", outs, args, (), scratch, CLOSURE_MIB)
 
 
 def sum_kernel(parts_ref, out_ref):
@@ -516,10 +512,8 @@
         costate.reshape(TRACERS * NZ * CX, CY), land_mask, flow_x, flow_y
     )
     halos = exchange("gx", north, south) + exchange("gy", west, east)
-    part, grads = late_closure(got, owners, land_mask, *split_weights, planes, base)
-    lam, down, packed, north, south, west, east = early_closure(
-        got, owners, land_mask, flow_x, flow_y, part, grads, halos, split_weights
-    )
+    part, grads, *brought = late_closure(got, owners, land_mask, *split_weights, planes, base)
+    lam, down, packed, north, south, west, east = early_closure(got, flow_x, flow_y, part, grads, brought, halos)
     halos_y = exchange("gy", west, east)
     spread = reduce_params(packed, halos_y)
     north, south, spread = lax.optimization_barrier((north, south, spread))

time: 125 us -> 125 us (level)
    unnamed x33 -> x27, local copies, waits for them, and re-layouts: 5.38 us -> 5.37 us
where the time goes in v7:
time: 125 us; the launch traced here: 124 us
  starting transfers between devices  45.4 us (36%)
  Pallas kernels  39.3 us (31%)
  waiting for transfers between devices  33.1 us (26%)
  local copies, waits for them, and re-layouts  5.37 us (4%)
    pallas_call x8, Pallas kernels, call(): pl.pallas_call(kernel, out_shape=tuple((out[0] if isinstance(out, list) e...  33.4 us
    ppermute x8, starting transfers between devices, exchange(): return (lax.ppermute(before, axis, down), lax.ppermute(after, axis, up))  21.9 us
    all_to_all x1, waiting for transfers between devices, on_device(): lax.all_to_all(payload, ('gx', 'gy'), split_axis=0, concat_axis=0, tiled=...  21.2 us
    all_to_all x1, starting transfers between devices, on_device(): lax.all_to_all(payload, ('gx', 'gy'), split_axis=0, concat_axis=0, tiled=...  11.5 us
    all_to_all x1, starting transfers between devices, finish_params(): lax.all_to_all(spread, ('gx', 'gy'), split_axis=0, concat_axis=0, tiled=T...  6.67 us
    pallas_call x1, Pallas kernels, pack(): pl.pallas_call(pack_kernel, out_shape=pltpu.HBM((DEV, 2 * BLOCK, 128), BF...  5.96 us
    unnamed x27, local copies, waits for them, and re-layouts  5.37 us
    all_to_all x1, starting transfers between devices, reduce_params(): lax.all_to_all(packed, ('gx', 'gy'), split_axis=0, concat_axis=0, tiled=T...  5.33 us
  transfers between devices with their start and end apart: 11, of which 4 were waited for; matrix products, arithmetic and copies ran while one was open for 1% of the time, Pallas kernels for 16%

profile of v7, /device:TPU:1, one launch (start us, length us, event | category | flops | bytes accessed | tf_op | source)
XLA Modules:
  0.0 124.1 jit_solution(10038097277520854153)
XLA Ops:
  0.6 6.0 %pack.1 = bf16[128,96,128]{2,1,0:T(8,128)(2,1)} custom-call(s32[1,128]{1,0:T(1,128)} %counts_ref.1, bf16[360,4096]{1,0:T(8,128)(2,1)} %bitcast.25), custom_call_target="tpu_custom_call" | custom-call | tf_op jit(solution)/shard_map/pack/pallas_call | solution.py:143
  6.6 0.0 copy-start.4
  6.6 0.0 copy-start.5
  6.6 11.5 %all-to-all-start = ((bf16[128,96,128]{2,1,0:T(8,128)(2,1)}), bf16[128,96,128]{2,1,0:T(8,128)(2,1)S(1)}, u32[]{:S(2)}, u32[]{:S(2)}) async-start(bf16[128,96,128]{2,1,0:T(8,128)(2,1)} %pack.1), calls=%async_computation | async-start | bytes 6291456 | tf_op jit(solution)/shard_map/all_to_all | solution.py:507
  18.2 1.4 %copy-done = f32[3,60,16,128]{3,2,1,0:T(8,128)S(1)} copy-done((f32[3,60,16,128]{3,2,1,0:T(8,128)S(1)}, f32[3,60,16,128]{3,2,1,0:T(8,128)}, u32[]{:S(2)}) %copy-start) | copy-done | bytes 1474584
  19.6 3.1 %edges.1 = (f32[16,192,128]{2,1,0:T(8,128)}, f32[16,192,128]{2,1,0:T(8,128)}, f32[192,128]{1,0:T(8,128)}, f32[192,128]{1,0:T(8,128)}, f32[192,128]{1,0:T(8,128)}, /*index=5*/f32[192,128]{1,0:T(8,128)}) custom-call(f32[2880,128]{1,0:T(8,128)S(1)} %bitcast.20, s32[16,128]{1,0:T(8,128)S(1)} %copy-done.5, f32[16,128]{1,0:T(8,128)S(1)} %copy-done.3, ...), custom_call_target="tpu_custom_call" | custom-call | tf_op jit(solution)/shard_map/edges/pallas_call | solution.py:80
  22.7 3.0 %collective-permute-start = (f32[192,128]{1,0:T(8,128)}, f32[192,128]{1,0:T(8,128)S(1)}, u32[]{:S(2)}, u32[]{:S(2)}) collective-permute-start(f32[192,128]{1,0:T(8,128)} %get-tuple-element.81), channel_id=1, source_target_pairs={{16,0},{32,16},{48,32},{64,48},{80,64},{96,80},{112,96},{17,1},{33... | collective-permute-start | bytes 294920 | tf_op jit(solution)/shard_map/ppermute | solution.py:487
  25.7 2.6 %collective-permute-start.1 = (f32[192,128]{1,0:T(8,128)}, f32[192,128]{1,0:T(8,128)S(1)}, u32[]{:S(2)}, u32[]{:S(2)}) collective-permute-start(f32[192,128]{1,0:T(8,128)} %get-tuple-element.82), channel_id=1, source_target_pairs={{0,16},{16,32},{32,48},{48,64},{64,80},{80,96},{96,112},{1,17},{17... | collective-permute-start | bytes 294920 | tf_op jit(solution)/shard_map/ppermute | solution.py:487
  28.3 1.3 %collective-permute-start.2 = (f32[192,128]{1,0:T(8,128)}, f32[192,128]{1,0:T(8,128)S(1)}, u32[]{:S(2)}, u32[]{:S(2)}) collective-permute-start(f32[192,128]{1,0:T(8,128)} %get-tuple-element.83), channel_id=1, source_target_pairs={{1,0},{2,1},{3,2},{4,3},{5,4},{6,5},{7,6},{8,7},{9,8},{10,9},{11,1... | collective-permute-start | bytes 294920 | tf_op jit(solution)/shard_map/ppermute | solution.py:487
  29.6 4.2 %collective-permute-start.3 = (f32[192,128]{1,0:T(8,128)}, f32[192,128]{1,0:T(8,128)S(1)}, u32[]{:S(2)}, u32[]{:S(2)}) collective-permute-start(f32[192,128]{1,0:T(8,128)} %get-tuple-element.84), channel_id=1, source_target_pairs={{0,1},{1,2},{2,3},{3,4},{4,5},{5,6},{6,7},{7,8},{8,9},{9,10},{10,1... | collective-permute-start | bytes 294920 | tf_op jit(solution)/shard_map/ppermute | solution.py:487
  33.8 0.8 copy-done.7
  34.6 0.7 copy-done.8
  35.3 0.7 copy-done.9
  36.0 0.7 copy-done.10
  36.6 1.2 weights.1
  37.8 21.2 %all-to-all-done.got_ref = bf16[128,96,128]{2,1,0:T(8,128)(2,1)S(1)} async-done(((bf16[128,96,128]{2,1,0:T(8,128)(2,1)}), bf16[128,96,128]{2,1,0:T(8,128)(2,1)S(1)}, u32[]{:S(2)}, u32[]{:S(2)}) %all-to-all-start) | async-done | bytes 3145760 | tf_op jit(solution)/shard_map/all_to_all | solution.py:507
  59.1 11.5 %closure1.1 = (f32[16,192,128]{2,1,0:T(8,128)S(1)}, f32[512,256]{1,0:T(8,128)S(1)}, s32[16,128]{1,0:T(8,128)S(1)}, s32[16,128]{1,0:T(8,128)S(1)}, bf16[512,192]{...) custom-call(bf16[128,96,128]{2,1,0:T(8,128)(2,1)S(1)} %all-to-all-do, ...), custom_call_target="tpu_custom_call" | custom-call | tf_op jit(solution)/shard_map/closure1/pallas_call | solution.py:80
  70.6 11.4 %closure0.1 = (f32[16,192,128]{2,1,0:T(8,128)}, f32[16,192,128]{2,1,0:T(8,128)}, f32[1024,128]{1,0:T(8,128)}, f32[192,128]{1,0:T(8,128)}, f32[192,128]{1,0:T(8,1...) custom-call(bf16[128,96,128]{2,1,0:T(8,128)(2,1)S(1)} %all-to-all-done.got_ref, f32[16,128]{1,0:T(8,128)S(1)} %copy-done.3, ...), custom_call_target="tpu_custom_call" | custom-call | tf_op jit(solution)/shard_map/closure0/pallas_call | solution.py:80
  82.1 5.3 %all-to-all-start.1 = ((f32[128,8,128]{2,1,0:T(8,128)}), f32[128,8,128]{2,1,0:T(8,128)S(1)}, u32[]{:S(2)}, u32[]{:S(2)}) async-start(f32[128,8,128]{2,1,0:T(8,128)} %bitcast.27), calls=%async_computation.1 | async-start | bytes 1048576 | tf_op jit(solution)/shard_map/all_to_all | solution.py:470
  87.4 1.3 %collective-permute-start.4 = (f32[192,128]{1,0:T(8,128)}, f32[192,128]{1,0:T(8,128)S(1)}, u32[]{:S(2)}, u32[]{:S(2)}) collective-permute-start(f32[192,128]{1,0:T(8,128)} %get-tuple-element.85), channel_id=1, source_target_pairs={{1,0},{2,1},{3,2},{4,3},{5,4},{6,5},{7,6},{8,7},{9,8},{10,9},{11,1... | collective-permute-start | bytes 294920 | tf_op jit(solution)/shard_map/ppermute | solution.py:487
  88.7 4.0 %collective-permute-start.5 = (f32[192,128]{1,0:T(8,128)}, f32[192,128]{1,0:T(8,128)S(1)}, u32[]{:S(2)}, u32[]{:S(2)}) collective-permute-start(f32[192,128]{1,0:T(8,128)} %get-tuple-element.86), channel_id=1, source_target_pairs={{0,1},{1,2},{2,3},{3,4},{4,5},{5,6},{6,7},{7,8},{8,9},{9,10},{10,1... | collective-permute-start | bytes 294920 | tf_op jit(solution)/shard_map/ppermute | solution.py:487
  92.7 3.9 %collective-permute-done.4.hw_ref = f32[192,128]{1,0:T(8,128)S(1)} collective-permute-done((f32[192,128]{1,0:T(8,128)}, f32[192,128]{1,0:T(8,128)S(1)}, u32[]{:S(2)}, u32[]{:S(2)}) %collective-permute-start.4) | collective-permute-done | bytes 98336 | tf_op jit(solution)/shard_map/ppermute | solution.py:487
  96.6 4.9 %all-to-all-done.1 = f32[128,8,128]{2,1,0:T(8,128)S(1)} async-done(((f32[128,8,128]{2,1,0:T(8,128)}), f32[128,8,128]{2,1,0:T(8,128)S(1)}, u32[]{:S(2)}, u32[]{:S(2)}) %all-to-all-start.1) | async-done | bytes 524320 | tf_op jit(solution)/shard_map/all_to_all | solution.py:470
  101.5 1.0 sum.1
  102.5 6.7 %all-to-all-start.2 = ((f32[128,8,128]{2,1,0:T(8,128)}), f32[128,8,128]{2,1,0:T(8,128)S(1)}, u32[]{:S(2)}, u32[]{:S(2)}) async-start(f32[128,8,128]{2,1,0:T(8,128)} %bitcast.26), calls=%async_computation.2 | async-start | bytes 1048576 | tf_op jit(solution)/shard_map/all_to_all | solution.py:477
  109.2 3.0 %collective-permute-start.6 = (f32[192,128]{1,0:T(8,128)S(1)}, f32[192,128]{1,0:T(8,128)S(1)}, u32[]{:S(2)}, u32[]{:S(2)}) collective-permute-start(f32[192,128]{1,0:T(8,128)S(1)} %copy-done.12), channel_id=1, source_target_pairs={{16,0},{32,16},{48,32},{64,48},{80,64},{96,80},{112,96},{17,1},{33... | collective-permute-start | bytes 294920 | tf_op jit(solution)/shard_map/ppermute | solution.py:487
  112.2 2.6 %collective-permute-start.7 = (f32[192,128]{1,0:T(8,128)S(1)}, f32[192,128]{1,0:T(8,128)S(1)}, u32[]{:S(2)}, u32[]{:S(2)}) collective-permute-start(f32[192,128]{1,0:T(8,128)S(1)} %copy-done.11), channel_id=1, source_target_pairs={{0,16},{16,32},{32,48},{48,64},{64,80},{80,96},{96,112},{1,17},{17... | collective-permute-start | bytes 294920 | tf_op jit(solution)/shard_map/ppermute | solution.py:487
  114.8 4.1 %stencil0.1.part_ref = f32[2880,128]{1,0:T(8,128)S(1)} custom-call(s32[16,128]{1,0:T(8,128)S(1)} %copy-done.6, f32[16,128]{1,0:T(8,128)S(1)} %copy-done.3, f32[16,128]{1,0:T(8,128)S(1)} %copy-done.4, f32[192,128]{1,0:T(8,128)S(1)} %collective-permute-done.4.hw_ref, f32[192,128]{1,0:T(8,128)S(1)} %collective-permute-done.5.he_ref, ...), custom_call_target="tpu_custom_call" | custom-call | tf_op jit(solution)/shard_map/stencil0/pallas_call | solution.py:80
  119.0 0.2 rows0.1
  119.2 1.1 copy.22
  120.3 3.0 %all-to-all-done.2 = f32[128,8,128]{2,1,0:T(8,128)S(1)} async-done(((f32[128,8,128]{2,1,0:T(8,128)}), f32[128,8,128]{2,1,0:T(8,128)S(1)}, u32[]{:S(2)}, u32[]{:S(2)}) %all-to-all-start.2) | async-done | bytes 524320 | tf_op jit(solution)/shard_map/all_to_all | solution.py:477
  123.3 0.8 unpack.1
  (26 shorter events, 0.1 us)
Async XLA Ops:
  6.6 11.6 %copy-start.3 = (f32[16,128]{1,0:T(8,128)S(1)}, f32[16,128]{1,0:T(8,128)}, u32[]{:S(2)}) copy-start(f32[16,128]{1,0:T(8,128)} %fx_ref.5) | copy-start | bytes 24580
  6.6 11.6 %copy-start.4 = (f32[16,128]{1,0:T(8,128)S(1)}, f32[16,128]{1,0:T(8,128)}, u32[]{:S(2)}) copy-start(f32[16,128]{1,0:T(8,128)} %fy_ref.5) | copy-start | bytes 24580
  6.6 11.6 %copy-start.5 = (s32[16,128]{1,0:T(8,128)S(1)}, s32[16,128]{1,0:T(8,128)}, u32[]{:S(2)}) copy-start(s32[16,128]{1,0:T(8,128)} %mask_ref.3) | copy-start | bytes 24580
  6.6 52.4 %all-to-all-start = ((bf16[128,96,128]{2,1,0:T(8,128)(2,1)}), bf16[128,96,128]{2,1,0:T(8,128)(2,1)S(1)}, u32[]{:S(2)}, u32[]{:S(2)}) async-start(bf16[128,96,128]{2,1,0:T(8,128)(2,1)} %pack.1), calls=%async_computation | async-start | bytes 6291456 | tf_op jit(solution)/shard_map/all_to_all | solution.py:507
  18.2 1.4 %copy-start = (f32[3,60,16,128]{3,2,1,0:T(8,128)S(1)}, f32[3,60,16,128]{3,2,1,0:T(8,128)}, u32[]{:S(2)}) copy-start(f32[3,60,16,128]{3,2,1,0:T(8,128)} %param.19) | copy-start | bytes 4423684
  19.6 14.2 %copy-start.1 = (f32[256,256]{1,0:T(8,128)S(1)}, f32[256,256]{1,0:T(8,128)}, u32[]{:S(2)}) copy-start(f32[256,256]{1,0:T(8,128)} %w2_ref) | copy-start | bytes 786436
  19.6 14.2 %copy-start.2 = (f32[180,256]{1,0:T(8,128)S(1)}, f32[180,256]{1,0:T(8,128)}, u32[]{:S(2)}) copy-start(f32[180,256]{1,0:T(8,128)} %w1_ref.1) | copy-start | bytes 552964
  22.7 47.9 %collective-permute-start = (f32[192,128]{1,0:T(8,128)}, f32[192,128]{1,0:T(8,128)S(1)}, u32[]{:S(2)}, u32[]{:S(2)}) collective-permute-start(f32[192,128]{1,0:T(8,128)} %get-tuple-element.81), channel_id=1, source_target_pairs={{16,0},{32,16},{48,32},{64,48},{80,64},{96,80},{112,96},{17,1},{33... | collective-permute-start | bytes 294920 | tf_op jit(solution)/shard_map/ppermute | solution.py:487
  25.7 44.9 %collective-permute-start.1 = (f32[192,128]{1,0:T(8,128)}, f32[192,128]{1,0:T(8,128)S(1)}, u32[]{:S(2)}, u32[]{:S(2)}) collective-permute-start(f32[192,128]{1,0:T(8,128)} %get-tuple-element.82), channel_id=1, source_target_pairs={{0,16},{16,32},{32,48},{48,64},{64,80},{80,96},{96,112},{1,17},{17... | collective-permute-start | bytes 294920 | tf_op jit(solution)/shard_map/ppermute | solution.py:487
  28.3 42.3 %collective-permute-start.2 = (f32[192,128]{1,0:T(8,128)}, f32[192,128]{1,0:T(8,128)S(1)}, u32[]{:S(2)}, u32[]{:S(2)}) collective-permute-start(f32[192,128]{1,0:T(8,128)} %get-tuple-element.83), channel_id=1, source_target_pairs={{1,0},{2,1},{3,2},{4,3},{5,4},{6,5},{7,6},{8,7},{9,8},{10,9},{11,1... | collective-permute-start | bytes 294920 | tf_op jit(solution)/shard_map/ppermute | solution.py:487
  29.6 41.0 %collective-permute-start.3 = (f32[192,128]{1,0:T(8,128)}, f32[192,128]{1,0:T(8,128)S(1)}, u32[]{:S(2)}, u32[]{:S(2)}) collective-permute-start(f32[192,128]{1,0:T(8,128)} %get-tuple-element.84), channel_id=1, source_target_pairs={{0,1},{1,2},{2,3},{3,4},{4,5},{5,6},{6,7},{7,8},{8,9},{9,10},{10,1... | collective-permute-start | bytes 294920 | tf_op jit(solution)/shard_map/ppermute | solution.py:487
  33.8 0.8 copy-start.7
  34.6 0.7 copy-start.8
  35.3 0.7 copy-start.9
  36.0 0.7 copy-start.10
  82.0 27.2 %copy-start.12 = (f32[192,128]{1,0:T(8,128)S(1)}, f32[192,128]{1,0:T(8,128)}, u32[]{:S(2)}) copy-start(f32[192,128]{1,0:T(8,128)} %get-tuple-element.96) | copy-start | bytes 294916
  82.0 30.1 %copy-start.11 = (f32[192,128]{1,0:T(8,128)S(1)}, f32[192,128]{1,0:T(8,128)}, u32[]{:S(2)}) copy-start(f32[192,128]{1,0:T(8,128)} %get-tuple-element.97) | copy-start | bytes 294916
  82.1 32.7 %copy-start.6 = (s32[16,128]{1,0:T(8,128)S(1)}, s32[16,128]{1,0:T(8,128)}, u32[]{:S(2)}) copy-start(s32[16,128]{1,0:T(8,128)} %mask_ref.3) | copy-start | bytes 24580
  82.1 19.5 %all-to-all-start.1 = ((f32[128,8,128]{2,1,0:T(8,128)}), f32[128,8,128]{2,1,0:T(8,128)S(1)}, u32[]{:S(2)}, u32[]{:S(2)}) async-start(f32[128,8,128]{2,1,0:T(8,128)} %bitcast.27), calls=%async_computation.1 | async-start | bytes 1048576 | tf_op jit(solution)/shard_map/all_to_all | solution.py:470
  87.4 9.2 %collective-permute-start.4 = (f32[192,128]{1,0:T(8,128)}, f32[192,128]{1,0:T(8,128)S(1)}, u32[]{:S(2)}, u32[]{:S(2)}) collective-permute-start(f32[192,128]{1,0:T(8,128)} %get-tuple-element.85), channel_id=1, source_target_pairs={{1,0},{2,1},{3,2},{4,3},{5,4},{6,5},{7,6},{8,7},{9,8},{10,9},{11,1... | collective-permute-start | bytes 294920 | tf_op jit(solution)/shard_map/ppermute | solution.py:487
  88.7 7.9 %collective-permute-start.5 = (f32[192,128]{1,0:T(8,128)}, f32[192,128]{1,0:T(8,128)S(1)}, u32[]{:S(2)}, u32[]{:S(2)}) collective-permute-start(f32[192,128]{1,0:T(8,128)} %get-tuple-element.86), channel_id=1, source_target_pairs={{0,1},{1,2},{2,3},{3,4},{4,5},{5,6},{6,7},{7,8},{8,9},{9,10},{10,1... | collective-permute-start | bytes 294920 | tf_op jit(solution)/shard_map/ppermute | solution.py:487
  102.5 20.8 %all-to-all-start.2 = ((f32[128,8,128]{2,1,0:T(8,128)}), f32[128,8,128]{2,1,0:T(8,128)S(1)}, u32[]{:S(2)}, u32[]{:S(2)}) async-start(f32[128,8,128]{2,1,0:T(8,128)} %bitcast.26), calls=%async_computation.2 | async-start | bytes 1048576 | tf_op jit(solution)/shard_map/all_to_all | solution.py:477
  109.2 9.7 %collective-permute-start.6 = (f32[192,128]{1,0:T(8,128)S(1)}, f32[192,128]{1,0:T(8,128)S(1)}, u32[]{:S(2)}, u32[]{:S(2)}) collective-permute-start(f32[192,128]{1,0:T(8,128)S(1)} %copy-done.12), channel_id=1, source_target_pairs={{16,0},{32,16},{48,32},{64,48},{80,64},{96,80},{112,96},{17,1},{33... | collective-permute-start | bytes 294920 | tf_op jit(solution)/shard_map/ppermute | solution.py:487
  112.2 6.8 %collective-permute-start.7 = (f32[192,128]{1,0:T(8,128)S(1)}, f32[192,128]{1,0:T(8,128)S(1)}, u32[]{:S(2)}, u32[]{:S(2)}) collective-permute-start(f32[192,128]{1,0:T(8,128)S(1)} %copy-done.11), channel_id=1, source_target_pairs={{0,16},{16,32},{32,48},{48,64},{64,80},{80,96},{96,112},{1,17},{17... | collective-permute-start | bytes 294920 | tf_op jit(solution)/shard_map/ppermute | solution.py:487

commit v8 on v7

--- a/solution.py
+++ b/solution.py
@@ -20,7 +20,8 @@
 CY = 128
 DEV = 128
 STORE = 4096
-UNROLL = 16
+UNROLL = DEV // 8
+BATCH = 4
 COLS = CX * CY
 
 CLOSURE_MIB = 24
@@ -90,19 +91,20 @@
 
 
 def pack_kernel(counts_ref, stored_ref, out_ref, near, padded, rows_out, in_sems, out_sem):
-    cut = (FEATS - TRACERS * (PAD - NZ) + 7) // 8 * 8
-    parts = (slice(0, cut), slice(cut, 2 * TRACERS * NZ))
-    copies = [pltpu.make_async_copy(stored_ref.at[p, :], near.at[p, :], in_sems.at[i]) for i, p in enumerate(parts)]
+    cut = STORE // 2 + 128
+    parts = (slice(0, cut), slice(cut, STORE))
+    copies = [pltpu.make_async_copy(stored_ref.at[:, p], near.at[:, p], in_sems.at[i]) for i, p in enumerate(parts)]
     for copy in copies:
         copy.start()
     lane = lax.broadcasted_iota(jnp.int32, (SLOT, 256), 1)
     offset = lane - lax.broadcasted_iota(jnp.int32, (SLOT, 256), 0)
     for block in range(2 * TRACERS):
         padded[block * PAD + NZ : (block + 1) * PAD, :] = jnp.zeros((PAD - NZ, STORE), BF)
-    for moment in range(2):
-        copies[moment].wait()
-        for block in range(moment * TRACERS, (moment + 1) * TRACERS):
-            padded[block * PAD : block * PAD + NZ, :] = near[block * NZ : (block + 1) * NZ, :]
+
+    def arrive(half):
+        copies[half].wait()
+        for block in range(2 * TRACERS):
+            padded[block * PAD : block * PAD + NZ, parts[half]] = near[block * NZ : (block + 1) * NZ, parts[half]]
 
     def group(g, start):
         base = pl.multiple_of(jnp.minimum((start // 128) * 128, STORE - 256), 128)
@@ -121,20 +123,20 @@
         return start
 
     def leave(j):
-        tiles = pl.ds(j * 4 * UNROLL, 4 * UNROLL)
+        tiles = pl.ds(j * 4 * BATCH, 4 * BATCH)
         return pltpu.make_async_copy(rows_out.at[tiles], out_ref.at[tiles], out_sem.at[j])
 
-    start = jnp.int32(0)
-    steps = DEV // 4 // UNROLL
-
-    def groups(j, start):
+    def groups(half, start):
+        pl.when(half == 0)(functools.partial(arrive, 0))
+        pl.when(half == 1)(functools.partial(arrive, 1))
         for u in range(UNROLL):
-            start = group(j * UNROLL + u, start)
-        leave(j).start()
+            start = group(half * UNROLL + u, start)
+            if u % BATCH == BATCH - 1:
+                leave(half * (UNROLL // BATCH) + u // BATCH).start()
         return start
 
-    lax.fori_loop(0, steps, groups, start)
-    for j in range(steps):
+    lax.fori_loop(0, 2, groups, jnp.int32(0))
+    for j in range(DEV // 4 // BATCH):
         leave(j).wait()
 
 
@@ -150,7 +152,7 @@
             pltpu.VMEM((2 * FEATS, STORE), BF),
             pltpu.VMEM((DEV, 2 * BLOCK, 128), BF),
             pltpu.SemaphoreType.DMA((2,)),
-            pltpu.SemaphoreType.DMA((DEV // 4 // UNROLL,)),
+            pltpu.SemaphoreType.DMA((DEV // 4 // BATCH,)),
         ],
         compiler_params=params(24),
         name="pack",
@@ -466,9 +468,8 @@
     b3_ref[...] = sums_ref[NZ + 2 : NZ + 3, :NZ] * scale
 
 
-def reduce_params(packed, tied):
+def reduce_params(packed):
     parts = lax.all_to_all(packed, ("gx", "gy"), split_axis=0, concat_axis=0, tiled=True)
-    parts, _ = lax.optimization_barrier((parts, tied))
     (spread,) = call(sum_kernel, "sum", (far(*packed.shape),), (parts,))
     return spread
 
@@ -515,8 +516,8 @@
     part, grads, *brought = late_closure(got, owners, land_mask, *split_weights, planes, base)
     lam, down, packed, north, south, west, east = early_closure(got, flow_x, flow_y, part, grads, brought, halos)
     halos_y = exchange("gy", west, east)
-    spread = reduce_params(packed, halos_y)
-    north, south, spread = lax.optimization_barrier((north, south, spread))
+    spread = reduce_params(packed)
+    north, south, spread, halos_y = lax.optimization_barrier((north, south, spread, halos_y))
     halos_x = exchange("gx", north, south)
     lam, down, spread = lax.optimization_barrier((lam, down, spread))
     adjoint = last_stencil(lam, down, land_mask, flow_x, flow_y, *halos_y)

time: 125 us -> 123 us (0.984)
    all_to_all x1, waiting for transfers between devices: 4.9 us -> 8.82 us  [reduce_params(): lax.all_to_all(packed, ('gx', 'gy'), split_axis=0, concat_axis=0, tiled=T...]
    ppermute x8, waiting for transfers between devices: 3.93 us -> 0.02 us  [exchange(): return (lax.ppermute(before, axis, down), lax.ppermute(after, axis, up))]
  transfers between devices with their start and end apart: 11 -> 11, of which waited for: 4 -> 3; matrix products, arithmetic and copies ran while one was open for 1% -> 1% of each run, Pallas kernels for 16% -> 17%
where the time goes in v8:
time: 123 us
  starting transfers between devices  44.4 us (36%)
  Pallas kernels  38.7 us (31%)
  waiting for transfers between devices  33.1 us (27%)
  local copies, waits for them, and re-layouts  5.37 us (4%)
    pallas_call x8, Pallas kernels, call(): pl.pallas_call(kernel, out_shape=tuple((out[0] if isinstance(out, list) e...  33.3 us
    ppermute x8, starting transfers between devices, exchange(): return (lax.ppermute(before, axis, down), lax.ppermute(after, axis, up))  21.9 us
    all_to_all x1, waiting for transfers between devices, on_device(): lax.all_to_all(payload, ('gx', 'gy'), split_axis=0, concat_axis=0, tiled=...  21.2 us
    all_to_all x1, starting transfers between devices, on_device(): lax.all_to_all(payload, ('gx', 'gy'), split_axis=0, concat_axis=0, tiled=...  11.5 us
    all_to_all x1, waiting for transfers between devices, reduce_params(): lax.all_to_all(packed, ('gx', 'gy'), split_axis=0, concat_axis=0, tiled=T...  8.82 us
    all_to_all x1, starting transfers between devices, finish_params(): lax.all_to_all(spread, ('gx', 'gy'), split_axis=0, concat_axis=0, tiled=T...  5.68 us
    unnamed x27, local copies, waits for them, and re-layouts  5.37 us
    pallas_call x1, Pallas kernels, pack(): pl.pallas_call(pack_kernel, out_shape=pltpu.HBM((DEV, 2 * BLOCK, 128), BF...  5.35 us
  transfers between devices with their start and end apart: 11, of which 3 were waited for; matrix products, arithmetic and copies ran while one was open for 1% of the time, Pallas kernels for 17%

profile of v8, /device:TPU:1, one launch (start us, length us, event | category | flops | bytes accessed | tf_op | source)
XLA Modules:
  0.0 122.5 jit_solution(5802129340430925679)
XLA Ops:
  0.6 5.4 %pack.1 = bf16[128,96,128]{2,1,0:T(8,128)(2,1)} custom-call(s32[1,128]{1,0:T(1,128)} %counts_ref.1, bf16[360,4096]{1,0:T(8,128)(2,1)} %bitcast.25), custom_call_target="tpu_custom_call" | custom-call | tf_op jit(solution)/shard_map/pack/pallas_call | solution.py:145
  6.0 0.0 copy-start.3
  6.0 0.0 copy-start.4
  6.0 11.5 %all-to-all-start = ((bf16[128,96,128]{2,1,0:T(8,128)(2,1)}), bf16[128,96,128]{2,1,0:T(8,128)(2,1)S(1)}, u32[]{:S(2)}, u32[]{:S(2)}) async-start(bf16[128,96,128]{2,1,0:T(8,128)(2,1)} %pack.1), calls=%async_computation | async-start | bytes 6291456 | tf_op jit(solution)/shard_map/all_to_all | solution.py:508
  17.6 0.0 copy-start
  17.6 1.4 %copy-done = f32[3,60,16,128]{3,2,1,0:T(8,128)S(1)} copy-done((f32[3,60,16,128]{3,2,1,0:T(8,128)S(1)}, f32[3,60,16,128]{3,2,1,0:T(8,128)}, u32[]{:S(2)}) %copy-start) | copy-done | bytes 1474584
  18.9 3.1 %edges.1 = (f32[16,192,128]{2,1,0:T(8,128)}, f32[16,192,128]{2,1,0:T(8,128)}, f32[192,128]{1,0:T(8,128)}, f32[192,128]{1,0:T(8,128)}, f32[192,128]{1,0:T(8,128)}, /*index=5*/f32[192,128]{1,0:T(8,128)}) custom-call(f32[2880,128]{1,0:T(8,128)S(1)} %bitcast.20, s32[16,128]{1,0:T(8,128)S(1)} %copy-done.5, f32[16,128]{1,0:T(8,128)S(1)} %copy-done.3, ...), custom_call_target="tpu_custom_call" | custom-call | tf_op jit(solution)/shard_map/edges/pallas_call | solution.py:81
  22.1 3.0 %collective-permute-start = (f32[192,128]{1,0:T(8,128)}, f32[192,128]{1,0:T(8,128)S(1)}, u32[]{:S(2)}, u32[]{:S(2)}) collective-permute-start(f32[192,128]{1,0:T(8,128)} %get-tuple-element.82), channel_id=1, source_target_pairs={{16,0},{32,16},{48,32},{64,48},{80,64},{96,80},{112,96},{17,1},{33... | collective-permute-start | bytes 294920 | tf_op jit(solution)/shard_map/ppermute | solution.py:488
  25.0 2.6 %collective-permute-start.1 = (f32[192,128]{1,0:T(8,128)}, f32[192,128]{1,0:T(8,128)S(1)}, u32[]{:S(2)}, u32[]{:S(2)}) collective-permute-start(f32[192,128]{1,0:T(8,128)} %get-tuple-element.83), channel_id=1, source_target_pairs={{0,16},{16,32},{32,48},{48,64},{64,80},{80,96},{96,112},{1,17},{17... | collective-permute-start | bytes 294920 | tf_op jit(solution)/shard_map/ppermute | solution.py:488
  27.6 1.3 %collective-permute-start.2 = (f32[192,128]{1,0:T(8,128)}, f32[192,128]{1,0:T(8,128)S(1)}, u32[]{:S(2)}, u32[]{:S(2)}) collective-permute-start(f32[192,128]{1,0:T(8,128)} %get-tuple-element.84), channel_id=1, source_target_pairs={{1,0},{2,1},{3,2},{4,3},{5,4},{6,5},{7,6},{8,7},{9,8},{10,9},{11,1... | collective-permute-start | bytes 294920 | tf_op jit(solution)/shard_map/ppermute | solution.py:488
  28.9 4.2 %collective-permute-start.3 = (f32[192,128]{1,0:T(8,128)}, f32[192,128]{1,0:T(8,128)S(1)}, u32[]{:S(2)}, u32[]{:S(2)}) collective-permute-start(f32[192,128]{1,0:T(8,128)} %get-tuple-element.85), channel_id=1, source_target_pairs={{0,1},{1,2},{2,3},{3,4},{4,5},{5,6},{6,7},{7,8},{8,9},{9,10},{10,1... | collective-permute-start | bytes 294920 | tf_op jit(solution)/shard_map/ppermute | solution.py:488
  33.2 0.8 copy-done.7
  34.0 0.7 copy-done.8
  34.7 0.7 copy-done.9
  35.4 0.7 copy-done.10
  36.0 1.2 weights.1
  37.2 21.2 %all-to-all-done.got_ref = bf16[128,96,128]{2,1,0:T(8,128)(2,1)S(1)} async-done(((bf16[128,96,128]{2,1,0:T(8,128)(2,1)}), bf16[128,96,128]{2,1,0:T(8,128)(2,1)S(1)}, u32[]{:S(2)}, u32[]{:S(2)}) %all-to-all-start) | async-done | bytes 3145760 | tf_op jit(solution)/shard_map/all_to_all | solution.py:508
  58.4 11.5 %closure1.1 = (f32[16,192,128]{2,1,0:T(8,128)S(1)}, f32[512,256]{1,0:T(8,128)S(1)}, s32[16,128]{1,0:T(8,128)S(1)}, s32[16,128]{1,0:T(8,128)S(1)}, bf16[512,192]{...) custom-call(bf16[128,96,128]{2,1,0:T(8,128)(2,1)S(1)} %all-to-all-do, ...), custom_call_target="tpu_custom_call" | custom-call | tf_op jit(solution)/shard_map/closure1/pallas_call | solution.py:81
  70.0 11.4 %closure0.1 = (f32[16,192,128]{2,1,0:T(8,128)}, f32[16,192,128]{2,1,0:T(8,128)}, f32[1024,128]{1,0:T(8,128)}, f32[192,128]{1,0:T(8,128)}, f32[192,128]{1,0:T(8,1...) custom-call(bf16[128,96,128]{2,1,0:T(8,128)(2,1)S(1)} %all-to-all-done.got_ref, f32[16,128]{1,0:T(8,128)S(1)} %copy-done.3, ...), custom_call_target="tpu_custom_call" | custom-call | tf_op jit(solution)/shard_map/closure0/pallas_call | solution.py:81
  81.4 5.3 %all-to-all-start.1 = ((f32[128,8,128]{2,1,0:T(8,128)}), f32[128,8,128]{2,1,0:T(8,128)S(1)}, u32[]{:S(2)}, u32[]{:S(2)}) async-start(f32[128,8,128]{2,1,0:T(8,128)} %bitcast.27), calls=%async_computation.1 | async-start | bytes 1048576 | tf_op jit(solution)/shard_map/all_to_all | solution.py:472
  86.8 1.3 %collective-permute-start.4 = (f32[192,128]{1,0:T(8,128)}, f32[192,128]{1,0:T(8,128)S(1)}, u32[]{:S(2)}, u32[]{:S(2)}) collective-permute-start(f32[192,128]{1,0:T(8,128)} %get-tuple-element.89), channel_id=1, source_target_pairs={{1,0},{2,1},{3,2},{4,3},{5,4},{6,5},{7,6},{8,7},{9,8},{10,9},{11,1... | collective-permute-start | bytes 294920 | tf_op jit(solution)/shard_map/ppermute | solution.py:488
  88.1 4.0 %collective-permute-start.5 = (f32[192,128]{1,0:T(8,128)}, f32[192,128]{1,0:T(8,128)S(1)}, u32[]{:S(2)}, u32[]{:S(2)}) collective-permute-start(f32[192,128]{1,0:T(8,128)} %get-tuple-element.90), channel_id=1, source_target_pairs={{0,1},{1,2},{2,3},{3,4},{4,5},{5,6},{6,7},{7,8},{8,9},{9,10},{10,1... | collective-permute-start | bytes 294920 | tf_op jit(solution)/shard_map/ppermute | solution.py:488
  92.1 8.8 %all-to-all-done.1 = f32[128,8,128]{2,1,0:T(8,128)S(1)} async-done(((f32[128,8,128]{2,1,0:T(8,128)}), f32[128,8,128]{2,1,0:T(8,128)S(1)}, u32[]{:S(2)}, u32[]{:S(2)}) %all-to-all-start.1) | async-done | bytes 524320 | tf_op jit(solution)/shard_map/all_to_all | solution.py:472
  100.9 1.0 sum.1
  101.9 5.7 %all-to-all-start.2 = ((f32[128,8,128]{2,1,0:T(8,128)}), f32[128,8,128]{2,1,0:T(8,128)S(1)}, u32[]{:S(2)}, u32[]{:S(2)}) async-start(f32[128,8,128]{2,1,0:T(8,128)} %bitcast.26), calls=%async_computation.2 | async-start | bytes 1048576 | tf_op jit(solution)/shard_map/all_to_all | solution.py:478
  107.6 3.0 %collective-permute-start.6 = (f32[192,128]{1,0:T(8,128)S(1)}, f32[192,128]{1,0:T(8,128)S(1)}, u32[]{:S(2)}, u32[]{:S(2)}) collective-permute-start(f32[192,128]{1,0:T(8,128)S(1)} %copy-done.12), channel_id=1, source_target_pairs={{16,0},{32,16},{48,32},{64,48},{80,64},{96,80},{112,96},{17,1},{33... | collective-permute-start | bytes 294920 | tf_op jit(solution)/shard_map/ppermute | solution.py:488
  110.6 2.6 %collective-permute-start.7 = (f32[192,128]{1,0:T(8,128)S(1)}, f32[192,128]{1,0:T(8,128)S(1)}, u32[]{:S(2)}, u32[]{:S(2)}) collective-permute-start(f32[192,128]{1,0:T(8,128)S(1)} %copy-done.11), channel_id=1, source_target_pairs={{0,16},{16,32},{32,48},{48,64},{64,80},{80,96},{96,112},{1,17},{17... | collective-permute-start | bytes 294920 | tf_op jit(solution)/shard_map/ppermute | solution.py:488
  113.2 4.1 %stencil0.1.part_ref = f32[2880,128]{1,0:T(8,128)S(1)} custom-call(s32[16,128]{1,0:T(8,128)S(1)} %copy-done.6, f32[16,128]{1,0:T(8,128)S(1)} %copy-done.3, f32[16,128]{1,0:T(8,128)S(1)} %copy-done.4, f32[192,128]{1,0:T(8,128)S(1)} %collective-permute-done.4.hw_ref, f32[192,128]{1,0:T(8,128)S(1)} %collective-permute-done.5.he_ref, ...), custom_call_target="tpu_custom_call" | custom-call | tf_op jit(solution)/shard_map/stencil0/pallas_call | solution.py:81
  117.3 0.2 rows0.1
  117.5 1.1 copy.22
  118.6 3.0 %all-to-all-done.2 = f32[128,8,128]{2,1,0:T(8,128)S(1)} async-done(((f32[128,8,128]{2,1,0:T(8,128)}), f32[128,8,128]{2,1,0:T(8,128)S(1)}, u32[]{:S(2)}, u32[]{:S(2)}) %all-to-all-start.2) | async-done | bytes 524320 | tf_op jit(solution)/shard_map/all_to_all | solution.py:478
  121.7 0.8 unpack.1
  (26 shorter events, 0.1 us)
Async XLA Ops:
  6.0 11.5 %copy-start.3 = (f32[16,128]{1,0:T(8,128)S(1)}, f32[16,128]{1,0:T(8,128)}, u32[]{:S(2)}) copy-start(f32[16,128]{1,0:T(8,128)} %fx_ref.5) | copy-start | bytes 24580
  6.0 11.5 %copy-start.4 = (f32[16,128]{1,0:T(8,128)S(1)}, f32[16,128]{1,0:T(8,128)}, u32[]{:S(2)}) copy-start(f32[16,128]{1,0:T(8,128)} %fy_ref.5) | copy-start | bytes 24580
  6.0 11.5 %copy-start.5 = (s32[16,128]{1,0:T(8,128)S(1)}, s32[16,128]{1,0:T(8,128)}, u32[]{:S(2)}) copy-start(s32[16,128]{1,0:T(8,128)} %mask_ref.3) | copy-start | bytes 24580
  6.0 52.4 %all-to-all-start = ((bf16[128,96,128]{2,1,0:T(8,128)(2,1)}), bf16[128,96,128]{2,1,0:T(8,128)(2,1)S(1)}, u32[]{:S(2)}, u32[]{:S(2)}) async-start(bf16[128,96,128]{2,1,0:T(8,128)(2,1)} %pack.1), calls=%async_computation | async-start | bytes 6291456 | tf_op jit(solution)/shard_map/all_to_all | solution.py:508
  17.6 1.4 %copy-start = (f32[3,60,16,128]{3,2,1,0:T(8,128)S(1)}, f32[3,60,16,128]{3,2,1,0:T(8,128)}, u32[]{:S(2)}) copy-start(f32[3,60,16,128]{3,2,1,0:T(8,128)} %param.19) | copy-start | bytes 4423684
  18.9 14.2 %copy-start.1 = (f32[256,256]{1,0:T(8,128)S(1)}, f32[256,256]{1,0:T(8,128)}, u32[]{:S(2)}) copy-start(f32[256,256]{1,0:T(8,128)} %w2_ref) | copy-start | bytes 786436
  18.9 14.2 %copy-start.2 = (f32[180,256]{1,0:T(8,128)S(1)}, f32[180,256]{1,0:T(8,128)}, u32[]{:S(2)}) copy-start(f32[180,256]{1,0:T(8,128)} %w1_ref.1) | copy-start | bytes 552964
  22.1 47.9 %collective-permute-start = (f32[192,128]{1,0:T(8,128)}, f32[192,128]{1,0:T(8,128)S(1)}, u32[]{:S(2)}, u32[]{:S(2)}) collective-permute-start(f32[192,128]{1,0:T(8,128)} %get-tuple-element.82), channel_id=1, source_target_pairs={{16,0},{32,16},{48,32},{64,48},{80,64},{96,80},{112,96},{17,1},{33... | collective-permute-start | bytes 294920 | tf_op jit(solution)/shard_map/ppermute | solution.py:488
  25.0 44.9 %collective-permute-start.1 = (f32[192,128]{1,0:T(8,128)}, f32[192,128]{1,0:T(8,128)S(1)}, u32[]{:S(2)}, u32[]{:S(2)}) collective-permute-start(f32[192,128]{1,0:T(8,128)} %get-tuple-element.83), channel_id=1, source_target_pairs={{0,16},{16,32},{32,48},{48,64},{64,80},{80,96},{96,112},{1,17},{17... | collective-permute-start | bytes 294920 | tf_op jit(solution)/shard_map/ppermute | solution.py:488
  27.6 42.3 %collective-permute-start.2 = (f32[192,128]{1,0:T(8,128)}, f32[192,128]{1,0:T(8,128)S(1)}, u32[]{:S(2)}, u32[]{:S(2)}) collective-permute-start(f32[192,128]{1,0:T(8,128)} %get-tuple-element.84), channel_id=1, source_target_pairs={{1,0},{2,1},{3,2},{4,3},{5,4},{6,5},{7,6},{8,7},{9,8},{10,9},{11,1... | collective-permute-start | bytes 294920 | tf_op jit(solution)/shard_map/ppermute | solution.py:488
  28.9 41.0 %collective-permute-start.3 = (f32[192,128]{1,0:T(8,128)}, f32[192,128]{1,0:T(8,128)S(1)}, u32[]{:S(2)}, u32[]{:S(2)}) collective-permute-start(f32[192,128]{1,0:T(8,128)} %get-tuple-element.85), channel_id=1, source_target_pairs={{0,1},{1,2},{2,3},{3,4},{4,5},{5,6},{6,7},{7,8},{8,9},{9,10},{10,1... | collective-permute-start | bytes 294920 | tf_op jit(solution)/shard_map/ppermute | solution.py:488
  33.2 0.8 copy-start.7
  34.0 0.7 copy-start.8
  34.7 0.7 copy-start.9
  35.4 0.7 copy-start.10
  81.4 26.2 %copy-start.12 = (f32[192,128]{1,0:T(8,128)S(1)}, f32[192,128]{1,0:T(8,128)}, u32[]{:S(2)}) copy-start(f32[192,128]{1,0:T(8,128)} %get-tuple-element.98) | copy-start | bytes 294916
  81.4 29.1 %copy-start.11 = (f32[192,128]{1,0:T(8,128)S(1)}, f32[192,128]{1,0:T(8,128)}, u32[]{:S(2)}) copy-start(f32[192,128]{1,0:T(8,128)} %get-tuple-element.99) | copy-start | bytes 294916
  81.4 31.7 %copy-start.6 = (s32[16,128]{1,0:T(8,128)S(1)}, s32[16,128]{1,0:T(8,128)}, u32[]{:S(2)}) copy-start(s32[16,128]{1,0:T(8,128)} %mask_ref.3) | copy-start | bytes 24580
  81.4 19.5 %all-to-all-start.1 = ((f32[128,8,128]{2,1,0:T(8,128)}), f32[128,8,128]{2,1,0:T(8,128)S(1)}, u32[]{:S(2)}, u32[]{:S(2)}) async-start(f32[128,8,128]{2,1,0:T(8,128)} %bitcast.27), calls=%async_computation.1 | async-start | bytes 1048576 | tf_op jit(solution)/shard_map/all_to_all | solution.py:472
  86.8 15.1 %collective-permute-start.4 = (f32[192,128]{1,0:T(8,128)}, f32[192,128]{1,0:T(8,128)S(1)}, u32[]{:S(2)}, u32[]{:S(2)}) collective-permute-start(f32[192,128]{1,0:T(8,128)} %get-tuple-element.89), channel_id=1, source_target_pairs={{1,0},{2,1},{3,2},{4,3},{5,4},{6,5},{7,6},{8,7},{9,8},{10,9},{11,1... | collective-permute-start | bytes 294920 | tf_op jit(solution)/shard_map/ppermute | solution.py:488
  88.1 13.8 %collective-permute-start.5 = (f32[192,128]{1,0:T(8,128)}, f32[192,128]{1,0:T(8,128)S(1)}, u32[]{:S(2)}, u32[]{:S(2)}) collective-permute-start(f32[192,128]{1,0:T(8,128)} %get-tuple-element.90), channel_id=1, source_target_pairs={{0,1},{1,2},{2,3},{3,4},{4,5},{5,6},{6,7},{7,8},{8,9},{9,10},{10,1... | collective-permute-start | bytes 294920 | tf_op jit(solution)/shard_map/ppermute | solution.py:488
  101.9 19.8 %all-to-all-start.2 = ((f32[128,8,128]{2,1,0:T(8,128)}), f32[128,8,128]{2,1,0:T(8,128)S(1)}, u32[]{:S(2)}, u32[]{:S(2)}) async-start(f32[128,8,128]{2,1,0:T(8,128)} %bitcast.26), calls=%async_computation.2 | async-start | bytes 1048576 | tf_op jit(solution)/shard_map/all_to_all | solution.py:478
  107.6 9.7 %collective-permute-start.6 = (f32[192,128]{1,0:T(8,128)S(1)}, f32[192,128]{1,0:T(8,128)S(1)}, u32[]{:S(2)}, u32[]{:S(2)}) collective-permute-start(f32[192,128]{1,0:T(8,128)S(1)} %copy-done.12), channel_id=1, source_target_pairs={{16,0},{32,16},{48,32},{64,48},{80,64},{96,80},{112,96},{17,1},{33... | collective-permute-start | bytes 294920 | tf_op jit(solution)/shard_map/ppermute | solution.py:488
  110.6 6.8 %collective-permute-start.7 = (f32[192,128]{1,0:T(8,128)S(1)}, f32[192,128]{1,0:T(8,128)S(1)}, u32[]{:S(2)}, u32[]{:S(2)}) collective-permute-start(f32[192,128]{1,0:T(8,128)S(1)} %copy-done.11), channel_id=1, source_target_pairs={{0,16},{16,32},{32,48},{48,64},{64,80},{80,96},{96,112},{1,17},{17... | collective-permute-start | bytes 294920 | tf_op jit(solution)/shard_map/ppermute | solution.py:488

commit v9 on v8

--- a/solution.py
+++ b/solution.py
@@ -18,6 +18,7 @@
 BLOCK = SLOT + HALF
 CX = 16
 CY = 128
+APART = 8
 DEV = 128
 STORE = 4096
 UNROLL = DEV // 8
@@ -201,15 +202,6 @@
     return call(weights_kernel, "weights", outs, args, scratch=[near(FEATS, HID), near(FEATS, HID)])
 
 
-def edge_plane(x, plane, mask_row, fy_row, ew_ref, ee_ref):
-    weighted = plane * mask_row
-    lane = lax.broadcasted_iota(jnp.int32, plane.shape, 1)
-    west = pltpu.roll(weighted * (flat_mix + 0.5 * fy_row), x, 1)
-    east = pltpu.roll(weighted * (flat_mix - 0.5 * fy_row), x + 1, 1)
-    ew_ref[...] = jnp.where(lane == x, west, ew_ref[...])
-    ee_ref[...] = jnp.where(lane == x, east, ee_ref[...])
-
-
 def north_edge(plane, mask_row, fx_row):
     return plane * mask_row * (flat_mix + 0.5 * fx_row)
 
@@ -236,18 +228,30 @@
     return total
 
 
-def halo_lanes(x, hw_ref, he_ref):
+def join_lanes(hw_ref, he_ref):
     lane = lax.broadcasted_iota(jnp.int32, hw_ref.shape, 1)
-    east = he_ref[...] if x == 0 else pltpu.roll(he_ref[...], CY - x, 1)
-    west = pltpu.roll(hw_ref[...], CY - 1 - x, 1)
-    return jnp.where(lane == CY - 1, west, 0.0) + jnp.where(lane == 0, east, 0.0)
+    return jnp.where(lane % APART == APART - 1, pltpu.roll(hw_ref[...], CY - 1, 1), he_ref[...])
+
+
+def halo_lanes(x, joined):
+    lane = lax.broadcasted_iota(jnp.int32, joined.shape, 1)
+    here = joined if x == 0 else pltpu.roll(joined, CY - APART * x, 1)
+    return jnp.where((lane == 0) | (lane == CY - 1), here, 0.0)
 
 
 def put_edges(lam_ref, mask_ref, fx_ref, fy_ref, en_ref, es_ref, ew_ref, ee_ref):
-    ew_ref[...] = jnp.zeros_like(ew_ref)
-    ee_ref[...] = jnp.zeros_like(ee_ref)
-    for x in range(CX):
-        edge_plane(x, lam_ref[x], row(mask_ref, x), row(fy_ref, x), ew_ref, ee_ref)
+    lane = lax.broadcasted_iota(jnp.int32, (PAD, CY), 1)
+    for t in range(TRACERS):
+        levels = slice(t * PAD, (t + 1) * PAD)
+        west = east = jnp.zeros((PAD, CY), F32)
+        for x in range(CX):
+            weighted = lam_ref[x, levels, :] * row(mask_ref, x)
+            fy = row(fy_ref, x)
+            at = APART * x
+            west = jnp.where(lane == at, pltpu.roll(weighted * (flat_mix + 0.5 * fy), at, 1), west)
+            east = jnp.where(lane == at, pltpu.roll(weighted * (flat_mix - 0.5 * fy), at + 1, 1), east)
+        ew_ref[levels, :] = west
+        ee_ref[levels, :] = east
     en_ref[...] = north_edge(lam_ref[0], row(mask_ref, 0), row(fx_ref, 0))
     es_ref[...] = south_edge(lam_ref[CX - 1], row(mask_ref, CX - 1), row(fx_ref, CX - 1))
 
@@ -267,14 +271,15 @@
 
 
 def edges(*args):
-    return call(edges_kernel, "edges", (far(*PLANE), far(*PLANE), EDGE, EDGE, EDGE, EDGE), args)
+    return call(edges_kernel, "edges", (far(*PLANE), far(*PLANE), EDGE, EDGE, EDGE, EDGE), args, mib=8)
 
 
 def last_kernel(mask_ref, fx_ref, fy_ref, hw_ref, he_ref, lam_far, down_far, out_ref, lam, down, sems):
     wait = bring(((0, lam_far, lam), (0, down_far, down)), sems)
+    joined = join_lanes(hw_ref, he_ref)
     wait(0)
     for x in range(CX):
-        total = local_plane(x, lam, mask_ref, fx_ref, fy_ref) + halo_lanes(x, hw_ref, he_ref)
+        total = local_plane(x, lam, mask_ref, fx_ref, fy_ref) + halo_lanes(x, joined)
         value = lam[x] + step_size * (total + down[x])
         for t in range(TRACERS):
             out_ref[pl.ds(t * NZ * CX + x, NZ, stride=CX), :] = value[t * PAD : t * PAD + NZ]
@@ -405,8 +410,9 @@
     split_weights, halos, refs = refs[:8], refs[8:12], refs[12:]
     (lam_far, down_far, grads_ref), sides, (rows_ref, lam, down, total, out_sems) = refs[:3], refs[3:7], refs[7:]
     hn_ref, hs_ref, hw_ref, he_ref = halos
+    joined = join_lanes(hw_ref, he_ref)
     for x in range(CX):
-        halo = halo_lanes(x, hw_ref, he_ref)
+        halo = halo_lanes(x, joined)
         if x == 0:
             halo = halo + hs_ref[...]
         if x == CX - 1:

time: 123 us -> 123 us (level)
  no operation moved by 1% of the time
where the time goes in v9:
time: 123 us; the launch traced here: 122 us
  starting transfers between devices  44.4 us (36%)
  Pallas kernels  38.1 us (31%)
  waiting for transfers between devices  33.6 us (27%)
  local copies, waits for them, and re-layouts  5.37 us (4%)
    pallas_call x8, Pallas kernels, call(): pl.pallas_call(kernel, out_shape=tuple((out[0] if isinstance(out, list) e...  32.8 us
    ppermute x8, starting transfers between devices, exchange(): return (lax.ppermute(before, axis, down), lax.ppermute(after, axis, up))  21.9 us
    all_to_all x1, waiting for transfers between devices, on_device(): lax.all_to_all(payload, ('gx', 'gy'), split_axis=0, concat_axis=0, tiled=...  21.3 us
    all_to_all x1, starting transfers between devices, on_device(): lax.all_to_all(payload, ('gx', 'gy'), split_axis=0, concat_axis=0, tiled=...  11.5 us
    all_to_all x1, waiting for transfers between devices, reduce_params(): lax.all_to_all(packed, ('gx', 'gy'), split_axis=0, concat_axis=0, tiled=T...  8.82 us
    all_to_all x1, starting transfers between devices, finish_params(): lax.all_to_all(spread, ('gx', 'gy'), split_axis=0, concat_axis=0, tiled=T...  5.68 us
    unnamed x27, local copies, waits for them, and re-layouts  5.37 us
    pallas_call x1, Pallas kernels, pack(): pl.pallas_call(pack_kernel, out_shape=pltpu.HBM((DEV, 2 * BLOCK, 128), BF...  5.35 us
  transfers between devices with their start and end apart: 11, of which 3 were waited for; matrix products, arithmetic and copies ran while one was open for 1% of the time, Pallas kernels for 17%

profile of v9, /device:TPU:1, one launch (start us, length us, event | category | flops | bytes accessed | tf_op | source)
XLA Modules:
  0.0 122.4 jit_solution(9063378793925756272)
XLA Ops:
  0.6 5.3 %pack.1 = bf16[128,96,128]{2,1,0:T(8,128)(2,1)} custom-call(s32[1,128]{1,0:T(1,128)} %counts_ref.1, bf16[360,4096]{1,0:T(8,128)(2,1)} %bitcast.25), custom_call_target="tpu_custom_call" | custom-call | tf_op jit(solution)/shard_map/pack/pallas_call | solution.py:146
  6.0 0.0 copy-start.5
  6.0 11.5 %all-to-all-start = ((bf16[128,96,128]{2,1,0:T(8,128)(2,1)}), bf16[128,96,128]{2,1,0:T(8,128)(2,1)S(1)}, u32[]{:S(2)}, u32[]{:S(2)}) async-start(bf16[128,96,128]{2,1,0:T(8,128)(2,1)} %pack.1), calls=%async_computation | async-start | bytes 6291456 | tf_op jit(solution)/shard_map/all_to_all | solution.py:514
  17.6 1.4 %copy-done = f32[3,60,16,128]{3,2,1,0:T(8,128)S(1)} copy-done((f32[3,60,16,128]{3,2,1,0:T(8,128)S(1)}, f32[3,60,16,128]{3,2,1,0:T(8,128)}, u32[]{:S(2)}) %copy-start) | copy-done | bytes 1474584
  19.0 3.1 %edges.1 = (f32[16,192,128]{2,1,0:T(8,128)}, f32[16,192,128]{2,1,0:T(8,128)}, f32[192,128]{1,0:T(8,128)}, f32[192,128]{1,0:T(8,128)}, f32[192,128]{1,0:T(8,128)}, /*index=5*/f32[192,128]{1,0:T(8,128)}) custom-call(f32[2880,128]{1,0:T(8,128)S(1)} %bitcast.20, s32[16,128]{1,0:T(8,128)S(1)} %copy-done.5, f32[16,128]{1,0:T(8,128)S(1)} %copy-done.3, ...), custom_call_target="tpu_custom_call" | custom-call | tf_op jit(solution)/shard_map/edges/pallas_call | solution.py:82
  22.0 3.0 %collective-permute-start = (f32[192,128]{1,0:T(8,128)}, f32[192,128]{1,0:T(8,128)S(1)}, u32[]{:S(2)}, u32[]{:S(2)}) collective-permute-start(f32[192,128]{1,0:T(8,128)} %get-tuple-element.82), channel_id=1, source_target_pairs={{16,0},{32,16},{48,32},{64,48},{80,64},{96,80},{112,96},{17,1},{33... | collective-permute-start | bytes 294920 | tf_op jit(solution)/shard_map/ppermute | solution.py:494
  25.0 2.6 %collective-permute-start.1 = (f32[192,128]{1,0:T(8,128)}, f32[192,128]{1,0:T(8,128)S(1)}, u32[]{:S(2)}, u32[]{:S(2)}) collective-permute-start(f32[192,128]{1,0:T(8,128)} %get-tuple-element.83), channel_id=1, source_target_pairs={{0,16},{16,32},{32,48},{48,64},{64,80},{80,96},{96,112},{1,17},{17... | collective-permute-start | bytes 294920 | tf_op jit(solution)/shard_map/ppermute | solution.py:494
  27.6 1.3 %collective-permute-start.2 = (f32[192,128]{1,0:T(8,128)}, f32[192,128]{1,0:T(8,128)S(1)}, u32[]{:S(2)}, u32[]{:S(2)}) collective-permute-start(f32[192,128]{1,0:T(8,128)} %get-tuple-element.84), channel_id=1, source_target_pairs={{1,0},{2,1},{3,2},{4,3},{5,4},{6,5},{7,6},{8,7},{9,8},{10,9},{11,1... | collective-permute-start | bytes 294920 | tf_op jit(solution)/shard_map/ppermute | solution.py:494
  28.9 4.2 %collective-permute-start.3 = (f32[192,128]{1,0:T(8,128)}, f32[192,128]{1,0:T(8,128)S(1)}, u32[]{:S(2)}, u32[]{:S(2)}) collective-permute-start(f32[192,128]{1,0:T(8,128)} %get-tuple-element.85), channel_id=1, source_target_pairs={{0,1},{1,2},{2,3},{3,4},{4,5},{5,6},{6,7},{7,8},{8,9},{9,10},{10,1... | collective-permute-start | bytes 294920 | tf_op jit(solution)/shard_map/ppermute | solution.py:494
  33.1 0.0 copy-start.7
  33.1 0.8 copy-done.7
  34.0 0.7 copy-done.8
  34.6 0.7 copy-done.9
  35.3 0.7 copy-done.10
  36.0 1.2 weights.1
  37.2 21.3 %all-to-all-done.got_ref = bf16[128,96,128]{2,1,0:T(8,128)(2,1)S(1)} async-done(((bf16[128,96,128]{2,1,0:T(8,128)(2,1)}), bf16[128,96,128]{2,1,0:T(8,128)(2,1)S(1)}, u32[]{:S(2)}, u32[]{:S(2)}) %all-to-all-start) | async-done | bytes 3145760 | tf_op jit(solution)/shard_map/all_to_all | solution.py:514
  58.5 11.5 %closure1.1 = (f32[16,192,128]{2,1,0:T(8,128)S(1)}, f32[512,256]{1,0:T(8,128)S(1)}, s32[16,128]{1,0:T(8,128)S(1)}, s32[16,128]{1,0:T(8,128)S(1)}, bf16[512,192]{...) custom-call(bf16[128,96,128]{2,1,0:T(8,128)(2,1)S(1)} %all-to-all-do, ...), custom_call_target="tpu_custom_call" | custom-call | tf_op jit(solution)/shard_map/closure1/pallas_call | solution.py:82
  70.0 11.3 %closure0.1 = (f32[16,192,128]{2,1,0:T(8,128)}, f32[16,192,128]{2,1,0:T(8,128)}, f32[1024,128]{1,0:T(8,128)}, f32[192,128]{1,0:T(8,128)}, f32[192,128]{1,0:T(8,1...) custom-call(bf16[128,96,128]{2,1,0:T(8,128)(2,1)S(1)} %all-to-all-done.got_ref, f32[16,128]{1,0:T(8,128)S(1)} %copy-done.3, ...), custom_call_target="tpu_custom_call" | custom-call | tf_op jit(solution)/shard_map/closure0/pallas_call | solution.py:82
  81.3 0.0 copy-start.11
  81.3 5.3 %all-to-all-start.1 = ((f32[128,8,128]{2,1,0:T(8,128)}), f32[128,8,128]{2,1,0:T(8,128)S(1)}, u32[]{:S(2)}, u32[]{:S(2)}) async-start(f32[128,8,128]{2,1,0:T(8,128)} %bitcast.27), calls=%async_computation.1 | async-start | bytes 1048576 | tf_op jit(solution)/shard_map/all_to_all | solution.py:478
  86.7 1.3 %collective-permute-start.4 = (f32[192,128]{1,0:T(8,128)}, f32[192,128]{1,0:T(8,128)S(1)}, u32[]{:S(2)}, u32[]{:S(2)}) collective-permute-start(f32[192,128]{1,0:T(8,128)} %get-tuple-element.89), channel_id=1, source_target_pairs={{1,0},{2,1},{3,2},{4,3},{5,4},{6,5},{7,6},{8,7},{9,8},{10,9},{11,1... | collective-permute-start | bytes 294920 | tf_op jit(solution)/shard_map/ppermute | solution.py:494
  88.0 4.0 %collective-permute-start.5 = (f32[192,128]{1,0:T(8,128)}, f32[192,128]{1,0:T(8,128)S(1)}, u32[]{:S(2)}, u32[]{:S(2)}) collective-permute-start(f32[192,128]{1,0:T(8,128)} %get-tuple-element.90), channel_id=1, source_target_pairs={{0,1},{1,2},{2,3},{3,4},{4,5},{5,6},{6,7},{7,8},{8,9},{9,10},{10,1... | collective-permute-start | bytes 294920 | tf_op jit(solution)/shard_map/ppermute | solution.py:494
  92.0 8.8 %all-to-all-done.1 = f32[128,8,128]{2,1,0:T(8,128)S(1)} async-done(((f32[128,8,128]{2,1,0:T(8,128)}), f32[128,8,128]{2,1,0:T(8,128)S(1)}, u32[]{:S(2)}, u32[]{:S(2)}) %all-to-all-start.1) | async-done | bytes 524320 | tf_op jit(solution)/shard_map/all_to_all | solution.py:478
  100.8 1.0 sum.1
  101.8 5.7 %all-to-all-start.2 = ((f32[128,8,128]{2,1,0:T(8,128)}), f32[128,8,128]{2,1,0:T(8,128)S(1)}, u32[]{:S(2)}, u32[]{:S(2)}) async-start(f32[128,8,128]{2,1,0:T(8,128)} %bitcast.26), calls=%async_computation.2 | async-start | bytes 1048576 | tf_op jit(solution)/shard_map/all_to_all | solution.py:484
  107.5 3.0 %collective-permute-start.6 = (f32[192,128]{1,0:T(8,128)S(1)}, f32[192,128]{1,0:T(8,128)S(1)}, u32[]{:S(2)}, u32[]{:S(2)}) collective-permute-start(f32[192,128]{1,0:T(8,128)S(1)} %copy-done.12), channel_id=1, source_target_pairs={{16,0},{32,16},{48,32},{64,48},{80,64},{96,80},{112,96},{17,1},{33... | collective-permute-start | bytes 294920 | tf_op jit(solution)/shard_map/ppermute | solution.py:494
  110.5 2.6 %collective-permute-start.7 = (f32[192,128]{1,0:T(8,128)S(1)}, f32[192,128]{1,0:T(8,128)S(1)}, u32[]{:S(2)}, u32[]{:S(2)}) collective-permute-start(f32[192,128]{1,0:T(8,128)S(1)} %copy-done.11), channel_id=1, source_target_pairs={{0,16},{16,32},{32,48},{48,64},{64,80},{80,96},{96,112},{1,17},{17... | collective-permute-start | bytes 294920 | tf_op jit(solution)/shard_map/ppermute | solution.py:494
  113.1 3.7 %stencil0.1.part_ref = f32[2880,128]{1,0:T(8,128)S(1)} custom-call(s32[16,128]{1,0:T(8,128)S(1)} %copy-done.6, f32[16,128]{1,0:T(8,128)S(1)} %copy-done.3, f32[16,128]{1,0:T(8,128)S(1)} %copy-done.4, f32[192,128]{1,0:T(8,128)S(1)} %collective-permute-done.4.hw_ref, f32[192,128]{1,0:T(8,128)S(1)} %collective-permute-done.5.he_ref, ...), custom_call_target="tpu_custom_call" | custom-call | tf_op jit(solution)/shard_map/stencil0/pallas_call | solution.py:82
  116.8 0.2 rows0.1
  117.0 1.1 copy.22
  118.1 3.5 %all-to-all-done.2 = f32[128,8,128]{2,1,0:T(8,128)S(1)} async-done(((f32[128,8,128]{2,1,0:T(8,128)}), f32[128,8,128]{2,1,0:T(8,128)S(1)}, u32[]{:S(2)}, u32[]{:S(2)}) %all-to-all-start.2) | async-done | bytes 524320 | tf_op jit(solution)/shard_map/all_to_all | solution.py:484
  121.6 0.8 unpack.1
  (26 shorter events, 0.1 us)
Async XLA Ops:
  6.0 11.6 %copy-start.3 = (f32[16,128]{1,0:T(8,128)S(1)}, f32[16,128]{1,0:T(8,128)}, u32[]{:S(2)}) copy-start(f32[16,128]{1,0:T(8,128)} %fx_ref.5) | copy-start | bytes 24580
  6.0 11.6 %copy-start.4 = (f32[16,128]{1,0:T(8,128)S(1)}, f32[16,128]{1,0:T(8,128)}, u32[]{:S(2)}) copy-start(f32[16,128]{1,0:T(8,128)} %fy_ref.5) | copy-start | bytes 24580
  6.0 11.6 %copy-start.5 = (s32[16,128]{1,0:T(8,128)S(1)}, s32[16,128]{1,0:T(8,128)}, u32[]{:S(2)}) copy-start(s32[16,128]{1,0:T(8,128)} %mask_ref.3) | copy-start | bytes 24580
  6.0 52.4 %all-to-all-start = ((bf16[128,96,128]{2,1,0:T(8,128)(2,1)}), bf16[128,96,128]{2,1,0:T(8,128)(2,1)S(1)}, u32[]{:S(2)}, u32[]{:S(2)}) async-start(bf16[128,96,128]{2,1,0:T(8,128)(2,1)} %pack.1), calls=%async_computation | async-start | bytes 6291456 | tf_op jit(solution)/shard_map/all_to_all | solution.py:514
  17.6 1.4 %copy-start = (f32[3,60,16,128]{3,2,1,0:T(8,128)S(1)}, f32[3,60,16,128]{3,2,1,0:T(8,128)}, u32[]{:S(2)}) copy-start(f32[3,60,16,128]{3,2,1,0:T(8,128)} %param.19) | copy-start | bytes 4423684
  18.9 14.1 %copy-start.1 = (f32[256,256]{1,0:T(8,128)S(1)}, f32[256,256]{1,0:T(8,128)}, u32[]{:S(2)}) copy-start(f32[256,256]{1,0:T(8,128)} %w2_ref) | copy-start | bytes 786436
  19.0 14.2 %copy-start.2 = (f32[180,256]{1,0:T(8,128)S(1)}, f32[180,256]{1,0:T(8,128)}, u32[]{:S(2)}) copy-start(f32[180,256]{1,0:T(8,128)} %w1_ref.1) | copy-start | bytes 552964
  22.0 47.9 %collective-permute-start = (f32[192,128]{1,0:T(8,128)}, f32[192,128]{1,0:T(8,128)S(1)}, u32[]{:S(2)}, u32[]{:S(2)}) collective-permute-start(f32[192,128]{1,0:T(8,128)} %get-tuple-element.82), channel_id=1, source_target_pairs={{16,0},{32,16},{48,32},{64,48},{80,64},{96,80},{112,96},{17,1},{33... | collective-permute-start | bytes 294920 | tf_op jit(solution)/shard_map/ppermute | solution.py:494
  25.0 45.0 %collective-permute-start.1 = (f32[192,128]{1,0:T(8,128)}, f32[192,128]{1,0:T(8,128)S(1)}, u32[]{:S(2)}, u32[]{:S(2)}) collective-permute-start(f32[192,128]{1,0:T(8,128)} %get-tuple-element.83), channel_id=1, source_target_pairs={{0,16},{16,32},{32,48},{48,64},{64,80},{80,96},{96,112},{1,17},{17... | collective-permute-start | bytes 294920 | tf_op jit(solution)/shard_map/ppermute | solution.py:494
  27.6 42.4 %collective-permute-start.2 = (f32[192,128]{1,0:T(8,128)}, f32[192,128]{1,0:T(8,128)S(1)}, u32[]{:S(2)}, u32[]{:S(2)}) collective-permute-start(f32[192,128]{1,0:T(8,128)} %get-tuple-element.84), channel_id=1, source_target_pairs={{1,0},{2,1},{3,2},{4,3},{5,4},{6,5},{7,6},{8,7},{9,8},{10,9},{11,1... | collective-permute-start | bytes 294920 | tf_op jit(solution)/shard_map/ppermute | solution.py:494
  28.9 41.1 %collective-permute-start.3 = (f32[192,128]{1,0:T(8,128)}, f32[192,128]{1,0:T(8,128)S(1)}, u32[]{:S(2)}, u32[]{:S(2)}) collective-permute-start(f32[192,128]{1,0:T(8,128)} %get-tuple-element.85), channel_id=1, source_target_pairs={{0,1},{1,2},{2,3},{3,4},{4,5},{5,6},{6,7},{7,8},{8,9},{9,10},{10,1... | collective-permute-start | bytes 294920 | tf_op jit(solution)/shard_map/ppermute | solution.py:494
  33.1 0.8 copy-start.7
  34.0 0.7 copy-start.8
  34.6 0.7 copy-start.9
  35.3 0.7 copy-start.10
  81.3 26.2 %copy-start.12 = (f32[192,128]{1,0:T(8,128)S(1)}, f32[192,128]{1,0:T(8,128)}, u32[]{:S(2)}) copy-start(f32[192,128]{1,0:T(8,128)} %get-tuple-element.98) | copy-start | bytes 294916
  81.3 29.2 %copy-start.11 = (f32[192,128]{1,0:T(8,128)S(1)}, f32[192,128]{1,0:T(8,128)}, u32[]{:S(2)}) copy-start(f32[192,128]{1,0:T(8,128)} %get-tuple-element.99) | copy-start | bytes 294916
  81.3 31.8 %copy-start.6 = (s32[16,128]{1,0:T(8,128)S(1)}, s32[16,128]{1,0:T(8,128)}, u32[]{:S(2)}) copy-start(s32[16,128]{1,0:T(8,128)} %mask_ref.3) | copy-start | bytes 24580
  81.3 19.5 %all-to-all-start.1 = ((f32[128,8,128]{2,1,0:T(8,128)}), f32[128,8,128]{2,1,0:T(8,128)S(1)}, u32[]{:S(2)}, u32[]{:S(2)}) async-start(f32[128,8,128]{2,1,0:T(8,128)} %bitcast.27), calls=%async_computation.1 | async-start | bytes 1048576 | tf_op jit(solution)/shard_map/all_to_all | solution.py:478
  86.7 15.1 %collective-permute-start.4 = (f32[192,128]{1,0:T(8,128)}, f32[192,128]{1,0:T(8,128)S(1)}, u32[]{:S(2)}, u32[]{:S(2)}) collective-permute-start(f32[192,128]{1,0:T(8,128)} %get-tuple-element.89), channel_id=1, source_target_pairs={{1,0},{2,1},{3,2},{4,3},{5,4},{6,5},{7,6},{8,7},{9,8},{10,9},{11,1... | collective-permute-start | bytes 294920 | tf_op jit(solution)/shard_map/ppermute | solution.py:494
  88.0 13.8 %collective-permute-start.5 = (f32[192,128]{1,0:T(8,128)}, f32[192,128]{1,0:T(8,128)S(1)}, u32[]{:S(2)}, u32[]{:S(2)}) collective-permute-start(f32[192,128]{1,0:T(8,128)} %get-tuple-element.90), channel_id=1, source_target_pairs={{0,1},{1,2},{2,3},{3,4},{4,5},{5,6},{6,7},{7,8},{8,9},{9,10},{10,1... | collective-permute-start | bytes 294920 | tf_op jit(solution)/shard_map/ppermute | solution.py:494
  101.8 19.8 %all-to-all-start.2 = ((f32[128,8,128]{2,1,0:T(8,128)}), f32[128,8,128]{2,1,0:T(8,128)S(1)}, u32[]{:S(2)}, u32[]{:S(2)}) async-start(f32[128,8,128]{2,1,0:T(8,128)} %bitcast.26), calls=%async_computation.2 | async-start | bytes 1048576 | tf_op jit(solution)/shard_map/all_to_all | solution.py:484
  107.5 9.3 %collective-permute-start.6 = (f32[192,128]{1,0:T(8,128)S(1)}, f32[192,128]{1,0:T(8,128)S(1)}, u32[]{:S(2)}, u32[]{:S(2)}) collective-permute-start(f32[192,128]{1,0:T(8,128)S(1)} %copy-done.12), channel_id=1, source_target_pairs={{16,0},{32,16},{48,32},{64,48},{80,64},{96,80},{112,96},{17,1},{33... | collective-permute-start | bytes 294920 | tf_op jit(solution)/shard_map/ppermute | solution.py:494
  110.5 6.3 %collective-permute-start.7 = (f32[192,128]{1,0:T(8,128)S(1)}, f32[192,128]{1,0:T(8,128)S(1)}, u32[]{:S(2)}, u32[]{:S(2)}) collective-permute-start(f32[192,128]{1,0:T(8,128)S(1)} %copy-done.11), channel_id=1, source_target_pairs={{0,16},{16,32},{32,48},{48,64},{64,80},{80,96},{96,112},{1,17},{17... | collective-permute-start | bytes 294920 | tf_op jit(solution)/shard_map/ppermute | solution.py:494

commit v10 on v9

--- a/solution.py
+++ b/solution.py
@@ -454,9 +454,10 @@
 
 
 def sum_kernel(parts_ref, out_ref):
-    value = parts_ref[0:8, :]
-    for i in range(1, DEV):
-        value = value + parts_ref[8 * i : 8 * i + 8, :]
+    values = [parts_ref[8 * i : 8 * i + 8, :] for i in range(DEV)]
+    while len(values) > 1:
+        values = [left + right for left, right in zip(values[::2], values[1::2])]
+    value = values[0]
     for i in range(DEV):
         out_ref[8 * i : 8 * i + 8, :] = value
 

time: 123 us -> 123 us (level)
  no operation moved by 1% of the time
where the time goes in v10:
time: 123 us; the launch traced here: 122 us
  starting transfers between devices  44.5 us (36%)
  Pallas kernels  38 us (31%)
  waiting for transfers between devices  33.6 us (27%)
  local copies, waits for them, and re-layouts  5.37 us (4%)
    pallas_call x8, Pallas kernels, call(): pl.pallas_call(kernel, out_shape=tuple((out[0] if isinstance(out, list) e...  32.6 us
    ppermute x8, starting transfers between devices, exchange(): return (lax.ppermute(before, axis, down), lax.ppermute(after, axis, up))  21.9 us
    all_to_all x1, waiting for transfers between devices, on_device(): lax.all_to_all(payload, ('gx', 'gy'), split_axis=0, concat_axis=0, tiled=...  21.3 us
    all_to_all x1, starting transfers between devices, on_device(): lax.all_to_all(payload, ('gx', 'gy'), split_axis=0, concat_axis=0, tiled=...  11.5 us
    all_to_all x1, waiting for transfers between devices, reduce_params(): lax.all_to_all(packed, ('gx', 'gy'), split_axis=0, concat_axis=0, tiled=T...  8.82 us
    all_to_all x1, starting transfers between devices, finish_params(): lax.all_to_all(spread, ('gx', 'gy'), split_axis=0, concat_axis=0, tiled=T...  5.79 us
    unnamed x27, local copies, waits for them, and re-layouts  5.37 us
    pallas_call x1, Pallas kernels, pack(): pl.pallas_call(pack_kernel, out_shape=pltpu.HBM((DEV, 2 * BLOCK, 128), BF...  5.36 us
  transfers between devices with their start and end apart: 11, of which 3 were waited for; matrix products, arithmetic and copies ran while one was open for 1% of the time, Pallas kernels for 17%

profile of v10, /device:TPU:1, one launch (start us, length us, event | category | flops | bytes accessed | tf_op | source)
XLA Modules:
  0.0 122.4 jit_solution(3195795731871358388)
XLA Ops:
  0.6 5.4 %pack.1 = bf16[128,96,128]{2,1,0:T(8,128)(2,1)} custom-call(s32[1,128]{1,0:T(1,128)} %counts_ref.1, bf16[360,4096]{1,0:T(8,128)(2,1)} %bitcast.25), custom_call_target="tpu_custom_call" | custom-call | tf_op jit(solution)/shard_map/pack/pallas_call | solution.py:146
  6.0 0.0 copy-start.3
  6.0 0.0 copy-start.4
  6.0 11.5 %all-to-all-start = ((bf16[128,96,128]{2,1,0:T(8,128)(2,1)}), bf16[128,96,128]{2,1,0:T(8,128)(2,1)S(1)}, u32[]{:S(2)}, u32[]{:S(2)}) async-start(bf16[128,96,128]{2,1,0:T(8,128)(2,1)} %pack.1), calls=%async_computation | async-start | bytes 6291456 | tf_op jit(solution)/shard_map/all_to_all | solution.py:515
  17.6 1.4 %copy-done = f32[3,60,16,128]{3,2,1,0:T(8,128)S(1)} copy-done((f32[3,60,16,128]{3,2,1,0:T(8,128)S(1)}, f32[3,60,16,128]{3,2,1,0:T(8,128)}, u32[]{:S(2)}) %copy-start) | copy-done | bytes 1474584
  19.0 3.1 %edges.1 = (f32[16,192,128]{2,1,0:T(8,128)}, f32[16,192,128]{2,1,0:T(8,128)}, f32[192,128]{1,0:T(8,128)}, f32[192,128]{1,0:T(8,128)}, f32[192,128]{1,0:T(8,128)}, /*index=5*/f32[192,128]{1,0:T(8,128)}) custom-call(f32[2880,128]{1,0:T(8,128)S(1)} %bitcast.20, s32[16,128]{1,0:T(8,128)S(1)} %copy-done.5, f32[16,128]{1,0:T(8,128)S(1)} %copy-done.3, ...), custom_call_target="tpu_custom_call" | custom-call | tf_op jit(solution)/shard_map/edges/pallas_call | solution.py:82
  22.0 3.0 %collective-permute-start = (f32[192,128]{1,0:T(8,128)}, f32[192,128]{1,0:T(8,128)S(1)}, u32[]{:S(2)}, u32[]{:S(2)}) collective-permute-start(f32[192,128]{1,0:T(8,128)} %get-tuple-element.82), channel_id=1, source_target_pairs={{16,0},{32,16},{48,32},{64,48},{80,64},{96,80},{112,96},{17,1},{33... | collective-permute-start | bytes 294920 | tf_op jit(solution)/shard_map/ppermute | solution.py:495
  25.0 2.6 %collective-permute-start.1 = (f32[192,128]{1,0:T(8,128)}, f32[192,128]{1,0:T(8,128)S(1)}, u32[]{:S(2)}, u32[]{:S(2)}) collective-permute-start(f32[192,128]{1,0:T(8,128)} %get-tuple-element.83), channel_id=1, source_target_pairs={{0,16},{16,32},{32,48},{48,64},{64,80},{80,96},{96,112},{1,17},{17... | collective-permute-start | bytes 294920 | tf_op jit(solution)/shard_map/ppermute | solution.py:495
  27.6 1.3 %collective-permute-start.2 = (f32[192,128]{1,0:T(8,128)}, f32[192,128]{1,0:T(8,128)S(1)}, u32[]{:S(2)}, u32[]{:S(2)}) collective-permute-start(f32[192,128]{1,0:T(8,128)} %get-tuple-element.84), channel_id=1, source_target_pairs={{1,0},{2,1},{3,2},{4,3},{5,4},{6,5},{7,6},{8,7},{9,8},{10,9},{11,1... | collective-permute-start | bytes 294920 | tf_op jit(solution)/shard_map/ppermute | solution.py:495
  28.9 4.2 %collective-permute-start.3 = (f32[192,128]{1,0:T(8,128)}, f32[192,128]{1,0:T(8,128)S(1)}, u32[]{:S(2)}, u32[]{:S(2)}) collective-permute-start(f32[192,128]{1,0:T(8,128)} %get-tuple-element.85), channel_id=1, source_target_pairs={{0,1},{1,2},{2,3},{3,4},{4,5},{5,6},{6,7},{7,8},{8,9},{9,10},{10,1... | collective-permute-start | bytes 294920 | tf_op jit(solution)/shard_map/ppermute | solution.py:495
  33.1 0.8 copy-done.7
  34.0 0.7 copy-done.8
  34.6 0.7 copy-done.9
  35.3 0.7 copy-done.10
  36.0 1.2 weights.1
  37.2 21.3 %all-to-all-done.got_ref = bf16[128,96,128]{2,1,0:T(8,128)(2,1)S(1)} async-done(((bf16[128,96,128]{2,1,0:T(8,128)(2,1)}), bf16[128,96,128]{2,1,0:T(8,128)(2,1)S(1)}, u32[]{:S(2)}, u32[]{:S(2)}) %all-to-all-start) | async-done | bytes 3145760 | tf_op jit(solution)/shard_map/all_to_all | solution.py:515
  58.4 11.5 %closure1.1 = (f32[16,192,128]{2,1,0:T(8,128)S(1)}, f32[512,256]{1,0:T(8,128)S(1)}, s32[16,128]{1,0:T(8,128)S(1)}, s32[16,128]{1,0:T(8,128)S(1)}, bf16[512,192]{...) custom-call(bf16[128,96,128]{2,1,0:T(8,128)(2,1)S(1)} %all-to-all-do, ...), custom_call_target="tpu_custom_call" | custom-call | tf_op jit(solution)/shard_map/closure1/pallas_call | solution.py:82
  70.0 11.3 %closure0.1 = (f32[16,192,128]{2,1,0:T(8,128)}, f32[16,192,128]{2,1,0:T(8,128)}, f32[1024,128]{1,0:T(8,128)}, f32[192,128]{1,0:T(8,128)}, f32[192,128]{1,0:T(8,1...) custom-call(bf16[128,96,128]{2,1,0:T(8,128)(2,1)S(1)} %all-to-all-done.got_ref, f32[16,128]{1,0:T(8,128)S(1)} %copy-done.3, ...), custom_call_target="tpu_custom_call" | custom-call | tf_op jit(solution)/shard_map/closure0/pallas_call | solution.py:82
  81.3 0.0 copy-start.11
  81.3 5.3 %all-to-all-start.1 = ((f32[128,8,128]{2,1,0:T(8,128)}), f32[128,8,128]{2,1,0:T(8,128)S(1)}, u32[]{:S(2)}, u32[]{:S(2)}) async-start(f32[128,8,128]{2,1,0:T(8,128)} %bitcast.27), calls=%async_computation.1 | async-start | bytes 1048576 | tf_op jit(solution)/shard_map/all_to_all | solution.py:479
  86.7 1.3 %collective-permute-start.4 = (f32[192,128]{1,0:T(8,128)}, f32[192,128]{1,0:T(8,128)S(1)}, u32[]{:S(2)}, u32[]{:S(2)}) collective-permute-start(f32[192,128]{1,0:T(8,128)} %get-tuple-element.89), channel_id=1, source_target_pairs={{1,0},{2,1},{3,2},{4,3},{5,4},{6,5},{7,6},{8,7},{9,8},{10,9},{11,1... | collective-permute-start | bytes 294920 | tf_op jit(solution)/shard_map/ppermute | solution.py:495
  88.0 4.0 %collective-permute-start.5 = (f32[192,128]{1,0:T(8,128)}, f32[192,128]{1,0:T(8,128)S(1)}, u32[]{:S(2)}, u32[]{:S(2)}) collective-permute-start(f32[192,128]{1,0:T(8,128)} %get-tuple-element.90), channel_id=1, source_target_pairs={{0,1},{1,2},{2,3},{3,4},{4,5},{5,6},{6,7},{7,8},{8,9},{9,10},{10,1... | collective-permute-start | bytes 294920 | tf_op jit(solution)/shard_map/ppermute | solution.py:495
  92.0 8.8 %all-to-all-done.1 = f32[128,8,128]{2,1,0:T(8,128)S(1)} async-done(((f32[128,8,128]{2,1,0:T(8,128)}), f32[128,8,128]{2,1,0:T(8,128)S(1)}, u32[]{:S(2)}, u32[]{:S(2)}) %all-to-all-start.1) | async-done | bytes 524320 | tf_op jit(solution)/shard_map/all_to_all | solution.py:479
  100.8 0.9 sum.1
  101.7 5.8 %all-to-all-start.2 = ((f32[128,8,128]{2,1,0:T(8,128)}), f32[128,8,128]{2,1,0:T(8,128)S(1)}, u32[]{:S(2)}, u32[]{:S(2)}) async-start(f32[128,8,128]{2,1,0:T(8,128)} %bitcast.26), calls=%async_computation.2 | async-start | bytes 1048576 | tf_op jit(solution)/shard_map/all_to_all | solution.py:485
  107.5 3.0 %collective-permute-start.6 = (f32[192,128]{1,0:T(8,128)S(1)}, f32[192,128]{1,0:T(8,128)S(1)}, u32[]{:S(2)}, u32[]{:S(2)}) collective-permute-start(f32[192,128]{1,0:T(8,128)S(1)} %copy-done.12), channel_id=1, source_target_pairs={{16,0},{32,16},{48,32},{64,48},{80,64},{96,80},{112,96},{17,1},{33... | collective-permute-start | bytes 294920 | tf_op jit(solution)/shard_map/ppermute | solution.py:495
  110.5 2.6 %collective-permute-start.7 = (f32[192,128]{1,0:T(8,128)S(1)}, f32[192,128]{1,0:T(8,128)S(1)}, u32[]{:S(2)}, u32[]{:S(2)}) collective-permute-start(f32[192,128]{1,0:T(8,128)S(1)} %copy-done.11), channel_id=1, source_target_pairs={{0,16},{16,32},{32,48},{48,64},{64,80},{80,96},{96,112},{1,17},{17... | collective-permute-start | bytes 294920 | tf_op jit(solution)/shard_map/ppermute | solution.py:495
  113.1 3.7 %stencil0.1.part_ref = f32[2880,128]{1,0:T(8,128)S(1)} custom-call(s32[16,128]{1,0:T(8,128)S(1)} %copy-done.6, f32[16,128]{1,0:T(8,128)S(1)} %copy-done.3, f32[16,128]{1,0:T(8,128)S(1)} %copy-done.4, f32[192,128]{1,0:T(8,128)S(1)} %collective-permute-done.4.hw_ref, f32[192,128]{1,0:T(8,128)S(1)} %collective-permute-done.5.he_ref, ...), custom_call_target="tpu_custom_call" | custom-call | tf_op jit(solution)/shard_map/stencil0/pallas_call | solution.py:82
  116.8 0.2 rows0.1
  117.0 1.1 copy.22
  118.1 3.5 %all-to-all-done.2 = f32[128,8,128]{2,1,0:T(8,128)S(1)} async-done(((f32[128,8,128]{2,1,0:T(8,128)}), f32[128,8,128]{2,1,0:T(8,128)S(1)}, u32[]{:S(2)}, u32[]{:S(2)}) %all-to-all-start.2) | async-done | bytes 524320 | tf_op jit(solution)/shard_map/all_to_all | solution.py:485
  121.6 0.8 unpack.1
  (26 shorter events, 0.1 us)
Async XLA Ops:
  6.0 11.5 %copy-start.3 = (f32[16,128]{1,0:T(8,128)S(1)}, f32[16,128]{1,0:T(8,128)}, u32[]{:S(2)}) copy-start(f32[16,128]{1,0:T(8,128)} %fx_ref.5) | copy-start | bytes 24580
  6.0 11.5 %copy-start.4 = (f32[16,128]{1,0:T(8,128)S(1)}, f32[16,128]{1,0:T(8,128)}, u32[]{:S(2)}) copy-start(f32[16,128]{1,0:T(8,128)} %fy_ref.5) | copy-start | bytes 24580
  6.0 11.5 %copy-start.5 = (s32[16,128]{1,0:T(8,128)S(1)}, s32[16,128]{1,0:T(8,128)}, u32[]{:S(2)}) copy-start(s32[16,128]{1,0:T(8,128)} %mask_ref.3) | copy-start | bytes 24580
  6.0 52.4 %all-to-all-start = ((bf16[128,96,128]{2,1,0:T(8,128)(2,1)}), bf16[128,96,128]{2,1,0:T(8,128)(2,1)S(1)}, u32[]{:S(2)}, u32[]{:S(2)}) async-start(bf16[128,96,128]{2,1,0:T(8,128)(2,1)} %pack.1), calls=%async_computation | async-start | bytes 6291456 | tf_op jit(solution)/shard_map/all_to_all | solution.py:515
  17.6 1.4 %copy-start = (f32[3,60,16,128]{3,2,1,0:T(8,128)S(1)}, f32[3,60,16,128]{3,2,1,0:T(8,128)}, u32[]{:S(2)}) copy-start(f32[3,60,16,128]{3,2,1,0:T(8,128)} %param.19) | copy-start | bytes 4423684
  18.9 14.1 %copy-start.1 = (f32[256,256]{1,0:T(8,128)S(1)}, f32[256,256]{1,0:T(8,128)}, u32[]{:S(2)}) copy-start(f32[256,256]{1,0:T(8,128)} %w2_ref) | copy-start | bytes 786436
  18.9 14.2 %copy-start.2 = (f32[180,256]{1,0:T(8,128)S(1)}, f32[180,256]{1,0:T(8,128)}, u32[]{:S(2)}) copy-start(f32[180,256]{1,0:T(8,128)} %w1_ref.1) | copy-start | bytes 552964
  22.0 47.9 %collective-permute-start = (f32[192,128]{1,0:T(8,128)}, f32[192,128]{1,0:T(8,128)S(1)}, u32[]{:S(2)}, u32[]{:S(2)}) collective-permute-start(f32[192,128]{1,0:T(8,128)} %get-tuple-element.82), channel_id=1, source_target_pairs={{16,0},{32,16},{48,32},{64,48},{80,64},{96,80},{112,96},{17,1},{33... | collective-permute-start | bytes 294920 | tf_op jit(solution)/shard_map/ppermute | solution.py:495
  25.0 45.0 %collective-permute-start.1 = (f32[192,128]{1,0:T(8,128)}, f32[192,128]{1,0:T(8,128)S(1)}, u32[]{:S(2)}, u32[]{:S(2)}) collective-permute-start(f32[192,128]{1,0:T(8,128)} %get-tuple-element.83), channel_id=1, source_target_pairs={{0,16},{16,32},{32,48},{48,64},{64,80},{80,96},{96,112},{1,17},{17... | collective-permute-start | bytes 294920 | tf_op jit(solution)/shard_map/ppermute | solution.py:495
  27.6 42.4 %collective-permute-start.2 = (f32[192,128]{1,0:T(8,128)}, f32[192,128]{1,0:T(8,128)S(1)}, u32[]{:S(2)}, u32[]{:S(2)}) collective-permute-start(f32[192,128]{1,0:T(8,128)} %get-tuple-element.84), channel_id=1, source_target_pairs={{1,0},{2,1},{3,2},{4,3},{5,4},{6,5},{7,6},{8,7},{9,8},{10,9},{11,1... | collective-permute-start | bytes 294920 | tf_op jit(solution)/shard_map/ppermute | solution.py:495
  28.9 41.1 %collective-permute-start.3 = (f32[192,128]{1,0:T(8,128)}, f32[192,128]{1,0:T(8,128)S(1)}, u32[]{:S(2)}, u32[]{:S(2)}) collective-permute-start(f32[192,128]{1,0:T(8,128)} %get-tuple-element.85), channel_id=1, source_target_pairs={{0,1},{1,2},{2,3},{3,4},{4,5},{5,6},{6,7},{7,8},{8,9},{9,10},{10,1... | collective-permute-start | bytes 294920 | tf_op jit(solution)/shard_map/ppermute | solution.py:495
  33.1 0.8 copy-start.7
  34.0 0.7 copy-start.8
  34.6 0.7 copy-start.9
  35.3 0.7 copy-start.10
  81.3 26.2 %copy-start.12 = (f32[192,128]{1,0:T(8,128)S(1)}, f32[192,128]{1,0:T(8,128)}, u32[]{:S(2)}) copy-start(f32[192,128]{1,0:T(8,128)} %get-tuple-element.98) | copy-start | bytes 294916
  81.3 29.2 %copy-start.11 = (f32[192,128]{1,0:T(8,128)S(1)}, f32[192,128]{1,0:T(8,128)}, u32[]{:S(2)}) copy-start(f32[192,128]{1,0:T(8,128)} %get-tuple-element.99) | copy-start | bytes 294916
  81.3 31.8 %copy-start.6 = (s32[16,128]{1,0:T(8,128)S(1)}, s32[16,128]{1,0:T(8,128)}, u32[]{:S(2)}) copy-start(s32[16,128]{1,0:T(8,128)} %mask_ref.3) | copy-start | bytes 24580
  81.3 19.5 %all-to-all-start.1 = ((f32[128,8,128]{2,1,0:T(8,128)}), f32[128,8,128]{2,1,0:T(8,128)S(1)}, u32[]{:S(2)}, u32[]{:S(2)}) async-start(f32[128,8,128]{2,1,0:T(8,128)} %bitcast.27), calls=%async_computation.1 | async-start | bytes 1048576 | tf_op jit(solution)/shard_map/all_to_all | solution.py:479
  86.7 15.0 %collective-permute-start.4 = (f32[192,128]{1,0:T(8,128)}, f32[192,128]{1,0:T(8,128)S(1)}, u32[]{:S(2)}, u32[]{:S(2)}) collective-permute-start(f32[192,128]{1,0:T(8,128)} %get-tuple-element.89), channel_id=1, source_target_pairs={{1,0},{2,1},{3,2},{4,3},{5,4},{6,5},{7,6},{8,7},{9,8},{10,9},{11,1... | collective-permute-start | bytes 294920 | tf_op jit(solution)/shard_map/ppermute | solution.py:495
  88.0 13.7 %collective-permute-start.5 = (f32[192,128]{1,0:T(8,128)}, f32[192,128]{1,0:T(8,128)S(1)}, u32[]{:S(2)}, u32[]{:S(2)}) collective-permute-start(f32[192,128]{1,0:T(8,128)} %get-tuple-element.90), channel_id=1, source_target_pairs={{0,1},{1,2},{2,3},{3,4},{4,5},{5,6},{6,7},{7,8},{8,9},{9,10},{10,1... | collective-permute-start | bytes 294920 | tf_op jit(solution)/shard_map/ppermute | solution.py:495
  101.7 19.9 %all-to-all-start.2 = ((f32[128,8,128]{2,1,0:T(8,128)}), f32[128,8,128]{2,1,0:T(8,128)S(1)}, u32[]{:S(2)}, u32[]{:S(2)}) async-start(f32[128,8,128]{2,1,0:T(8,128)} %bitcast.26), calls=%async_computation.2 | async-start | bytes 1048576 | tf_op jit(solution)/shard_map/all_to_all | solution.py:485
  107.5 9.3 %collective-permute-start.6 = (f32[192,128]{1,0:T(8,128)S(1)}, f32[192,128]{1,0:T(8,128)S(1)}, u32[]{:S(2)}, u32[]{:S(2)}) collective-permute-start(f32[192,128]{1,0:T(8,128)S(1)} %copy-done.12), channel_id=1, source_target_pairs={{16,0},{32,16},{48,32},{64,48},{80,64},{96,80},{112,96},{17,1},{33... | collective-permute-start | bytes 294920 | tf_op jit(solution)/shard_map/ppermute | solution.py:495
  110.5 6.3 %collective-permute-start.7 = (f32[192,128]{1,0:T(8,128)S(1)}, f32[192,128]{1,0:T(8,128)S(1)}, u32[]{:S(2)}, u32[]{:S(2)}) collective-permute-start(f32[192,128]{1,0:T(8,128)S(1)} %copy-done.11), channel_id=1, source_target_pairs={{0,16},{16,32},{32,48},{48,64},{64,80},{80,96},{96,112},{1,17},{17... | collective-permute-start | bytes 294920 | tf_op jit(solution)/shard_map/ppermute | solution.py:495
